TPU v7x, 512 devices: a whole 4x8x8 slice. The times are simulated.
512 devices in a mesh: ctx: 32 (over y, x), db: 16 (over z, core).
Axes of the slice: x: 4, y: 8, z: 8, core: 2. Of those that a mesh axis runs over, the one named last changes fastest.
Arguments:
- stream: bfloat16 [12288, 4096], P('ctx', 'db'), may hold values from -6 to 6
- history: bfloat16 [8, 12288, 4096], P(None, 'ctx', 'db'), may hold values from -6 to 6
- dwa_weights: float32 [9], replicated, may hold values from -0.5 to 1
- w_query: bfloat16 [4096, 4096], P('ctx', 'db'), may hold values from -0.09375 to 0.09375
- w_out: bfloat16 [4096, 4096], P('db', 'ctx'), may hold values from -0.1875 to 0.1875
- encoded_kv: bfloat16 [16, 24, 128, 2, 4096], P('db', None, 'ctx'), may hold values from -340 to 340
- neighbour_ids: int32 [384], replicated, may hold values from 0 to 383, each once
Outputs:
- block_out: bfloat16 [12288, 4096], P('ctx', 'db')
- dense: bfloat16 [12288, 4096], P('ctx', 'db')
Inputs may be any that keep to these rules, and one draw needn't show every extreme that they name: `neighbour_ids`: each stored neighbour is named by exactly one slot.
All inputs are finite; a program needn't handle non-finite values.
Results may differ from a plain program's by a relative error of at most 0.014.
The roundings to bfloat16 on the way count: a program that leaves them out, or rounds other values in their place, can miss the bound.
Values may be sent and summed in bfloat16 or wider, within the bound.
No kernel may reach another device: no remote copies, remote signals or barrier semaphores. Data moves between devices by JAX's collectives and lax.ppermute only.
A program may use at most 64 MiB of HBM per device.

v0:
```python
import jax
import jax.numpy as jnp
from jax import lax
from jax.sharding import PartitionSpec as P

HDIM = 128
SPAN = 64
NNB = 2


def shifted(block, axis, distance):
    devices = range(lax.axis_size(axis))
    route = [(i - distance, i) for i in devices if i - distance in devices]
    return lax.ppermute(block, axis, route)


def attend(queries, key_rows, value_rows):
    group_count, row_count, width = queries.shape
    head_count = width // HDIM
    query_heads = queries.reshape(group_count, row_count, head_count, HDIM)
    key_heads = key_rows.reshape(group_count, key_rows.shape[1], head_count, HDIM)
    value_heads = value_rows.reshape(group_count, value_rows.shape[1], head_count, HDIM)
    scores = jnp.einsum(
        "gqhd,gkhd->ghqk", query_heads, key_heads, preferred_element_type=jnp.float32
    ) * HDIM ** (-0.5)
    row_max = jnp.max(scores, axis=-1, keepdims=True)
    exponent = jnp.exp(scores - row_max)
    weights = (exponent / jnp.sum(exponent, axis=-1, keepdims=True)).astype(jnp.bfloat16)
    mixed = jnp.einsum("ghqk,gkhd->gqhd", weights, value_heads, preferred_element_type=jnp.float32)
    return mixed.astype(jnp.bfloat16).reshape(group_count, row_count, width)


def on_device(stream, history, dwa_weights, w_query, w_out, encoded_kv, neighbour_ids):
    tok_rows = stream.shape[0]
    local_width = w_query.shape[1]
    spans_here = tok_rows // SPAN
    lead_rows = SPAN - 1
    full_stream = lax.all_gather(stream, "db", axis=1, tiled=True)
    queries = jnp.dot(
        full_stream,
        lax.all_gather(w_query, "ctx", axis=0, tiled=True),
        preferred_element_type=jnp.float32,
    ).astype(jnp.bfloat16)
    out_full = lax.all_gather(w_out, "ctx", axis=1, tiled=True)
    groups_here = lax.all_to_all(encoded_kv, "db", split_axis=4, concat_axis=0, tiled=True)
    slab_rows = encoded_kv.shape[2]
    store = groups_here.reshape(-1, slab_rows, 2, local_width)
    ctx_count = lax.axis_size("ctx")
    row_requests = neighbour_ids.shape[0] // ctx_count
    wanted = neighbour_ids.reshape(ctx_count, row_requests).T
    outgoing = jnp.take(store, wanted, axis=0)
    arrived = lax.all_to_all(outgoing, "ctx", split_axis=1, concat_axis=1, tiled=True)
    neighbours = arrived.reshape(spans_here, NNB * ctx_count * slab_rows, 2, local_width)
    key_rows = neighbours[:, :, 0]
    value_rows = neighbours[:, :, 1]
    carried = shifted(neighbours[spans_here - 1], "ctx", 1)
    all_keys = jnp.concatenate([carried[None, :, 0], key_rows], 0)
    all_values = jnp.concatenate([carried[None, :, 1], value_rows], 0)
    padded = jnp.concatenate(
        [
            jnp.zeros((1, local_width), jnp.bfloat16),
            queries,
            jnp.zeros((lead_rows, local_width), jnp.bfloat16),
        ],
        0,
    )
    padded = padded.reshape(spans_here + 1, SPAN, local_width)
    mixed = attend(padded, all_keys, all_values).reshape(-1, local_width)
    attended = mixed[1 : tok_rows + 1]
    partial_value = jnp.dot(attended, out_full, preferred_element_type=jnp.float32)
    summed = lax.psum_scatter(
        partial_value.astype(jnp.bfloat16), "db", scatter_dimension=1, tiled=True
    ).astype(jnp.float32)
    block = stream.astype(jnp.float32) + summed
    dense = dwa_weights[-1] * block + jnp.sum(
        history.astype(jnp.float32) * dwa_weights[:-1, None, None], axis=0
    )
    return (block.astype(jnp.bfloat16), dense.astype(jnp.bfloat16))


def solution(mesh):
    placed = (
        P("ctx", "db"),
        P(None, "ctx", "db"),
        P(),
        P("ctx", "db"),
        P("db", "ctx"),
        P("db", None, "ctx", None, None),
        P(),
    )
    return jax.shard_map(
        on_device,
        mesh=mesh,
        in_specs=placed,
        out_specs=(P("ctx", "db"), P("ctx", "db")),
        check_vma=False,
    )
```

profile of v0, /device:TPU:4, one launch (start us, length us, event | category | flops | bytes accessed | tf_op | source)
XLA Modules:
  0.0 305.9 jit_solution(4108286600987173053)
XLA Ops:
  7.2 0.0 all-gather.6.cloned.1.call-start
  7.2 0.7 all-gather.6.cloned.1.call-update
  7.9 0.0 all-gather.4.cloned.1.call-start
  7.9 0.7 all-gather.4.cloned.1.call-update
  8.6 13.2 %copy.54 = bf16[1,24,4,2,4096]{1,2,3,0,4:T(4,128)(2,1)} copy(bf16[1,24,4,2,4096]{4,3,2,1,0:T(2,128)(2,1)} %param.12) | data formatting | bytes 3145728 | tf_op args[5]
  21.8 12.7 %reshape.48 = bf16[16,2,24576]{2,1,0:T(2,128)(2,1)} reshape(bf16[4096,1,2,4,24]{4,3,2,1,0:T(4,128)(2,1)} %bitcast.32) | data formatting | bytes 3145728
  34.6 0.0 copy-start.3
  34.6 10.6 %all-to-all-start = ((bf16[16,2,24576]{2,1,0:T(2,128)(2,1)}), bf16[16,2,24576]{2,1,0:T(2,128)(2,1)S(1)}, u32[]{:S(2)}, u32[]{:S(2)}) async-start(bf16[16,2,24576]{2,1,0:T(2,128)(2,1)} %reshape.48), calls=%async_computation | async-start | bytes 3145728 | tf_op jit(solution)/shard_map/all_to_all | solution.py:45
  45.1 0.0 copy-done.3
  45.1 0.1 reshape.34
  45.3 0.1 copy.57
  45.3 0.1 reshape.39
  45.5 37.5 %all-to-all-done = bf16[16,2,24576]{2,1,0:T(2,128)(2,1)S(1)} async-done(((bf16[16,2,24576]{2,1,0:T(2,128)(2,1)}), bf16[16,2,24576]{2,1,0:T(2,128)(2,1)S(1)}, u32[]{:S(2)}, u32[]{:S(2)}) %all-to-all-start) | async-done | bytes 1572896 | tf_op jit(solution)/shard_map/all_to_all | solution.py:45
  83.0 12.9 %reshape.49 = bf16[4096,1,2,4,24]{4,3,2,1,0:T(4,128)(2,1)} reshape(bf16[16,2,24576]{2,1,0:T(2,128)(2,1)S(1)} %all-to-all-done) | data formatting | bytes 3145728
  95.8 10.8 %copy.73 = bf16[1,24,4,2,16,256]{5,1,4,3,2,0:T(8,128)(2,1)S(1)} copy(bf16[1,24,4,2,16,256]{1,2,3,5,4,0:T(4,128)(2,1)} %bitcast.31) | data formatting | bytes 3145728 | tf_op jit(solution)/shard_map/all_to_all | solution.py:45
  106.6 1.2 copy.58
  107.9 3.2 %gather_fusion = bf16[384,4,2,256]{3,1,2,0:T(4,128)(2,1)S(1)} fusion(bf16[384,4,2,256]{3,1,2,0:T(4,128)(2,1)S(1)} %copy.58, s32[1024]{0:T(1024)S(1)} %pad_clamp_fusion), kind=kCustom, calls=%fused_computation | custom fusion | bytes 3147264 | tf_op jit(solution)/shard_map/jit(_take)/gather | solution.py:51
  111.0 3.0 broadcast_select_fusion
  114.0 10.2 %all-to-all-start.1 = ((bf16[12,32,4,2,256]{4,3,2,0,1:T(2,128)(2,1)}), bf16[12,32,4,2,256]{4,3,2,0,1:T(2,128)(2,1)S(1)}, u32[]{:S(2)}, u32[]{:S(2)}) async-start(bf16[12,32,4,2,256]{4,3,2,0,1:T(2,128)(2,1)} %broadcast_select_fusion), calls=%async_computation.1 | async-start | bytes 3145728 | tf_op jit(solution)/shard_map/all_to_all | solution.py:52
  124.2 0.0 all-gather.8.cloned.1.call-start
  124.3 0.7 all-gather.8.cloned.1.call-update
  125.0 0.0 reduce-scatter.2.cloned.1.call-start
  125.0 0.1 pad.6.clone
  125.1 0.0 all-gather.6.cloned.1.call-done
  125.1 21.3 %all-gather.4.cloned.1.call-done = bf16[384,4096]{1,0:T(8,128)(2,1)} async-done(((bf16[384,256]{1,0:T(8,128)(2,1)}), bf16[384,4096]{1,0:T(8,128)(2,1)}) %all-gather.4.cloned.1.call-update) | async-done | bytes 3145744 | tf_op jit(solution)/shard_map/all_gather | solution.py:38
  146.4 3.5 %convolution_convert_fusion.2 = bf16[384,256]{1,0:T(8,128)(2,1)S(1)} fusion(bf16[384,4096]{1,0:T(8,128)(2,1)} %all-gather.4.cloned.1.call-done, bf16[4096,256]{1,0:T(8,128)(2,1)} %all-gather.6.cloned.1.call-done), kind=kOutput, calls=%fused_computation.9 | convolution fusion | flops 805404672 | bytes 5439488 | tf_op jit(solution)/shard_map/dot_general | solution.py:39
  149.9 0.2 maximum_maximum_fusion
  150.1 0.8 reshape_reshape.6
  150.9 14.0 %all-to-all-done.1 = bf16[12,32,4,2,256]{4,3,2,0,1:T(2,128)(2,1)S(1)} async-done(((bf16[12,32,4,2,256]{4,3,2,0,1:T(2,128)(2,1)}), bf16[12,32,4,2,256]{4,3,2,0,1:T(2,128)(2,1)S(1)}, u32[]{:S(2)}, u32[]{:S(2)}) %all-to-all-start.1) | async-done | bytes 1572896 | tf_op jit(solution)/shard_map/all_to_all | solution.py:52
  164.9 0.2 slice.35
  165.1 0.9 copy.60
  166.0 2.1 collective-permute-start
  168.1 1.3 copy.62
  169.5 2.2 fusion.28
  171.7 2.6 copy.67
  174.3 1.5 copy.69
  175.8 0.9 copy.63
  176.7 0.4 copy.65
  177.1 0.0 copy-start.2
  177.1 0.0 collective-permute-done
  177.1 0.4 fusion.29
  177.5 0.1 copy.66
  177.6 0.1 copy.68
  177.8 0.1 copy.61
  177.9 0.1 copy.64
  178.0 0.0 copy-done.2
  178.0 1.5 fusion.30
  179.5 1.5 fusion.3
  181.0 0.2 copy.71
  181.3 46.6 %all-gather.8.cloned.1.call-done = bf16[256,4096]{1,0:T(8,128)(2,1)} async-done(((bf16[256,128]{1,0:T(8,128)(2,1)}), bf16[256,4096]{1,0:T(8,128)(2,1)}) %all-gather.8.cloned.1.call-update) | async-done | bytes 2097168 | tf_op jit(solution)/shard_map/all_gather | solution.py:44
  228.0 4.2 %convolution_convert_fusion = bf16[384,4096]{1,0:T(8,128)(2,1)} fusion(bf16[256,4096]{1,0:T(8,128)(2,1)} %all-gather.8.cloned.1.call-done, bf16[448,256]{1,0:T(8,128)(2,1)S(1)} %bitcast.38), kind=kOutput, calls=%fused_computation.2 | convolution fusion | flops 806879232 | bytes 5439488 | tf_op jit(solution)/shard_map/dot_general | solution.py:70
  232.2 0.0 copy-start.4
  232.2 0.0 copy-start
  232.2 0.0 reduce-scatter.2.cloned.1.call-update
  232.2 0.6 copy-done.4
  232.8 0.0 copy-start.1
  232.8 0.6 slice.31
  233.4 0.2 copy-done
  233.6 0.4 multiply_reduce_fusion
  234.0 63.0 %reduce-scatter.2.cloned.1.call-done = bf16[384,256]{1,0:T(8,128)(2,1)} async-done(((bf16[384,4096]{1,0:T(8,128)(2,1)}), bf16[384,256]{1,0:T(8,128)(2,1)}) %reduce-scatter.2.cloned.1.call-update) | async-done | bytes 196624 | tf_op jit(solution)/shard_map/reduce_scatter | solution.py:71
  297.0 0.0 copy-done.1
  297.0 2.4 add_convert_fusion
  (6 shorter events, 0.1 us)
Async XLA Ops:
  7.2 118.0 %all-gather.6.cloned.1.call-start = ((), (), s32[]{:S(2)}) async-start(), calls=%async_computation.4 | async-start | bytes 2162688 | tf_op jit(solution)/shard_map/all_gather | solution.py:41
  7.9 138.5 %all-gather.4.cloned.1.call-start = ((), (), s32[]{:S(2)}) async-start(), calls=%async_computation.3 | async-start | bytes 3342336 | tf_op jit(solution)/shard_map/all_gather | solution.py:38
  34.6 10.6 %copy-start.3 = (s32[384]{0:T(512)S(1)}, s32[384]{0:T(512)}, u32[]{:S(2)}) copy-start(s32[384]{0:T(512)} %param.13) | copy-start | bytes 4612
  34.6 48.4 %all-to-all-start = ((bf16[16,2,24576]{2,1,0:T(2,128)(2,1)}), bf16[16,2,24576]{2,1,0:T(2,128)(2,1)S(1)}, u32[]{:S(2)}, u32[]{:S(2)}) async-start(bf16[16,2,24576]{2,1,0:T(2,128)(2,1)} %reshape.48), calls=%async_computation | async-start | bytes 3145728 | tf_op jit(solution)/shard_map/all_to_all | solution.py:45
  114.0 50.9 %all-to-all-start.1 = ((bf16[12,32,4,2,256]{4,3,2,0,1:T(2,128)(2,1)}), bf16[12,32,4,2,256]{4,3,2,0,1:T(2,128)(2,1)S(1)}, u32[]{:S(2)}, u32[]{:S(2)}) async-start(bf16[12,32,4,2,256]{4,3,2,0,1:T(2,128)(2,1)} %broadcast_select_fusion), calls=%async_computation.1 | async-start | bytes 3145728 | tf_op jit(solution)/shard_map/all_to_all | solution.py:52
  124.2 103.7 %all-gather.8.cloned.1.call-start = ((), (), s32[]{:S(2)}) async-start(), calls=%async_computation.5 | async-start | bytes 2162688 | tf_op jit(solution)/shard_map/all_gather | solution.py:44
  125.0 172.0 %reduce-scatter.2.cloned.1.call-start = ((), (), s32[]{:S(2)}) async-start(), calls=%async_computation.6 | async-start | bytes 3342336 | tf_op jit(solution)/shard_map/reduce_scatter | solution.py:71
  166.0 11.1 %collective-permute-start = (bf16[256,2,256]{2,1,0:T(2,128)(2,1)}, bf16[256,2,256]{2,1,0:T(2,128)(2,1)S(1)}, u32[]{:S(2)}, u32[]{:S(2)}) collective-permute-start(bf16[256,2,256]{2,1,0:T(2,128)(2,1)} %bitcast.6), channel_id=1, source_target_pairs={{0,16},{16,32},{32,48},{48,64},{64,80},{80,96},{96,112},{112,128},... | collective-permute-start | bytes 786440 | tf_op jit(solution)/shard_map/ppermute | solution.py:14
  177.1 0.9 copy-start.2
  232.2 0.7 copy-start.4
  232.2 1.4 copy-start
  232.8 64.2 %copy-start.1 = (bf16[384,256]{1,0:T(8,128)(2,1)S(1)}, bf16[384,256]{1,0:T(8,128)(2,1)}, u32[]{:S(2)}) copy-start(bf16[384,256]{1,0:T(8,128)(2,1)} %param.7) | copy-start | bytes 589828
Sparse Core Ops, SparseCore 0:
  11.1 86.3 all-gather.5
  99.6 46.7 all-gather.3
  149.4 78.4 all-gather.7
  232.3 64.6 reduce-scatter.1
where the time goes:
time: 307 us; the launch traced here: 306 us
  waiting for transfers between devices  185 us (60%)
  local copies, waits for them, and re-layouts  67.7 us (22%)
  starting transfers between devices  23.1 us (8%)
  between operations  14 us (5%)
  matrix products  10.7 us (3%)
  other arithmetic  5.92 us (2%)
    reduce_scatter x1, waiting for transfers between devices, on_device(): lax.psum_scatter(partial_value.astype(jnp.bfloat16), 'db', scatter_dimens...  63 us
    all_gather x1, waiting for transfers between devices, on_device(): out_full = lax.all_gather(w_out, 'ctx', axis=1, tiled=True)  46.6 us
    unnamed x14, local copies, waits for them, and re-layouts  39.6 us
    all_to_all x1, waiting for transfers between devices, on_device(): lax.all_to_all(encoded_kv, 'db', split_axis=4, concat_axis=0, tiled=True)  37.5 us
    all_gather x1, waiting for transfers between devices, on_device(): full_stream = lax.all_gather(stream, 'db', axis=1, tiled=True)  21.3 us
    all_to_all x1, waiting for transfers between devices, on_device(): lax.all_to_all(outgoing, 'ctx', split_axis=1, concat_axis=1, tiled=True)  14 us
    all_to_all x1, local copies, waits for them, and re-layouts, on_device(): lax.all_to_all(encoded_kv, 'db', split_axis=4, concat_axis=0, tiled=True)  10.8 us
    all_to_all x1, starting transfers between devices, on_device(): lax.all_to_all(encoded_kv, 'db', split_axis=4, concat_axis=0, tiled=True)  10.6 us
  transfers between devices with their start and end apart: 7, of which 5 were waited for; matrix products, arithmetic and copies ran while one was open for 25% of the time, Pallas kernels for 0%

commit v1 on v0

v1 whole, which is shorter than its diff:
```python
import jax
import jax.numpy as jnp
from jax import lax
from jax.experimental import pallas as pl
from jax.experimental.pallas import tpu as pltpu
from jax.sharding import Mesh, PartitionSpec as P

ROOM = pltpu.CompilerParams(vmem_limit_bytes=24 * 1024 * 1024)
HDIM = 128
SPAN = 64
NNB = 2
LEAD = SPAN - 1
CTX = ("y", "x")
DB = ("z", "core")


def any_space():
    return pl.BlockSpec(memory_space=pl.ANY)


def vmem_space():
    return pl.BlockSpec(memory_space=pltpu.VMEM)


def split_heads_kernel(source, out, sems):
    heads, local_heads = source.shape[4] // HDIM, out.shape[2]
    copies = []
    for head in range(heads):
        target = out.at[head // local_heads, :, head % local_heads]
        copies.append(
            pltpu.make_async_copy(
                source.at[0, :, :, :, pl.ds(head * HDIM, HDIM)], target, sems.at[head]
            )
        )
        copies[-1].start()
    for copy in copies:
        copy.wait()


def split_heads(encoded, local_heads):
    _, held, rows, pair, width = encoded.shape
    heads = width // HDIM
    return pl.pallas_call(
        split_heads_kernel,
        out_shape=jax.ShapeDtypeStruct(
            (heads // local_heads, held, local_heads, rows, pair, HDIM), encoded.dtype
        ),
        in_specs=[any_space()],
        out_specs=vmem_space(),
        scratch_shapes=[pltpu.SemaphoreType.DMA((heads,))],
        compiler_params=ROOM,
        name="split_heads",
    )(encoded)


def pick_kernel(ids, store, out):
    def body(i, carry):
        out[i] = store[ids[i]]
        return carry

    lax.fori_loop(0, out.shape[0], body, 0, unroll=8)


def pick(ids, store):
    count = ids.shape[0]
    block = store.shape[1:]
    return pl.pallas_call(
        pick_kernel,
        out_shape=jax.ShapeDtypeStruct((count,) + block, store.dtype),
        grid_spec=pltpu.PrefetchScalarGridSpec(
            num_scalar_prefetch=1,
            grid=(1,),
            in_specs=[pl.BlockSpec(store.shape, lambda i, s: (0, 0, 0))],
            out_specs=pl.BlockSpec((count,) + block, lambda i, s: (0, 0, 0)),
        ),
        compiler_params=ROOM,
        name="pick",
    )(ids, store)


def attend_kernel(q_ref, kv_ref, o_ref):
    slabs, slots, heads, rows, _ = kv_ref.shape
    keys = slabs * NNB * rows
    lane = lax.broadcasted_iota(jnp.int32, (SPAN, keys), 1)
    is_key = (lane & 1) == 0
    for span in range(slots // NNB):
        tokens = slice(span * SPAN, (span + 1) * SPAN)
        for head in range(heads):
            columns = slice(head * HDIM, (head + 1) * HDIM)
            rows_kv = kv_ref[:, NNB * span : NNB * span + NNB, head].reshape(keys, HDIM)
            scores = lax.dot_general(
                q_ref[tokens, columns],
                rows_kv,
                (((1,), (1,)), ((), ())),
                preferred_element_type=jnp.float32,
            ) * HDIM ** (-0.5)
            scores = jnp.where(is_key, scores, -jnp.inf)
            row_max = jnp.max(scores, axis=-1, keepdims=True)
            exponent = jnp.exp(scores - row_max)
            weights = exponent / jnp.sum(exponent, axis=-1, keepdims=True)
            on_values = pltpu.roll(weights, 1, 1).astype(jnp.bfloat16)
            mixed = lax.dot_general(
                on_values, rows_kv, (((1,), (0,)), ((), ())), preferred_element_type=jnp.float32
            )
            o_ref[tokens, columns] = mixed.astype(jnp.bfloat16)


def attend(queries, kv):
    return pl.pallas_call(
        attend_kernel,
        out_shape=jax.ShapeDtypeStruct(queries.shape, jnp.bfloat16),
        in_specs=[vmem_space(), vmem_space()],
        out_specs=vmem_space(),
        compiler_params=ROOM,
        name="attend",
    )(queries, kv)


def shifted(block, distance):
    count = lax.axis_size(CTX)
    route = [(i - distance, i) for i in range(count) if 0 <= i - distance < count]
    return lax.ppermute(block, CTX, route)


def ring(count, step):
    return [(i, (i + step) % count) for i in range(count)]


def around(block, axis):
    count = lax.axis_size(axis)
    parts = {0: block}
    right = left = block
    for step in range(1, count // 2 + 1):
        right = lax.ppermute(right, axis, ring(count, 1))
        parts[-step] = right
        if step < count - count // 2:
            left = lax.ppermute(left, axis, ring(count, -1))
            parts[step] = left
    return jnp.stack([parts[i] for i in sorted(parts)])


def partner(block):
    return lax.ppermute(block, "core", [(0, 1), (1, 0)])


def project_kernel(place, mine, other, weights, out):
    steps, _, depth = mine.shape
    z, core = place[0], place[1]

    def body(i, total):
        at = lax.rem(z + i + steps - steps // 2, steps) * 2
        w_mine = weights[pl.ds((at + core) * 2, 2), 0].reshape(depth, -1)
        w_other = weights[pl.ds((at + 1 - core) * 2, 2), 0].reshape(depth, -1)
        total += jnp.dot(mine[i], w_mine, preferred_element_type=jnp.float32)
        total += jnp.dot(other[i], w_other, preferred_element_type=jnp.float32)
        return total

    total = lax.fori_loop(0, steps, body, jnp.zeros(out.shape, jnp.float32))
    out[...] = total.astype(out.dtype)


def project(place, mine, other, weights):
    rows, width = mine.shape[1], weights.shape[3]
    return pl.pallas_call(
        project_kernel,
        out_shape=jax.ShapeDtypeStruct((rows, width), jnp.bfloat16),
        in_specs=[pl.BlockSpec(memory_space=pltpu.SMEM)] + [vmem_space()] * 3,
        out_specs=vmem_space(),
        compiler_params=ROOM,
        name="project",
    )(place, mine, other, weights)


def finish_kernel(dwa, attended, weights, stream, past, block_out, dense_out):
    groups, _, depth = attended.shape

    def body(g, total):
        w = weights[pl.ds(g * 2, 2), 1].reshape(depth, -1)
        part = jnp.dot(attended[g], w, preferred_element_type=jnp.float32)
        return total + part.astype(jnp.bfloat16).astype(jnp.float32)

    total = lax.fori_loop(0, groups, body, jnp.zeros(stream.shape, jnp.float32))
    block = stream[...].astype(jnp.float32) + total
    block_out[...] = block.astype(block_out.dtype)
    dense_out[...] = (dwa[dwa.shape[0] - 1] * block + past[...]).astype(dense_out.dtype)


def finish(dwa, attended, weights, stream, past):
    shape = jax.ShapeDtypeStruct(stream.shape, jnp.bfloat16)
    return pl.pallas_call(
        finish_kernel,
        out_shape=(shape, shape),
        in_specs=[pl.BlockSpec(memory_space=pltpu.SMEM)] + [vmem_space()] * 4,
        out_specs=(vmem_space(), vmem_space()),
        compiler_params=ROOM,
        name="finish",
    )(dwa, attended, weights, stream, past)


def columns_here(w_out):
    ctx_count, db_count = lax.axis_size(CTX), lax.axis_size(DB)
    odd = lax.rem(lax.axis_index(CTX), 2)
    half = w_out.shape[0] // 2
    pieces = []
    for flip in range(2):
        route = [
            (c * db_count + d, (2 * d + (c + flip) % 2) * db_count + c // 2)
            for c in range(ctx_count)
            for d in range(db_count)
        ]
        row = (odd + flip) % 2 * half
        send = lax.dynamic_slice_in_dim(w_out, row, half, 0)
        pieces.append(lax.ppermute(send, CTX + DB, route))
    straight = jnp.concatenate(pieces, 1)
    crossed = jnp.concatenate(pieces[::-1], 1)
    return jnp.where(odd == 0, straight, crossed)


def on_device(stream, history, dwa_weights, w_query, w_out, encoded_kv, neighbour_ids):
    tok_rows = stream.shape[0]
    local_heads = w_query.shape[1] // HDIM
    ctx_count = lax.axis_size(CTX)
    db_count = lax.axis_size(DB)
    slots = neighbour_ids.shape[0] // ctx_count
    slab_rows = 2 * encoded_kv.shape[2]
    place = jnp.stack([lax.axis_index("z"), lax.axis_index("core")]).astype(jnp.int32)

    weights = lax.all_gather(jnp.stack([w_query, columns_here(w_out)]), CTX, axis=0)
    after = shifted(stream[:SPAN], -1)
    own_spans = jnp.concatenate([stream[LEAD:], after[:LEAD]], 0)
    past = jnp.sum(history.astype(jnp.float32) * dwa_weights[:-1, None, None], axis=0)

    by_head = split_heads(encoded_kv, local_heads)
    store = lax.all_to_all(
        by_head.reshape(db_count, -1, HDIM), DB, split_axis=0, concat_axis=0, tiled=True
    )
    picked = pick(neighbour_ids, store.reshape(-1, local_heads * slab_rows, HDIM))
    own_spans, picked = lax.optimization_barrier((own_spans, picked))
    arrived = lax.all_to_all(
        picked.reshape(ctx_count, -1, HDIM), CTX, split_axis=0, concat_axis=0, tiled=True
    ).reshape(ctx_count, slots, local_heads, slab_rows, HDIM)
    mine = around(own_spans, "z")
    queries = project(place, mine, partner(mine), weights)
    mixed = attend(queries, arrived)
    before = shifted(mixed[tok_rows - SPAN :], 1)
    attended = jnp.concatenate([before[1:], mixed[: tok_rows - LEAD]], 0)
    everyone = lax.all_gather(attended, DB, axis=0)
    return finish(dwa_weights, everyone, weights, stream, past)


def solution(mesh):
    devices = mesh.devices
    cores = 2
    z = devices.shape[1] // cores
    x = 4
    y = devices.shape[0] // x
    split = Mesh(devices.reshape(y, x, z, cores), ("y", "x", "z", "core"))
    placed = (
        P(CTX, DB),
        P(None, CTX, DB),
        P(),
        P(CTX, DB),
        P(DB, CTX),
        P(DB, None, CTX, None, None),
        P(),
    )
    return jax.shard_map(
        on_device,
        mesh=split,
        in_specs=placed,
        out_specs=(P(CTX, DB), P(CTX, DB)),
        check_vma=False,
    )
```

time: 307 us -> 237 us (0.77)
  the two profiles are of different devices: /device:TPU:4 before, /device:TPU:1 now
where the time goes in v1:
time: 237 us; the launch traced here: 236 us
  waiting for transfers between devices  115 us (49%)
  starting transfers between devices  70.5 us (30%)
  Pallas kernels  19.5 us (8%)
  between operations  14.4 us (6%)
  local copies, waits for them, and re-layouts  13.3 us (6%)
  other arithmetic  2.71 us (1%)
    all_gather x1, waiting for transfers between devices, on_device(): everyone = lax.all_gather(attended, DB, axis=0)  43.7 us
    all_to_all x1, waiting for transfers between devices, on_device(): lax.all_to_all(by_head.reshape(db_count, -1, HDIM), DB, split_axis=0, con...  33.8 us
    all_to_all x1, starting transfers between devices, on_device(): lax.all_to_all(by_head.reshape(db_count, -1, HDIM), DB, split_axis=0, con...  21.8 us
    ppermute x3, starting transfers between devices, around(): left = lax.ppermute(left, axis, ring(count, -1))  13.8 us
    ppermute x4, waiting for transfers between devices, around(): right = lax.ppermute(right, axis, ring(count, 1))  13.3 us
    all_to_all x1, waiting for transfers between devices, on_device(): lax.all_to_all(picked.reshape(ctx_count, -1, HDIM), CTX, split_axis=0, co...  12.6 us
    unnamed x31, local copies, waits for them, and re-layouts  12.4 us
    all_to_all x1, starting transfers between devices, on_device(): lax.all_to_all(picked.reshape(ctx_count, -1, HDIM), CTX, split_axis=0, co...  8.11 us
  transfers between devices with their start and end apart: 16, of which 10 were waited for; matrix products, arithmetic and copies ran while one was open for 2% of the time, Pallas kernels for 4%

profile of v1, /device:TPU:1, one launch (start us, length us, event | category | flops | bytes accessed | tf_op | source)
XLA Modules:
  0.0 235.8 jit_solution(11177071886681855687)
XLA Ops:
  7.2 0.0 all-gather.5.cloned.1.call-start
  7.2 0.8 constant_dynamic-slice_fusion.1
  8.0 5.8 %collective-permute-start.10 = (bf16[128,128]{1,0:T(8,128)(2,1)S(1)}, bf16[128,128]{1,0:T(8,128)(2,1)S(1)}, u32[]{:S(2)}, u32[]{:S(2)}) collective-permute-start(bf16[128,128]{1,0:T(8,128)(2,1)S(1)} %get-tuple-element.7), channel_id=1, source_target_pairs={{0,16},{1,48},{2,80},{3,112},{4,144},{5,176},{6,208},{7,240},{8,27... | collective-permute-start | bytes 98312 | tf_op jit(solution)/shard_map/ppermute | solution.py:213
  13.8 2.2 collective-permute-start.9
  16.0 0.0 collective-permute-done.10
  16.0 4.5 %collective-permute-done.9 = bf16[128,128]{1,0:T(8,128)(2,1)S(1)} collective-permute-done((bf16[128,128]{1,0:T(8,128)(2,1)S(1)}, bf16[128,128]{1,0:T(8,128)(2,1)S(1)}, u32[]{:S(2)}, u32[]{:S(2)}) %collective-permute-start.9) | collective-permute-done | bytes 32800 | tf_op jit(solution)/shard_map/ppermute | solution.py:213
  20.6 1.5 pad_maximum_fusion.2
  22.1 0.0 all-gather.5.cloned.1.call-update
  22.1 0.0 copy-start.3
  22.1 1.4 copy-done.3
  23.5 3.1 %split_heads.1 = bf16[16,24,2,4,2,128]{5,4,3,2,1,0:T(2,128)(2,1)} custom-call(bf16[1,24,4,2,4096]{4,3,2,1,0:T(2,128)(2,1)S(1)} %copy-done.3), custom_call_target="tpu_custom_call" | custom-call | tf_op jit(solution)/shard_map/split_heads/pallas_call | solution.py:43
  26.6 0.0 copy-start.4
  26.7 0.0 copy-start.6
  26.7 21.8 %all-to-all-start = ((bf16[16,384,128]{2,1,0:T(8,128)(2,1)}), bf16[16,384,128]{2,1,0:T(8,128)(2,1)S(1)}, u32[]{:S(2)}, u32[]{:S(2)}) async-start(bf16[16,384,128]{2,1,0:T(8,128)(2,1)} %bitcast.2), calls=%async_computation | async-start | bytes 3145728 | tf_op jit(solution)/shard_map/all_to_all | solution.py:234
  48.5 0.0 copy-done.4
  48.5 1.3 collective-permute-start
  49.8 3.3 %collective-permute-done = bf16[64,256]{1,0:T(8,128)(2,1)S(1)} collective-permute-done((bf16[64,256]{1,0:T(8,128)(2,1)S(1)}, bf16[64,256]{1,0:T(8,128)(2,1)S(1)}, u32[]{:S(2)}, u32[]{:S(2)}) %collective-permute-start) | collective-permute-done | bytes 32800 | tf_op jit(solution)/shard_map/ppermute | solution.py:122
  53.2 33.8 %all-to-all-done = bf16[16,384,128]{2,1,0:T(8,128)(2,1)S(1)} async-done(((bf16[16,384,128]{2,1,0:T(8,128)(2,1)}), bf16[16,384,128]{2,1,0:T(8,128)(2,1)S(1)}, u32[]{:S(2)}, u32[]{:S(2)}) %all-to-all-start) | async-done | bytes 1572896 | tf_op jit(solution)/shard_map/all_to_all | solution.py:234
  87.0 0.0 copy-done.6
  87.0 2.4 %pick.1 = bf16[384,16,128]{2,1,0:T(8,128)(2,1)} custom-call(s32[384]{0:T(512)S(1)} %copy-done.6, bf16[384,16,128]{2,1,0:T(8,128)(2,1)S(1)} %bitcast.32), custom_call_target="tpu_custom_call" | custom-call | tf_op jit(solution)/shard_map/pick/pallas_call | solution.py:67
  89.4 1.9 collective-permute-start.1
  91.3 8.1 %collective-permute-done.1 = bf16[384,256]{1,0:T(8,128)(2,1)} collective-permute-done((bf16[384,256]{1,0:T(8,128)(2,1)S(1)}, bf16[384,256]{1,0:T(8,128)(2,1)}, u32[]{:S(2)}, u32[]{:S(2)}) %collective-permute-start.1) | collective-permute-done | bytes 196640 | tf_op jit(solution)/shard_map/ppermute | solution.py:134
  99.4 1.9 collective-permute-start.2
  101.3 4.6 %collective-permute-start.5 = (bf16[384,256]{1,0:T(8,128)(2,1)S(1)}, bf16[384,256]{1,0:T(8,128)(2,1)S(1)}, u32[]{:S(2)}, u32[]{:S(2)}) collective-permute-start(bf16[384,256]{1,0:T(8,128)(2,1)S(1)} %pad_maximum_fusion), channel_id=1, source_target_pairs={{0,14},{2,0},{4,2},{6,4},{8,6},{10,8},{12,10},{14,12},{1,15},{3,1}... | collective-permute-start | bytes 589832 | tf_op jit(solution)/shard_map/ppermute | solution.py:137
  105.9 3.1 %collective-permute-done.2 = bf16[384,256]{1,0:T(8,128)(2,1)S(1)} collective-permute-done((bf16[384,256]{1,0:T(8,128)(2,1)}, bf16[384,256]{1,0:T(8,128)(2,1)S(1)}, u32[]{:S(2)}, u32[]{:S(2)}) %collective-permute-start.2) | collective-permute-done | bytes 196640 | tf_op jit(solution)/shard_map/ppermute | solution.py:134
  109.0 1.9 collective-permute-start.3
  110.9 0.0 collective-permute-done.5
  110.9 4.6 %collective-permute-start.6 = (bf16[384,256]{1,0:T(8,128)(2,1)S(1)}, bf16[384,256]{1,0:T(8,128)(2,1)}, u32[]{:S(2)}, u32[]{:S(2)}) collective-permute-start(bf16[384,256]{1,0:T(8,128)(2,1)S(1)} %collective-permute-done.5), channel_id=1, source_target_pairs={{0,14},{2,0},{4,2},{6,4},{8,6},{10,8},{12,10},{14,12},{1,15},{3,1}... | collective-permute-start | bytes 589832 | tf_op jit(solution)/shard_map/ppermute | solution.py:137
  115.5 2.1 collective-permute-done.3
  117.6 1.9 collective-permute-start.4
  119.5 0.0 copy-done.8
  119.5 8.1 %all-to-all-start.1 = ((bf16[32,192,128]{2,1,0:T(8,128)(2,1)}), bf16[32,192,128]{2,1,0:T(8,128)(2,1)S(1)}, u32[]{:S(2)}, u32[]{:S(2)}) async-start(bf16[32,192,128]{2,1,0:T(8,128)(2,1)} %bitcast.16), calls=%async_computation.1 | async-start | bytes 3145728 | tf_op jit(solution)/shard_map/all_to_all | solution.py:239
  127.6 0.0 all-gather.7.cloned.1.call-start
  127.7 0.0 copy-start.9
  127.7 0.0 collective-permute-done.6
  127.7 4.7 %collective-permute-start.7 = (bf16[384,256]{1,0:T(8,128)(2,1)}, bf16[384,256]{1,0:T(8,128)(2,1)S(1)}, u32[]{:S(2)}, u32[]{:S(2)}) collective-permute-start(bf16[384,256]{1,0:T(8,128)(2,1)} %collective-permute-done.6), channel_id=1, source_target_pairs={{0,14},{2,0},{4,2},{6,4},{8,6},{10,8},{12,10},{14,12},{1,15},{3,1}... | collective-permute-start | bytes 589832 | tf_op jit(solution)/shard_map/ppermute | solution.py:137
  132.4 0.0 collective-permute-done.4
  132.4 0.9 bitcast_dynamic-update-slice_fusion.7
  133.4 0.9 bitcast_dynamic-update-slice_fusion.6
  134.3 0.9 bitcast_dynamic-update-slice_fusion.5
  135.3 0.9 bitcast_dynamic-update-slice_fusion.4
  136.2 0.0 copy-done.9
  136.3 0.9 bitcast_dynamic-update-slice_fusion.1
  137.2 0.0 collective-permute-done.7
  137.3 4.6 %collective-permute-start.8 = (bf16[8,384,256]{2,1,0:T(8,128)(2,1)S(1)}, bf16[8,384,256]{2,1,0:T(8,128)(2,1)}, u32[]{:S(2)}, u32[]{:S(2)}) collective-permute-start(bf16[8,384,256]{2,1,0:T(8,128)(2,1)S(1)} %bitcast_dynamic-update-slice_fusion.mine), channel_id=1, source_target_pairs={{0,1},{1,0},{2,3},{3,2},{4,5},{5,4},{6,7},{7,6},{8,9},{9,8},{10,11... | collective-permute-start | bytes 4718600 | tf_op jit(solution)/shard_map/ppermute | solution.py:143
  141.9 0.1 pad_add_fusion.place
  142.0 3.1 %collective-permute-done.8.other = bf16[8,384,256]{2,1,0:T(8,128)(2,1)} collective-permute-done((bf16[8,384,256]{2,1,0:T(8,128)(2,1)S(1)}, bf16[8,384,256]{2,1,0:T(8,128)(2,1)}, u32[]{:S(2)}, u32[]{:S(2)}) %collective-permute-start.8) | collective-permute-done | bytes 1572896 | tf_op jit(solution)/shard_map/ppermute | solution.py:143
  145.1 2.2 copy-done
  147.2 3.7 %project.1.q_ref = bf16[384,256]{1,0:T(8,128)(2,1)S(1)} custom-call(s32[2]{0:T(128)S(1)} %pad_add_fusion.place, bf16[8,384,256]{2,1,0:T(8,128)(2,1)S(1)} %bitcast_dynamic-update-slice_fusion.mine, bf16[8,384,256]{2,1,0:T(8,128)(2,1)} %collective-permute-done.8.other, bf16[32,2,128,256]{3,2,1,0:T(8,128)(2,1)S(1)} %bitcast.29), custom_call_target="tpu_custom_call" | custom-call | tf_op jit(solution)/shard_map/project/pallas_call | solution.py:164
  150.9 0.0 copy-start.5
  150.9 0.0 copy-start.7
  150.9 12.6 %all-to-all-done.1 = bf16[32,192,128]{2,1,0:T(8,128)(2,1)S(1)} async-done(((bf16[32,192,128]{2,1,0:T(8,128)(2,1)}), bf16[32,192,128]{2,1,0:T(8,128)(2,1)S(1)}, u32[]{:S(2)}, u32[]{:S(2)}) %all-to-all-start.1) | async-done | bytes 1572896 | tf_op jit(solution)/shard_map/all_to_all | solution.py:239
  163.5 5.1 %attend.1 = bf16[384,256]{1,0:T(8,128)(2,1)S(1)} custom-call(bf16[384,256]{1,0:T(8,128)(2,1)S(1)} %project.1.q_ref, bf16[32,12,2,8,128]{4,3,2,1,0:T(8,128)(2,1)S(1)} %bitcast.31), custom_call_target="tpu_custom_call" | custom-call | tf_op jit(solution)/shard_map/attend/pallas_call | solution.py:109
  168.6 5.2 %collective-permute-start.11 = (bf16[64,256]{1,0:T(8,128)(2,1)S(1)}, bf16[64,256]{1,0:T(8,128)(2,1)S(1)}, u32[]{:S(2)}, u32[]{:S(2)}) collective-permute-start(bf16[64,256]{1,0:T(8,128)(2,1)S(1)} %slice.29), channel_id=1, source_target_pairs={{0,16},{16,32},{32,48},{48,64},{64,80},{80,96},{96,112},{112,128},... | collective-permute-start | bytes 98312 | tf_op jit(solution)/shard_map/ppermute | solution.py:122
  173.8 1.0 collective-permute-done.11
  174.8 0.7 pad_maximum_fusion.1
  175.5 0.0 all-gather.7.cloned.1.call-update
  175.5 0.0 copy-done.5
  175.5 0.0 copy-done.7
  175.5 0.4 multiply_reduce_fusion.past
  175.9 43.7 %all-gather.7.cloned.1.call-done = bf16[6144,256]{1,0:T(8,128)(2,1)} async-done(((bf16[384,256]{1,0:T(8,128)(2,1)}), bf16[6144,256]{1,0:T(8,128)(2,1)}) %all-gather.7.cloned.1.call-update) | async-done | bytes 3145744 | tf_op jit(solution)/shard_map/all_gather | solution.py:247
  219.7 2.2 copy-done.1
  221.8 1.9 copy-done.2
  223.7 5.2 %finish.1 = (bf16[384,256]{1,0:T(8,128)(2,1)}, bf16[384,256]{1,0:T(8,128)(2,1)}) custom-call(f32[9]{0:T(128)S(1)} %copy-done.5, bf16[16,384,256]{2,1,0:T(8,128)(2,1)S(1)} %bitcast.33, bf16[32,2,128,256]{3,2,1,0:T(8,128)(2,1)S(1)} %bitcast.30, bf16[384,256]{1,0:T(8,128)(2,1)S(1)} %copy-done.4, f32[384,256]{1,0:T(8,128)S(1)} %multiply_reduce_fusion.past), custom_call_target="tpu_custom_call" | custom-call | tf_op jit(solution)/shard_map/finish/pallas_call | solution.py:190
  (19 shorter events, 0.2 us)
Async XLA Ops:
  7.2 137.9 %all-gather.5.cloned.1.call-start = ((), (), s32[]{:S(2)}) async-start(), calls=%async_computation.2 | async-start | bytes 4325376 | tf_op jit(solution)/shard_map/all_gather | solution.py:228
  8.0 8.0 %collective-permute-start.10 = (bf16[128,128]{1,0:T(8,128)(2,1)S(1)}, bf16[128,128]{1,0:T(8,128)(2,1)S(1)}, u32[]{:S(2)}, u32[]{:S(2)}) collective-permute-start(bf16[128,128]{1,0:T(8,128)(2,1)S(1)} %get-tuple-element.7), channel_id=1, source_target_pairs={{0,16},{1,48},{2,80},{3,112},{4,144},{5,176},{6,208},{7,240},{8,27... | collective-permute-start | bytes 98312 | tf_op jit(solution)/shard_map/ppermute | solution.py:213
  13.8 6.7 %collective-permute-start.9 = (bf16[128,128]{1,0:T(8,128)(2,1)S(1)}, bf16[128,128]{1,0:T(8,128)(2,1)S(1)}, u32[]{:S(2)}, u32[]{:S(2)}) collective-permute-start(bf16[128,128]{1,0:T(8,128)(2,1)S(1)} %get-tuple-element.6), channel_id=1, source_target_pairs={{0,0},{1,32},{2,64},{3,96},{4,128},{5,160},{6,192},{7,224},{8,256}... | collective-permute-start | bytes 98312 | tf_op jit(solution)/shard_map/ppermute | solution.py:213
  22.1 1.4 copy-start.3
  26.6 21.8 %copy-start.4 = (bf16[384,256]{1,0:T(8,128)(2,1)S(1)}, bf16[384,256]{1,0:T(8,128)(2,1)}, u32[]{:S(2)}) copy-start(bf16[384,256]{1,0:T(8,128)(2,1)} %stream.1) | copy-start | bytes 589828
  26.7 60.3 %copy-start.6 = (s32[384]{0:T(512)S(1)}, s32[384]{0:T(512)}, u32[]{:S(2)}) copy-start(s32[384]{0:T(512)} %ids.1) | copy-start | bytes 4612
  26.7 60.3 %all-to-all-start = ((bf16[16,384,128]{2,1,0:T(8,128)(2,1)}), bf16[16,384,128]{2,1,0:T(8,128)(2,1)S(1)}, u32[]{:S(2)}, u32[]{:S(2)}) async-start(bf16[16,384,128]{2,1,0:T(8,128)(2,1)} %bitcast.2), calls=%async_computation | async-start | bytes 3145728 | tf_op jit(solution)/shard_map/all_to_all | solution.py:234
  48.5 4.7 %collective-permute-start = (bf16[64,256]{1,0:T(8,128)(2,1)S(1)}, bf16[64,256]{1,0:T(8,128)(2,1)S(1)}, u32[]{:S(2)}, u32[]{:S(2)}) collective-permute-start(bf16[64,256]{1,0:T(8,128)(2,1)S(1)} %slice.22), channel_id=1, source_target_pairs={{16,0},{32,16},{48,32},{64,48},{80,64},{96,80},{112,96},{128,112},... | collective-permute-start | bytes 98312 | tf_op jit(solution)/shard_map/ppermute | solution.py:122
  89.4 10.0 %collective-permute-start.1 = (bf16[384,256]{1,0:T(8,128)(2,1)S(1)}, bf16[384,256]{1,0:T(8,128)(2,1)}, u32[]{:S(2)}, u32[]{:S(2)}) collective-permute-start(bf16[384,256]{1,0:T(8,128)(2,1)S(1)} %pad_maximum_fusion), channel_id=1, source_target_pairs={{0,2},{2,4},{4,6},{6,8},{8,10},{10,12},{12,14},{14,0},{1,3},{3,5},... | collective-permute-start | bytes 589832 | tf_op jit(solution)/shard_map/ppermute | solution.py:134
  99.4 9.6 %collective-permute-start.2 = (bf16[384,256]{1,0:T(8,128)(2,1)}, bf16[384,256]{1,0:T(8,128)(2,1)S(1)}, u32[]{:S(2)}, u32[]{:S(2)}) collective-permute-start(bf16[384,256]{1,0:T(8,128)(2,1)} %collective-permute-done.1), channel_id=1, source_target_pairs={{0,2},{2,4},{4,6},{6,8},{8,10},{10,12},{12,14},{14,0},{1,3},{3,5},... | collective-permute-start | bytes 589832 | tf_op jit(solution)/shard_map/ppermute | solution.py:134
  101.3 9.6 %collective-permute-start.5 = (bf16[384,256]{1,0:T(8,128)(2,1)S(1)}, bf16[384,256]{1,0:T(8,128)(2,1)S(1)}, u32[]{:S(2)}, u32[]{:S(2)}) collective-permute-start(bf16[384,256]{1,0:T(8,128)(2,1)S(1)} %pad_maximum_fusion), channel_id=1, source_target_pairs={{0,14},{2,0},{4,2},{6,4},{8,6},{10,8},{12,10},{14,12},{1,15},{3,1}... | collective-permute-start | bytes 589832 | tf_op jit(solution)/shard_map/ppermute | solution.py:137
  109.0 23.5 %copy-start.10 = (bf16[384,256]{1,0:T(8,128)(2,1)}, bf16[384,256]{1,0:T(8,128)(2,1)S(1)}, u32[]{:S(2)}) copy-start(bf16[384,256]{1,0:T(8,128)(2,1)S(1)} %collective-permute-done.2) | copy-start | bytes 589828
  109.0 8.6 %collective-permute-start.3 = (bf16[384,256]{1,0:T(8,128)(2,1)S(1)}, bf16[384,256]{1,0:T(8,128)(2,1)S(1)}, u32[]{:S(2)}, u32[]{:S(2)}) collective-permute-start(bf16[384,256]{1,0:T(8,128)(2,1)S(1)} %collective-permute-done.2), channel_id=1, source_target_pairs={{0,2},{2,4},{4,6},{6,8},{8,10},{10,12},{12,14},{14,0},{1,3},{3,5},... | collective-permute-start | bytes 589832 | tf_op jit(solution)/shard_map/ppermute | solution.py:134
  110.9 8.6 %copy-start.8 = (bf16[384,256]{1,0:T(8,128)(2,1)}, bf16[384,256]{1,0:T(8,128)(2,1)S(1)}, u32[]{:S(2)}) copy-start(bf16[384,256]{1,0:T(8,128)(2,1)S(1)} %collective-permute-done.5) | copy-start | bytes 589828
  110.9 16.8 %collective-permute-start.6 = (bf16[384,256]{1,0:T(8,128)(2,1)S(1)}, bf16[384,256]{1,0:T(8,128)(2,1)}, u32[]{:S(2)}, u32[]{:S(2)}) collective-permute-start(bf16[384,256]{1,0:T(8,128)(2,1)S(1)} %collective-permute-done.5), channel_id=1, source_target_pairs={{0,14},{2,0},{4,2},{6,4},{8,6},{10,8},{12,10},{14,12},{1,15},{3,1}... | collective-permute-start | bytes 589832 | tf_op jit(solution)/shard_map/ppermute | solution.py:137
  117.6 14.8 %copy-start.11 = (bf16[384,256]{1,0:T(8,128)(2,1)}, bf16[384,256]{1,0:T(8,128)(2,1)S(1)}, u32[]{:S(2)}) copy-start(bf16[384,256]{1,0:T(8,128)(2,1)S(1)} %collective-permute-done.3) | copy-start | bytes 589828
  117.6 14.8 %collective-permute-start.4 = (bf16[384,256]{1,0:T(8,128)(2,1)S(1)}, bf16[384,256]{1,0:T(8,128)(2,1)}, u32[]{:S(2)}, u32[]{:S(2)}) collective-permute-start(bf16[384,256]{1,0:T(8,128)(2,1)S(1)} %collective-permute-done.3), channel_id=1, source_target_pairs={{0,2},{2,4},{4,6},{6,8},{8,10},{10,12},{12,14},{14,0},{1,3},{3,5},... | collective-permute-start | bytes 589832 | tf_op jit(solution)/shard_map/ppermute | solution.py:134
  119.5 44.0 %all-to-all-start.1 = ((bf16[32,192,128]{2,1,0:T(8,128)(2,1)}), bf16[32,192,128]{2,1,0:T(8,128)(2,1)S(1)}, u32[]{:S(2)}, u32[]{:S(2)}) async-start(bf16[32,192,128]{2,1,0:T(8,128)(2,1)} %bitcast.16), calls=%async_computation.1 | async-start | bytes 3145728 | tf_op jit(solution)/shard_map/all_to_all | solution.py:239
  127.6 92.0 %all-gather.7.cloned.1.call-start = ((), (), s32[]{:S(2)}) async-start(), calls=%async_computation.3 | async-start | bytes 3342336 | tf_op jit(solution)/shard_map/all_gather | solution.py:247
  127.7 8.6 %copy-start.9 = (bf16[384,256]{1,0:T(8,128)(2,1)S(1)}, bf16[384,256]{1,0:T(8,128)(2,1)}, u32[]{:S(2)}) copy-start(bf16[384,256]{1,0:T(8,128)(2,1)} %copy-done.8) | copy-start | bytes 589828
  127.7 9.5 %collective-permute-start.7 = (bf16[384,256]{1,0:T(8,128)(2,1)}, bf16[384,256]{1,0:T(8,128)(2,1)S(1)}, u32[]{:S(2)}, u32[]{:S(2)}) collective-permute-start(bf16[384,256]{1,0:T(8,128)(2,1)} %collective-permute-done.6), channel_id=1, source_target_pairs={{0,14},{2,0},{4,2},{6,4},{8,6},{10,8},{12,10},{14,12},{1,15},{3,1}... | collective-permute-start | bytes 589832 | tf_op jit(solution)/shard_map/ppermute | solution.py:137
  137.3 7.8 %collective-permute-start.8 = (bf16[8,384,256]{2,1,0:T(8,128)(2,1)S(1)}, bf16[8,384,256]{2,1,0:T(8,128)(2,1)}, u32[]{:S(2)}, u32[]{:S(2)}) collective-permute-start(bf16[8,384,256]{2,1,0:T(8,128)(2,1)S(1)} %bitcast_dynamic-update-slice_fusion.mine), channel_id=1, source_target_pairs={{0,1},{1,0},{2,3},{3,2},{4,5},{5,4},{6,7},{7,6},{8,9},{9,8},{10,11... | collective-permute-start | bytes 4718600 | tf_op jit(solution)/shard_map/ppermute | solution.py:143
  145.1 2.2 copy-start
  150.9 24.6 %copy-start.5 = (f32[9]{0:T(128)S(1)}, f32[9]{0:T(128)}, u32[]{:S(2)}) copy-start(f32[9]{0:T(128)} %dwa.1) | copy-start | bytes 112
  150.9 24.6 %copy-start.7 = (bf16[8,384,256]{2,1,0:T(8,128)(2,1)S(1)}, bf16[8,384,256]{2,1,0:T(8,128)(2,1)}, u32[]{:S(2)}) copy-start(bf16[8,384,256]{2,1,0:T(8,128)(2,1)} %param.8) | copy-start | bytes 4718596
  168.6 6.2 %collective-permute-start.11 = (bf16[64,256]{1,0:T(8,128)(2,1)S(1)}, bf16[64,256]{1,0:T(8,128)(2,1)S(1)}, u32[]{:S(2)}, u32[]{:S(2)}) collective-permute-start(bf16[64,256]{1,0:T(8,128)(2,1)S(1)} %slice.29), channel_id=1, source_target_pairs={{0,16},{16,32},{32,48},{48,64},{64,80},{80,96},{96,112},{112,128},... | collective-permute-start | bytes 98312 | tf_op jit(solution)/shard_map/ppermute | solution.py:122
  219.7 2.2 copy-start.1
  221.8 1.9 copy-start.2
Sparse Core Ops, SparseCore 0:
  22.2 97.2 all-gather.4
  175.6 43.9 all-gather.6

commit v2 on v1

--- a/solution.py
+++ b/solution.py
@@ -1,3 +1,5 @@
+import functools
+
 import jax
 import jax.numpy as jnp
 from jax import lax
@@ -78,12 +80,13 @@
     )(ids, store)
 
 
-def attend_kernel(q_ref, kv_ref, o_ref):
-    slabs, slots, heads, rows, _ = kv_ref.shape
+def attend_kernel(first, q_ref, kv_ref, o_ref):
+    slabs, _, heads, rows, _ = kv_ref.shape
     keys = slabs * NNB * rows
     lane = lax.broadcasted_iota(jnp.int32, (SPAN, keys), 1)
     is_key = (lane & 1) == 0
-    for span in range(slots // NNB):
+    for at in range(o_ref.shape[0] // SPAN):
+        span = first + at
         tokens = slice(span * SPAN, (span + 1) * SPAN)
         for head in range(heads):
             columns = slice(head * HDIM, (head + 1) * HDIM)
@@ -102,17 +105,16 @@
             mixed = lax.dot_general(
                 on_values, rows_kv, (((1,), (0,)), ((), ())), preferred_element_type=jnp.float32
             )
-            o_ref[tokens, columns] = mixed.astype(jnp.bfloat16)
-
-
-def attend(queries, kv):
-    return pl.pallas_call(
-        attend_kernel,
-        out_shape=jax.ShapeDtypeStruct(queries.shape, jnp.bfloat16),
+            o_ref[at * SPAN : (at + 1) * SPAN, columns] = mixed.astype(jnp.bfloat16)
+
+
+def attend(queries, kv, first, spans):
+    return pl.pallas_call(
+        functools.partial(attend_kernel, first),
+        out_shape=jax.ShapeDtypeStruct((spans * SPAN, queries.shape[1]), jnp.bfloat16),
         in_specs=[vmem_space(), vmem_space()],
         out_specs=vmem_space(),
         compiler_params=ROOM,
-        name="attend",
     )(queries, kv)
 
 
@@ -149,8 +151,8 @@
 
     def body(i, total):
         at = lax.rem(z + i + steps - steps // 2, steps) * 2
-        w_mine = weights[pl.ds((at + core) * 2, 2), 0].reshape(depth, -1)
-        w_other = weights[pl.ds((at + 1 - core) * 2, 2), 0].reshape(depth, -1)
+        w_mine = weights[pl.ds((at + core) * 2, 2)].reshape(depth, -1)
+        w_other = weights[pl.ds((at + 1 - core) * 2, 2)].reshape(depth, -1)
         total += jnp.dot(mine[i], w_mine, preferred_element_type=jnp.float32)
         total += jnp.dot(other[i], w_other, preferred_element_type=jnp.float32)
         return total
@@ -160,7 +162,7 @@
 
 
 def project(place, mine, other, weights):
-    rows, width = mine.shape[1], weights.shape[3]
+    rows, width = mine.shape[1], weights.shape[2]
     return pl.pallas_call(
         project_kernel,
         out_shape=jax.ShapeDtypeStruct((rows, width), jnp.bfloat16),
@@ -171,30 +173,56 @@
     )(place, mine, other, weights)
 
 
-def finish_kernel(dwa, attended, weights, stream, past, block_out, dense_out):
-    groups, _, depth = attended.shape
-
-    def body(g, total):
-        w = weights[pl.ds(g * 2, 2), 1].reshape(depth, -1)
-        part = jnp.dot(attended[g], w, preferred_element_type=jnp.float32)
-        return total + part.astype(jnp.bfloat16).astype(jnp.float32)
-
-    total = lax.fori_loop(0, groups, body, jnp.zeros(stream.shape, jnp.float32))
-    block = stream[...].astype(jnp.float32) + total
-    block_out[...] = block.astype(block_out.dtype)
-    dense_out[...] = (dwa[dwa.shape[0] - 1] * block + past[...]).astype(dense_out.dtype)
-
-
-def finish(dwa, attended, weights, stream, past):
+def finish_kernel(x, dwa, attended, weights, stream, past, block_out, dense_out, total):
+    step = pl.program_id(0)
+    across, _, depth, _ = weights.shape
+
+    @pl.when(step == 0)
+    def _():
+        total[...] = jnp.zeros(total.shape, jnp.float32)
+
+    pieces = attended.shape[2] // depth
+    for g in range(attended.shape[0]):
+        part = jnp.zeros(total.shape, jnp.float32)
+        for piece in range(pieces):
+            at = lax.rem(g * pieces + piece + across - x[0], across)
+            part += jnp.dot(
+                attended[g, :, piece * depth : (piece + 1) * depth],
+                weights[at, 0],
+                preferred_element_type=jnp.float32,
+            )
+        total[...] += part.astype(jnp.bfloat16).astype(jnp.float32)
+
+    @pl.when(step == pl.num_programs(0) - 1)
+    def _():
+        block = stream[...].astype(jnp.float32) + total[...]
+        block_out[...] = block.astype(block_out.dtype)
+        dense_out[...] = (dwa[dwa.shape[0] - 1] * block + past[...]).astype(dense_out.dtype)
+
+
+def finish(x, dwa, attended, weights, stream, past):
+    groups, rows, depth = attended.shape
+    across, along, cut, width = weights.shape
+    here = groups // along
+    scalars = pl.BlockSpec(memory_space=pltpu.SMEM)
+    whole = pl.BlockSpec(stream.shape, lambda i: (0, 0))
     shape = jax.ShapeDtypeStruct(stream.shape, jnp.bfloat16)
     return pl.pallas_call(
         finish_kernel,
+        grid=(along,),
         out_shape=(shape, shape),
-        in_specs=[pl.BlockSpec(memory_space=pltpu.SMEM)] + [vmem_space()] * 4,
-        out_specs=(vmem_space(), vmem_space()),
-        compiler_params=ROOM,
+        in_specs=[
+            scalars,
+            scalars,
+            pl.BlockSpec((here, rows, depth), lambda i: (i, 0, 0)),
+            pl.BlockSpec((across, 1, cut, width), lambda i: (0, i, 0, 0)),
+            whole,
+            whole,
+        ],
+        out_specs=(whole, whole),
+        scratch_shapes=[pltpu.VMEM(stream.shape, jnp.float32)],
         name="finish",
-    )(dwa, attended, weights, stream, past)
+    )(x, dwa, attended, weights, stream, past)
 
 
 def columns_here(w_out):
@@ -216,36 +244,53 @@
     return jnp.where(odd == 0, straight, crossed)
 
 
+def along_x(block):
+    count = lax.axis_size("x")
+    half = block.shape[0] // 2
+    before = lax.ppermute(block, "x", ring(count, 1))
+    after = lax.ppermute(block, "x", ring(count, -1))
+    low = lax.ppermute(before[:half], "x", ring(count, 1))
+    high = lax.ppermute(after[half:], "x", ring(count, -1))
+    return jnp.stack([block, after, jnp.concatenate([low, high], 0), before])
+
+
 def on_device(stream, history, dwa_weights, w_query, w_out, encoded_kv, neighbour_ids):
-    tok_rows = stream.shape[0]
+    tok_rows, _ = stream.shape
     local_heads = w_query.shape[1] // HDIM
     ctx_count = lax.axis_size(CTX)
     db_count = lax.axis_size(DB)
     slots = neighbour_ids.shape[0] // ctx_count
     slab_rows = 2 * encoded_kv.shape[2]
     place = jnp.stack([lax.axis_index("z"), lax.axis_index("core")]).astype(jnp.int32)
-
-    weights = lax.all_gather(jnp.stack([w_query, columns_here(w_out)]), CTX, axis=0)
-    after = shifted(stream[:SPAN], -1)
-    own_spans = jnp.concatenate([stream[LEAD:], after[:LEAD]], 0)
-    past = jnp.sum(history.astype(jnp.float32) * dwa_weights[:-1, None, None], axis=0)
-
+    x = lax.axis_index("x").astype(jnp.int32).reshape(1)
+
+    w_in = lax.all_gather(w_query, CTX, axis=0)
     by_head = split_heads(encoded_kv, local_heads)
     store = lax.all_to_all(
         by_head.reshape(db_count, -1, HDIM), DB, split_axis=0, concat_axis=0, tiled=True
     )
+    after = shifted(stream[:SPAN], -1)
+    own_spans = jnp.concatenate([stream[LEAD:], after[:LEAD]], 0)
+    turned = columns_here(w_out)
+    turned = lax.all_gather(turned, "y", axis=0)
+
     picked = pick(neighbour_ids, store.reshape(-1, local_heads * slab_rows, HDIM))
-    own_spans, picked = lax.optimization_barrier((own_spans, picked))
+    own_spans, turned, picked = lax.optimization_barrier((own_spans, turned, picked))
     arrived = lax.all_to_all(
         picked.reshape(ctx_count, -1, HDIM), CTX, split_axis=0, concat_axis=0, tiled=True
     ).reshape(ctx_count, slots, local_heads, slab_rows, HDIM)
     mine = around(own_spans, "z")
-    queries = project(place, mine, partner(mine), weights)
-    mixed = attend(queries, arrived)
-    before = shifted(mixed[tok_rows - SPAN :], 1)
-    attended = jnp.concatenate([before[1:], mixed[: tok_rows - LEAD]], 0)
+    past = jnp.sum(history.astype(jnp.float32) * dwa_weights[:-1, None, None], axis=0)
+    queries = project(place, mine, partner(mine), w_in)
+    spans = tok_rows // SPAN
+    last = attend(queries, arrived, spans - 1, 1)
+    before = shifted(last, 1)
+    rest = attend(queries, arrived, 0, spans - 1)
+    attended = jnp.concatenate([before[1:], rest, last[:1]], 0)
+    attended, turned = lax.optimization_barrier((attended, turned))
     everyone = lax.all_gather(attended, DB, axis=0)
-    return finish(dwa_weights, everyone, weights, stream, past)
+    columns = along_x(turned)
+    return finish(x, dwa_weights, everyone, columns, stream, past)
 
 
 def solution(mesh):

time: 237 us -> 238 us (level)
  waiting for transfers between devices: 115 us -> 73.3 us
  blocking collectives: 0 us -> 36.7 us
  starting transfers between devices: 70.5 us -> 79 us
  local copies, waits for them, and re-layouts: 13.3 us -> 6.98 us
    all_gather x0 -> x1, blocking collectives: none -> 36.7 us  [on_device(): turned = lax.all_gather(turned, 'y', axis=0)]
    all_to_all x1, waiting for transfers between devices: 33.8 us -> 0.01 us  [on_device(): lax.all_to_all(by_head.reshape(db_count, -1, HDIM), DB, split_axis=0, con...]
    all_gather x1, waiting for transfers between devices: 0.01 us -> 32.6 us  [on_device(): w_in = lax.all_gather(w_query, CTX, axis=0)]
    all_gather x1, waiting for transfers between devices: 43.7 us -> 22.4 us  [on_device(): everyone = lax.all_gather(attended, DB, axis=0)]
    ppermute x0 -> x4, starting transfers between devices: none -> 13 us  [the longest x1 4.04 us: along_x(): high = lax.ppermute(after[half:], 'x', ring(count, -1))]
    all_to_all x1, waiting for transfers between devices: 12.6 us -> 0.01 us  [on_device(): lax.all_to_all(picked.reshape(ctx_count, -1, HDIM), CTX, split_axis=0, co...]
    all_to_all x1, starting transfers between devices: 21.8 us -> 12 us  [on_device(): lax.all_to_all(by_head.reshape(db_count, -1, HDIM), DB, split_axis=0, con...]
    ppermute x1, starting transfers between devices: 4.64 us -> 13.2 us  [partner(): return lax.ppermute(block, 'core', [(0, 1), (1, 0)])]
  transfers between devices with their start and end apart: 16 -> 20, of which waited for: 10 -> 9; matrix products, arithmetic and copies ran while one was open for 2% -> 3% of each run, Pallas kernels for 4% -> 3%
where the time goes in v2:
time: 238 us; the launch traced here: 237 us
  starting transfers between devices  79 us (33%)
  waiting for transfers between devices  73.3 us (31%)
  blocking collectives  36.7 us (15%)
  Pallas kernels  21.8 us (9%)
  between operations  14.5 us (6%)
  local copies, waits for them, and re-layouts  6.98 us (3%)
  other arithmetic  5.06 us (2%)
    all_gather x1, blocking collectives, on_device(): turned = lax.all_gather(turned, 'y', axis=0)  36.7 us
    all_gather x1, waiting for transfers between devices, on_device(): w_in = lax.all_gather(w_query, CTX, axis=0)  32.6 us
    all_gather x1, waiting for transfers between devices, on_device(): everyone = lax.all_gather(attended, DB, axis=0)  22.4 us
    ppermute x3, starting transfers between devices, around(): left = lax.ppermute(left, axis, ring(count, -1))  13.8 us
    ppermute x1, starting transfers between devices, partner(): return lax.ppermute(block, 'core', [(0, 1), (1, 0)])  13.2 us
    all_to_all x1, starting transfers between devices, on_device(): lax.all_to_all(by_head.reshape(db_count, -1, HDIM), DB, split_axis=0, con...  12 us
    ppermute x4, waiting for transfers between devices, around(): right = lax.ppermute(right, axis, ring(count, 1))  8.28 us
    ppermute x2, starting transfers between devices, columns_here(): pieces.append(lax.ppermute(send, CTX + DB, route))  7.7 us
  transfers between devices with their start and end apart: 20, of which 9 were waited for; matrix products, arithmetic and copies ran while one was open for 3% of the time, Pallas kernels for 3%

profile of v2, /device:TPU:1, one launch (start us, length us, event | category | flops | bytes accessed | tf_op | source)
XLA Modules:
  0.0 237.4 jit_solution(499542713656083930)
XLA Ops:
  7.2 1.4 copy-done.1
  8.6 3.1 %split_heads.1 = bf16[16,24,2,4,2,128]{5,4,3,2,1,0:T(2,128)(2,1)} custom-call(bf16[1,24,4,2,4096]{4,3,2,1,0:T(2,128)(2,1)S(1)} %copy-done.1), custom_call_target="tpu_custom_call" | custom-call | tf_op jit(solution)/shard_map/split_heads/pallas_call | solution.py:45
  11.7 0.0 copy-start.9
  11.7 0.0 copy-start.4
  11.8 12.0 %all-to-all-start = ((bf16[16,384,128]{2,1,0:T(8,128)(2,1)}), bf16[16,384,128]{2,1,0:T(8,128)(2,1)S(1)}, u32[]{:S(2)}, u32[]{:S(2)}) async-start(bf16[16,384,128]{2,1,0:T(8,128)(2,1)} %bitcast.5), calls=%async_computation | async-start | bytes 3145728 | tf_op jit(solution)/shard_map/all_to_all | solution.py:269
  23.7 0.0 all-gather.5.cloned.1.call-start
  23.8 0.0 copy-done.9
  23.8 4.6 %collective-permute-start.1 = (bf16[128,128]{1,0:T(8,128)(2,1)S(1)}, bf16[128,128]{1,0:T(8,128)(2,1)S(1)}, u32[]{:S(2)}, u32[]{:S(2)}) collective-permute-start(bf16[128,128]{1,0:T(8,128)(2,1)S(1)} %get-tuple-element.12), channel_id=1, source_target_pairs={{0,0},{1,32},{2,64},{3,96},{4,128},{5,160},{6,192},{7,224},{8,256}... | collective-permute-start | bytes 98312 | tf_op jit(solution)/shard_map/ppermute | solution.py:241
  28.5 3.1 %collective-permute-start.2 = (bf16[128,128]{1,0:T(8,128)(2,1)S(1)}, bf16[128,128]{1,0:T(8,128)(2,1)S(1)}, u32[]{:S(2)}, u32[]{:S(2)}) collective-permute-start(bf16[128,128]{1,0:T(8,128)(2,1)S(1)} %get-tuple-element.13), channel_id=1, source_target_pairs={{0,16},{1,48},{2,80},{3,112},{4,144},{5,176},{6,208},{7,240},{8,27... | collective-permute-start | bytes 98312 | tf_op jit(solution)/shard_map/ppermute | solution.py:241
  31.6 1.3 collective-permute-start
  32.9 0.0 collective-permute-done.1
  32.9 2.3 collective-permute-done.2
  35.3 1.3 collective-permute-done
  36.6 36.7 %all_gather.16 = bf16[8,128,256]{2,1,0:T(8,128)(2,1)} all-gather(bf16[1,128,256]{2,1,0:T(8,128)(2,1)S(1)} %maximum_select_fusion), channel_id=1, replica_groups=mesh['y'=8,'x'=4,'z'=8,'core'=2] {'y'}, dimensions={0}, use_global_device_ids=true | all-gather | bytes 589824 | tf_op jit(solution)/shard_map/all_gather | solution.py:275
  73.2 0.0 all-to-all-done
  73.2 2.4 pick.1
  75.6 1.9 collective-permute-start.3
  77.5 0.0 all-gather.5.cloned.1.call-update
  77.5 5.7 %collective-permute-done.3 = bf16[384,256]{1,0:T(8,128)(2,1)S(1)} collective-permute-done((bf16[384,256]{1,0:T(8,128)(2,1)S(1)}, bf16[384,256]{1,0:T(8,128)(2,1)S(1)}, u32[]{:S(2)}, u32[]{:S(2)}) %collective-permute-start.3) | collective-permute-done | bytes 196640 | tf_op jit(solution)/shard_map/ppermute | solution.py:136
  83.2 1.9 collective-permute-start.4
  85.1 4.6 %collective-permute-start.7 = (bf16[384,256]{1,0:T(8,128)(2,1)S(1)}, bf16[384,256]{1,0:T(8,128)(2,1)S(1)}, u32[]{:S(2)}, u32[]{:S(2)}) collective-permute-start(bf16[384,256]{1,0:T(8,128)(2,1)S(1)} %pad_maximum_fusion.1), channel_id=1, source_target_pairs={{0,14},{2,0},{4,2},{6,4},{8,6},{10,8},{12,10},{14,12},{1,15},{3,1}... | collective-permute-start | bytes 589832 | tf_op jit(solution)/shard_map/ppermute | solution.py:139
  89.7 1.1 collective-permute-done.4
  90.8 1.9 collective-permute-start.5
  92.7 0.0 collective-permute-done.7
  92.8 4.6 %collective-permute-start.8 = (bf16[384,256]{1,0:T(8,128)(2,1)S(1)}, bf16[384,256]{1,0:T(8,128)(2,1)}, u32[]{:S(2)}, u32[]{:S(2)}) collective-permute-start(bf16[384,256]{1,0:T(8,128)(2,1)S(1)} %collective-permute-done.7), channel_id=1, source_target_pairs={{0,14},{2,0},{4,2},{6,4},{8,6},{10,8},{12,10},{14,12},{1,15},{3,1}... | collective-permute-start | bytes 589832 | tf_op jit(solution)/shard_map/ppermute | solution.py:139
  97.4 1.5 collective-permute-done.5
  98.8 1.9 collective-permute-start.6
  100.8 7.3 %all-to-all-start.1 = ((bf16[32,192,128]{2,1,0:T(8,128)(2,1)}), bf16[32,192,128]{2,1,0:T(8,128)(2,1)S(1)}, u32[]{:S(2)}, u32[]{:S(2)}) async-start(bf16[32,192,128]{2,1,0:T(8,128)(2,1)} %bitcast.16), calls=%async_computation.1 | async-start | bytes 3145728 | tf_op jit(solution)/shard_map/all_to_all | solution.py:279
  108.0 0.0 all-gather.7.cloned.1.call-start
  108.1 0.0 collective-permute-done.8
  108.1 4.7 %collective-permute-start.9 = (bf16[384,256]{1,0:T(8,128)(2,1)}, bf16[384,256]{1,0:T(8,128)(2,1)S(1)}, u32[]{:S(2)}, u32[]{:S(2)}) collective-permute-start(bf16[384,256]{1,0:T(8,128)(2,1)} %collective-permute-done.8), channel_id=1, source_target_pairs={{0,14},{2,0},{4,2},{6,4},{8,6},{10,8},{12,10},{14,12},{1,15},{3,1}... | collective-permute-start | bytes 589832 | tf_op jit(solution)/shard_map/ppermute | solution.py:139
  112.8 0.0 collective-permute-done.6
  112.9 0.9 bitcast_dynamic-update-slice_fusion.7
  113.8 0.9 bitcast_dynamic-update-slice_fusion.6
  114.8 0.9 bitcast_dynamic-update-slice_fusion.5
  115.8 0.9 bitcast_dynamic-update-slice_fusion.1
  116.7 0.0 collective-permute-done.9
  116.8 13.2 %collective-permute-start.10 = (bf16[8,384,256]{2,1,0:T(8,128)(2,1)S(1)}, bf16[8,384,256]{2,1,0:T(8,128)(2,1)}, u32[]{:S(2)}, u32[]{:S(2)}) collective-permute-start(bf16[8,384,256]{2,1,0:T(8,128)(2,1)S(1)} %bitcast_dynamic-update-slice_fusion.mine), channel_id=1, source_target_pairs={{0,1},{1,0},{2,3},{3,2},{4,5},{5,4},{6,7},{7,6},{8,9},{9,8},{10,11... | collective-permute-start | bytes 4718600 | tf_op jit(solution)/shard_map/ppermute | solution.py:145
  129.9 0.1 pad_add_fusion.place
  130.0 32.6 %all-gather.5.cloned.1.call-done = bf16[4096,256]{1,0:T(8,128)(2,1)} async-done(((bf16[128,256]{1,0:T(8,128)(2,1)}), bf16[4096,256]{1,0:T(8,128)(2,1)}) %all-gather.5.cloned.1.call-update) | async-done | bytes 2097168 | tf_op jit(solution)/shard_map/all_gather | solution.py:267
  162.6 0.0 collective-permute-done.10.other
  162.6 1.6 copy-done
  164.2 3.7 %project.1.q_ref = bf16[384,256]{1,0:T(8,128)(2,1)S(1)} custom-call(s32[2]{0:T(128)S(1)} %pad_add_fusion.place, bf16[8,384,256]{2,1,0:T(8,128)(2,1)S(1)} %bitcast_dynamic-update-slice_fusion.mine, bf16[8,384,256]{2,1,0:T(8,128)(2,1)} %collective-permute-done.10.other, bf16[32,128,256]{2,1,0:T(8,128)(2,1)S(1)} %bitcast.37), custom_call_target="tpu_custom_call" | custom-call | tf_op jit(solution)/shard_map/project/pallas_call | solution.py:166
  167.9 0.0 all-to-all-done.1
  167.9 1.0 shard_map.86
  168.9 0.0 copy-start.10
  168.9 3.1 %collective-permute-start.11 = (bf16[64,256]{1,0:T(8,128)(2,1)S(1)}, bf16[64,256]{1,0:T(8,128)(2,1)S(1)}, u32[]{:S(2)}, u32[]{:S(2)}) collective-permute-start(bf16[64,256]{1,0:T(8,128)(2,1)S(1)} %shard_map.86), channel_id=1, source_target_pairs={{0,16},{16,32},{32,48},{48,64},{64,80},{80,96},{96,112},{112,128},... | collective-permute-start | bytes 98312 | tf_op jit(solution)/shard_map/ppermute | solution.py:124
  172.0 4.2 %shard_map.87 = bf16[320,256]{1,0:T(8,128)(2,1)S(1)} custom-call(bf16[384,256]{1,0:T(8,128)(2,1)S(1)} %project.1.q_ref, bf16[32,12,2,8,128]{4,3,2,1,0:T(8,128)(2,1)S(1)} %bitcast.35), custom_call_target="tpu_custom_call" | custom-call | tf_op jit(solution)/shard_map/pallas_call | solution.py:112
  176.2 0.0 collective-permute-done.11
  176.3 0.7 pad_maximum_fusion.2
  177.0 0.0 all-gather.7.cloned.1.call-update
  177.0 3.0 %collective-permute-start.13 = (bf16[8,128,256]{2,1,0:T(8,128)(2,1)S(1)}, bf16[8,128,256]{2,1,0:T(8,128)(2,1)S(1)}, u32[]{:S(2)}, u32[]{:S(2)}) collective-permute-start(bf16[8,128,256]{2,1,0:T(8,128)(2,1)S(1)} %copy-done.3), channel_id=1, source_target_pairs={{0,16},{16,32},{32,48},{48,0},{1,17},{17,33},{33,49},{49,1},{2,18}... | collective-permute-start | bytes 1572872 | tf_op jit(solution)/shard_map/ppermute | solution.py:250
  180.0 3.5 %collective-permute-start.12 = (bf16[8,128,256]{2,1,0:T(8,128)(2,1)S(1)}, bf16[8,128,256]{2,1,0:T(8,128)(2,1)S(1)}, u32[]{:S(2)}, u32[]{:S(2)}) collective-permute-start(bf16[8,128,256]{2,1,0:T(8,128)(2,1)S(1)} %copy-done.3), channel_id=1, source_target_pairs={{0,48},{16,0},{32,16},{48,32},{1,49},{17,1},{33,17},{49,33},{2,50}... | collective-permute-start | bytes 1572872 | tf_op jit(solution)/shard_map/ppermute | solution.py:251
  183.5 5.6 %collective-permute-done.13 = bf16[8,128,256]{2,1,0:T(8,128)(2,1)S(1)} collective-permute-done((bf16[8,128,256]{2,1,0:T(8,128)(2,1)S(1)}, bf16[8,128,256]{2,1,0:T(8,128)(2,1)S(1)}, u32[]{:S(2)}, u32[]{:S(2)}) %collective-permute-start.13) | collective-permute-done | bytes 524320 | tf_op jit(solution)/shard_map/ppermute | solution.py:250
  189.1 2.5 %collective-permute-start.14 = (bf16[4,128,256]{2,1,0:T(8,128)(2,1)S(1)}, bf16[4,128,256]{2,1,0:T(8,128)(2,1)S(1)}, u32[]{:S(2)}, u32[]{:S(2)}) collective-permute-start(bf16[4,128,256]{2,1,0:T(8,128)(2,1)S(1)} %slice.35), channel_id=1, source_target_pairs={{0,16},{16,32},{32,48},{48,0},{1,17},{17,33},{33,49},{49,1},{2,18}... | collective-permute-start | bytes 786440 | tf_op jit(solution)/shard_map/ppermute | solution.py:252
  191.6 0.0 collective-permute-done.12
  191.6 4.0 %collective-permute-start.15 = (bf16[4,128,256]{2,1,0:T(8,128)(2,1)S(1)}, bf16[4,128,256]{2,1,0:T(8,128)(2,1)S(1)}, u32[]{:S(2)}, u32[]{:S(2)}) collective-permute-start(bf16[4,128,256]{2,1,0:T(8,128)(2,1)S(1)} %slice.36), channel_id=1, source_target_pairs={{0,48},{16,0},{32,16},{48,32},{1,49},{17,1},{33,17},{49,33},{2,50}... | collective-permute-start | bytes 786440 | tf_op jit(solution)/shard_map/ppermute | solution.py:253
  195.7 0.0 copy-done.10
  195.7 2.6 %multiply_reduce_fusion.past = f32[384,256]{1,0:T(8,128)} fusion(bf16[8,384,256]{2,1,0:T(8,128)(2,1)} %param.8, f32[8]{0:T(128)S(1)} %bitcast.45), kind=kLoop, calls=%fused_computation | loop fusion | flops 2260992 | bytes 1966112 | tf_op jit(solution)/shard_map/reduce_sum | solution.py:283
  198.3 0.0 collective-permute-done.14
  198.3 0.9 collective-permute-done.15
  199.2 1.6 pad_maximum_fusion.weights
  200.8 22.4 %all-gather.7.cloned.1.call-done = bf16[6144,256]{1,0:T(8,128)(2,1)} async-done(((bf16[384,256]{1,0:T(8,128)(2,1)}), bf16[6144,256]{1,0:T(8,128)(2,1)}) %all-gather.7.cloned.1.call-update) | async-done | bytes 3145744 | tf_op jit(solution)/shard_map/all_gather | solution.py:291
  223.2 7.4 %finish.1 = (bf16[384,256]{1,0:T(8,128)(2,1)}, bf16[384,256]{1,0:T(8,128)(2,1)}) custom-call(s32[1]{0:T(128)} %bitcast.x, f32[9]{0:T(128)} %dwa.1, bf16[16,384,256]{2,1,0:T(8,128)(2,1)} %bitcast.38, bf16[4,8,128,256]{3,2,1,0:T(8,128)(2,1)} %pad_maximum_fusion.weights, bf16[384,256]{1,0:T(8,128)(2,1)} %stream.1, f32[384,256]{1,0:T(8,128)} %multiply_reduce_fusion.past), custom_call_target="tpu_custom_call" | custom-call | tf_op jit(solution)/shard_map/finish/pallas_call | solution.py:210
  (29 shorter events, 0.3 us)
Async XLA Ops:
  7.2 1.4 copy-start.1
  11.7 12.1 %copy-start.9 = (bf16[256,128]{1,0:T(8,128)(2,1)S(1)}, bf16[256,128]{1,0:T(8,128)(2,1)}, u32[]{:S(2)}) copy-start(bf16[256,128]{1,0:T(8,128)(2,1)} %param.11) | copy-start | bytes 196612
  11.7 19.8 %copy-start.4 = (bf16[384,256]{1,0:T(8,128)(2,1)S(1)}, bf16[384,256]{1,0:T(8,128)(2,1)}, u32[]{:S(2)}) copy-start(bf16[384,256]{1,0:T(8,128)(2,1)} %stream.1) | copy-start | bytes 589828
  11.8 61.5 %all-to-all-start = ((bf16[16,384,128]{2,1,0:T(8,128)(2,1)}), bf16[16,384,128]{2,1,0:T(8,128)(2,1)S(1)}, u32[]{:S(2)}, u32[]{:S(2)}) async-start(bf16[16,384,128]{2,1,0:T(8,128)(2,1)} %bitcast.5), calls=%async_computation | async-start | bytes 3145728 | tf_op jit(solution)/shard_map/all_to_all | solution.py:269
  23.7 49.5 %copy-start.2 = (s32[384]{0:T(512)S(1)}, s32[384]{0:T(512)}, u32[]{:S(2)}) copy-start(s32[384]{0:T(512)} %ids.1) | copy-start | bytes 4612
  23.7 138.9 %all-gather.5.cloned.1.call-start = ((), (), s32[]{:S(2)}) async-start(), calls=%async_computation.2 | async-start | bytes 2162688 | tf_op jit(solution)/shard_map/all_gather | solution.py:267
  23.8 9.1 %collective-permute-start.1 = (bf16[128,128]{1,0:T(8,128)(2,1)S(1)}, bf16[128,128]{1,0:T(8,128)(2,1)S(1)}, u32[]{:S(2)}, u32[]{:S(2)}) collective-permute-start(bf16[128,128]{1,0:T(8,128)(2,1)S(1)} %get-tuple-element.12), channel_id=1, source_target_pairs={{0,0},{1,32},{2,64},{3,96},{4,128},{5,160},{6,192},{7,224},{8,256}... | collective-permute-start | bytes 98312 | tf_op jit(solution)/shard_map/ppermute | solution.py:241
  28.5 6.7 %collective-permute-start.2 = (bf16[128,128]{1,0:T(8,128)(2,1)S(1)}, bf16[128,128]{1,0:T(8,128)(2,1)S(1)}, u32[]{:S(2)}, u32[]{:S(2)}) collective-permute-start(bf16[128,128]{1,0:T(8,128)(2,1)S(1)} %get-tuple-element.13), channel_id=1, source_target_pairs={{0,16},{1,48},{2,80},{3,112},{4,144},{5,176},{6,208},{7,240},{8,27... | collective-permute-start | bytes 98312 | tf_op jit(solution)/shard_map/ppermute | solution.py:241
  31.6 5.0 %collective-permute-start = (bf16[64,256]{1,0:T(8,128)(2,1)S(1)}, bf16[64,256]{1,0:T(8,128)(2,1)S(1)}, u32[]{:S(2)}, u32[]{:S(2)}) collective-permute-start(bf16[64,256]{1,0:T(8,128)(2,1)S(1)} %slice.25), channel_id=1, source_target_pairs={{16,0},{32,16},{48,32},{64,48},{80,64},{96,80},{112,96},{128,112},... | collective-permute-start | bytes 98312 | tf_op jit(solution)/shard_map/ppermute | solution.py:124
  75.6 7.6 %collective-permute-start.3 = (bf16[384,256]{1,0:T(8,128)(2,1)S(1)}, bf16[384,256]{1,0:T(8,128)(2,1)S(1)}, u32[]{:S(2)}, u32[]{:S(2)}) collective-permute-start(bf16[384,256]{1,0:T(8,128)(2,1)S(1)} %pad_maximum_fusion.1), channel_id=1, source_target_pairs={{0,2},{2,4},{4,6},{6,8},{8,10},{10,12},{12,14},{14,0},{1,3},{3,5},... | collective-permute-start | bytes 589832 | tf_op jit(solution)/shard_map/ppermute | solution.py:136
  83.2 7.6 %collective-permute-start.4 = (bf16[384,256]{1,0:T(8,128)(2,1)S(1)}, bf16[384,256]{1,0:T(8,128)(2,1)S(1)}, u32[]{:S(2)}, u32[]{:S(2)}) collective-permute-start(bf16[384,256]{1,0:T(8,128)(2,1)S(1)} %collective-permute-done.3), channel_id=1, source_target_pairs={{0,2},{2,4},{4,6},{6,8},{8,10},{10,12},{12,14},{14,0},{1,3},{3,5},... | collective-permute-start | bytes 589832 | tf_op jit(solution)/shard_map/ppermute | solution.py:136
  85.1 7.6 %collective-permute-start.7 = (bf16[384,256]{1,0:T(8,128)(2,1)S(1)}, bf16[384,256]{1,0:T(8,128)(2,1)S(1)}, u32[]{:S(2)}, u32[]{:S(2)}) collective-permute-start(bf16[384,256]{1,0:T(8,128)(2,1)S(1)} %pad_maximum_fusion.1), channel_id=1, source_target_pairs={{0,14},{2,0},{4,2},{6,4},{8,6},{10,8},{12,10},{14,12},{1,15},{3,1}... | collective-permute-start | bytes 589832 | tf_op jit(solution)/shard_map/ppermute | solution.py:139
  90.8 22.0 %copy-start.7 = (bf16[384,256]{1,0:T(8,128)(2,1)}, bf16[384,256]{1,0:T(8,128)(2,1)S(1)}, u32[]{:S(2)}) copy-start(bf16[384,256]{1,0:T(8,128)(2,1)S(1)} %collective-permute-done.4) | copy-start | bytes 589828
  90.8 8.0 %collective-permute-start.5 = (bf16[384,256]{1,0:T(8,128)(2,1)S(1)}, bf16[384,256]{1,0:T(8,128)(2,1)S(1)}, u32[]{:S(2)}, u32[]{:S(2)}) collective-permute-start(bf16[384,256]{1,0:T(8,128)(2,1)S(1)} %collective-permute-done.4), channel_id=1, source_target_pairs={{0,2},{2,4},{4,6},{6,8},{8,10},{10,12},{12,14},{14,0},{1,3},{3,5},... | collective-permute-start | bytes 589832 | tf_op jit(solution)/shard_map/ppermute | solution.py:136
  92.8 8.0 %copy-start.5 = (bf16[384,256]{1,0:T(8,128)(2,1)}, bf16[384,256]{1,0:T(8,128)(2,1)S(1)}, u32[]{:S(2)}) copy-start(bf16[384,256]{1,0:T(8,128)(2,1)S(1)} %collective-permute-done.7) | copy-start | bytes 589828
  92.8 15.3 %collective-permute-start.8 = (bf16[384,256]{1,0:T(8,128)(2,1)S(1)}, bf16[384,256]{1,0:T(8,128)(2,1)}, u32[]{:S(2)}, u32[]{:S(2)}) collective-permute-start(bf16[384,256]{1,0:T(8,128)(2,1)S(1)} %collective-permute-done.7), channel_id=1, source_target_pairs={{0,14},{2,0},{4,2},{6,4},{8,6},{10,8},{12,10},{14,12},{1,15},{3,1}... | collective-permute-start | bytes 589832 | tf_op jit(solution)/shard_map/ppermute | solution.py:139
  98.8 14.0 %copy-start.8 = (bf16[384,256]{1,0:T(8,128)(2,1)}, bf16[384,256]{1,0:T(8,128)(2,1)S(1)}, u32[]{:S(2)}) copy-start(bf16[384,256]{1,0:T(8,128)(2,1)S(1)} %collective-permute-done.5) | copy-start | bytes 589828
  98.8 14.0 %collective-permute-start.6 = (bf16[384,256]{1,0:T(8,128)(2,1)S(1)}, bf16[384,256]{1,0:T(8,128)(2,1)}, u32[]{:S(2)}, u32[]{:S(2)}) collective-permute-start(bf16[384,256]{1,0:T(8,128)(2,1)S(1)} %collective-permute-done.5), channel_id=1, source_target_pairs={{0,2},{2,4},{4,6},{6,8},{8,10},{10,12},{12,14},{14,0},{1,3},{3,5},... | collective-permute-start | bytes 589832 | tf_op jit(solution)/shard_map/ppermute | solution.py:136
  100.8 67.1 %all-to-all-start.1 = ((bf16[32,192,128]{2,1,0:T(8,128)(2,1)}), bf16[32,192,128]{2,1,0:T(8,128)(2,1)S(1)}, u32[]{:S(2)}, u32[]{:S(2)}) async-start(bf16[32,192,128]{2,1,0:T(8,128)(2,1)} %bitcast.16), calls=%async_computation.1 | async-start | bytes 3145728 | tf_op jit(solution)/shard_map/all_to_all | solution.py:279
  108.0 115.1 %all-gather.7.cloned.1.call-start = ((), (), s32[]{:S(2)}) async-start(), calls=%async_computation.3 | async-start | bytes 3342336 | tf_op jit(solution)/shard_map/all_gather | solution.py:291
  108.1 7.7 %copy-start.6 = (bf16[384,256]{1,0:T(8,128)(2,1)S(1)}, bf16[384,256]{1,0:T(8,128)(2,1)}, u32[]{:S(2)}) copy-start(bf16[384,256]{1,0:T(8,128)(2,1)} %copy-done.5) | copy-start | bytes 589828
  108.1 8.6 %collective-permute-start.9 = (bf16[384,256]{1,0:T(8,128)(2,1)}, bf16[384,256]{1,0:T(8,128)(2,1)S(1)}, u32[]{:S(2)}, u32[]{:S(2)}) collective-permute-start(bf16[384,256]{1,0:T(8,128)(2,1)} %collective-permute-done.8), channel_id=1, source_target_pairs={{0,14},{2,0},{4,2},{6,4},{8,6},{10,8},{12,10},{14,12},{1,15},{3,1}... | collective-permute-start | bytes 589832 | tf_op jit(solution)/shard_map/ppermute | solution.py:139
  116.8 45.9 %collective-permute-start.10 = (bf16[8,384,256]{2,1,0:T(8,128)(2,1)S(1)}, bf16[8,384,256]{2,1,0:T(8,128)(2,1)}, u32[]{:S(2)}, u32[]{:S(2)}) collective-permute-start(bf16[8,384,256]{2,1,0:T(8,128)(2,1)S(1)} %bitcast_dynamic-update-slice_fusion.mine), channel_id=1, source_target_pairs={{0,1},{1,0},{2,3},{3,2},{4,5},{5,4},{6,7},{7,6},{8,9},{9,8},{10,11... | collective-permute-start | bytes 4718600 | tf_op jit(solution)/shard_map/ppermute | solution.py:145
  162.6 1.6 copy-start
  168.8 8.2 %copy-start.3 = (bf16[8,128,256]{2,1,0:T(8,128)(2,1)S(1)}, bf16[8,128,256]{2,1,0:T(8,128)(2,1)}, u32[]{:S(2)}) copy-start(bf16[8,128,256]{2,1,0:T(8,128)(2,1)} %all_gather.16) | copy-start | bytes 1572868
  168.9 26.8 %copy-start.10 = (f32[9]{0:T(128)S(1)}, f32[9]{0:T(128)}, u32[]{:S(2)}) copy-start(f32[9]{0:T(128)} %dwa.1) | copy-start | bytes 112
  168.9 7.4 %collective-permute-start.11 = (bf16[64,256]{1,0:T(8,128)(2,1)S(1)}, bf16[64,256]{1,0:T(8,128)(2,1)S(1)}, u32[]{:S(2)}, u32[]{:S(2)}) collective-permute-start(bf16[64,256]{1,0:T(8,128)(2,1)S(1)} %shard_map.86), channel_id=1, source_target_pairs={{0,16},{16,32},{32,48},{48,64},{64,80},{80,96},{96,112},{112,128},... | collective-permute-start | bytes 98312 | tf_op jit(solution)/shard_map/ppermute | solution.py:124
  177.0 12.1 %collective-permute-start.13 = (bf16[8,128,256]{2,1,0:T(8,128)(2,1)S(1)}, bf16[8,128,256]{2,1,0:T(8,128)(2,1)S(1)}, u32[]{:S(2)}, u32[]{:S(2)}) collective-permute-start(bf16[8,128,256]{2,1,0:T(8,128)(2,1)S(1)} %copy-done.3), channel_id=1, source_target_pairs={{0,16},{16,32},{32,48},{48,0},{1,17},{17,33},{33,49},{49,1},{2,18}... | collective-permute-start | bytes 1572872 | tf_op jit(solution)/shard_map/ppermute | solution.py:250
  180.0 11.6 %collective-permute-start.12 = (bf16[8,128,256]{2,1,0:T(8,128)(2,1)S(1)}, bf16[8,128,256]{2,1,0:T(8,128)(2,1)S(1)}, u32[]{:S(2)}, u32[]{:S(2)}) collective-permute-start(bf16[8,128,256]{2,1,0:T(8,128)(2,1)S(1)} %copy-done.3), channel_id=1, source_target_pairs={{0,48},{16,0},{32,16},{48,32},{1,49},{17,1},{33,17},{49,33},{2,50}... | collective-permute-start | bytes 1572872 | tf_op jit(solution)/shard_map/ppermute | solution.py:251
  189.1 9.1 %collective-permute-start.14 = (bf16[4,128,256]{2,1,0:T(8,128)(2,1)S(1)}, bf16[4,128,256]{2,1,0:T(8,128)(2,1)S(1)}, u32[]{:S(2)}, u32[]{:S(2)}) collective-permute-start(bf16[4,128,256]{2,1,0:T(8,128)(2,1)S(1)} %slice.35), channel_id=1, source_target_pairs={{0,16},{16,32},{32,48},{48,0},{1,17},{17,33},{33,49},{49,1},{2,18}... | collective-permute-start | bytes 786440 | tf_op jit(solution)/shard_map/ppermute | solution.py:252
  191.6 7.5 %collective-permute-start.15 = (bf16[4,128,256]{2,1,0:T(8,128)(2,1)S(1)}, bf16[4,128,256]{2,1,0:T(8,128)(2,1)S(1)}, u32[]{:S(2)}, u32[]{:S(2)}) collective-permute-start(bf16[4,128,256]{2,1,0:T(8,128)(2,1)S(1)} %slice.36), channel_id=1, source_target_pairs={{0,48},{16,0},{32,16},{48,32},{1,49},{17,1},{33,17},{49,33},{2,50}... | collective-permute-start | bytes 786440 | tf_op jit(solution)/shard_map/ppermute | solution.py:253
Sparse Core Ops, SparseCore 0:
  77.7 84.9 all-gather.4
  177.1 45.9 all-gather.6

commit v3 on v2

--- a/solution.py
+++ b/solution.py
@@ -128,6 +128,114 @@
     return [(i, (i + step) % count) for i in range(count)]
 
 
+STEPS = 4
+BAND = 128
+
+
+def project_kernel(x, blocks, weights, out, total):
+    step = pl.program_id(0)
+    across, _, depth, _ = weights.shape
+    pieces = blocks.shape[2] // depth
+
+    @pl.when(step == 0)
+    def _():
+        total[...] = jnp.zeros(total.shape, jnp.float32)
+
+    for row in range(0, total.shape[0], BAND):
+        rows = slice(row, row + BAND)
+        value = total[rows, :]
+        for g in range(blocks.shape[0]):
+            for piece in range(pieces):
+                column = g * pieces + piece
+                at = lax.rem(column % across + across - x[0], across)
+                value += jnp.dot(
+                    blocks[g, rows, piece * depth : (piece + 1) * depth],
+                    weights[at, column // across],
+                    preferred_element_type=jnp.float32,
+                )
+        total[rows, :] = value
+
+    @pl.when(step == pl.num_programs(0) - 1)
+    def _():
+        out[...] = total[...].astype(out.dtype)
+
+
+def project(x, blocks, weights):
+    groups, rows, depth = blocks.shape
+    across, along, cut, width = weights.shape
+    return pl.pallas_call(
+        project_kernel,
+        grid=(STEPS,),
+        out_shape=jax.ShapeDtypeStruct((rows, width), jnp.bfloat16),
+        in_specs=[
+            pl.BlockSpec(memory_space=pltpu.SMEM),
+            pl.BlockSpec((groups // STEPS, rows, depth), lambda i: (i, 0, 0)),
+            pl.BlockSpec((across, along // STEPS, cut, width), lambda i: (0, i, 0, 0)),
+        ],
+        out_specs=pl.BlockSpec((rows, width), lambda i: (0, 0)),
+        scratch_shapes=[pltpu.VMEM((rows, width), jnp.float32)],
+        name="project",
+    )(x, blocks, weights)
+
+
+def finish_kernel(y, dwa, first, second, weights, stream, past, block_out, dense_out, total):
+    step = pl.program_id(0)
+    width = weights.shape[3]
+
+    @pl.when(step == 0)
+    def _():
+        total[...] = jnp.zeros(total.shape, jnp.float32)
+
+    for row in range(0, total.shape[0], BAND):
+        rows = slice(row, row + BAND)
+        value = total[rows, :]
+        for which, blocks in enumerate((first, second)):
+            groups, _, depth = blocks.shape
+            matching = weights[which].reshape(groups, depth, width)
+            for g in range(groups):
+                part = jnp.dot(blocks[g, rows, :], matching[g], preferred_element_type=jnp.float32)
+                value += part.astype(jnp.bfloat16).astype(jnp.float32)
+        total[rows, :] = value
+
+    @pl.when(step == pl.num_programs(0) - 1)
+    def _():
+        block = stream[...].astype(jnp.float32) + total[...]
+        block_out[...] = block.astype(block_out.dtype)
+        dense_out[...] = (dwa[dwa.shape[0] - 1] * block + past[...]).astype(dense_out.dtype)
+
+
+def finish(y, dwa, blocks, weights, stream, past):
+    groups, rows, depth = blocks.shape
+    along, across, cut, width = weights.shape
+    steps = along // 2
+    here = groups // along
+
+    def at(which):
+        return lambda i, y: (lax.rem(y[0] + 2 * i + which + along - along // 2, along), 0, 0)
+
+    whole = pl.BlockSpec((rows, width), lambda i, y: (0, 0))
+    shape = jax.ShapeDtypeStruct(stream.shape, jnp.bfloat16)
+    return pl.pallas_call(
+        finish_kernel,
+        out_shape=(shape, shape),
+        grid_spec=pltpu.PrefetchScalarGridSpec(
+            num_scalar_prefetch=1,
+            grid=(steps,),
+            in_specs=[
+                pl.BlockSpec(memory_space=pltpu.SMEM),
+                pl.BlockSpec((here, rows, depth), at(0)),
+                pl.BlockSpec((here, rows, depth), at(1)),
+                pl.BlockSpec((2, across, cut, width), lambda i, y: (i, 0, 0, 0)),
+                whole,
+                whole,
+            ],
+            out_specs=(whole, whole),
+            scratch_shapes=[pltpu.VMEM(stream.shape, jnp.float32)],
+        ),
+        name="finish",
+    )(y, dwa, blocks, blocks, weights, stream, past)
+
+
 def around(block, axis):
     count = lax.axis_size(axis)
     parts = {0: block}
@@ -139,90 +247,6 @@
             left = lax.ppermute(left, axis, ring(count, -1))
             parts[step] = left
     return jnp.stack([parts[i] for i in sorted(parts)])
-
-
-def partner(block):
-    return lax.ppermute(block, "core", [(0, 1), (1, 0)])
-
-
-def project_kernel(place, mine, other, weights, out):
-    steps, _, depth = mine.shape
-    z, core = place[0], place[1]
-
-    def body(i, total):
-        at = lax.rem(z + i + steps - steps // 2, steps) * 2
-        w_mine = weights[pl.ds((at + core) * 2, 2)].reshape(depth, -1)
-        w_other = weights[pl.ds((at + 1 - core) * 2, 2)].reshape(depth, -1)
-        total += jnp.dot(mine[i], w_mine, preferred_element_type=jnp.float32)
-        total += jnp.dot(other[i], w_other, preferred_element_type=jnp.float32)
-        return total
-
-    total = lax.fori_loop(0, steps, body, jnp.zeros(out.shape, jnp.float32))
-    out[...] = total.astype(out.dtype)
-
-
-def project(place, mine, other, weights):
-    rows, width = mine.shape[1], weights.shape[2]
-    return pl.pallas_call(
-        project_kernel,
-        out_shape=jax.ShapeDtypeStruct((rows, width), jnp.bfloat16),
-        in_specs=[pl.BlockSpec(memory_space=pltpu.SMEM)] + [vmem_space()] * 3,
-        out_specs=vmem_space(),
-        compiler_params=ROOM,
-        name="project",
-    )(place, mine, other, weights)
-
-
-def finish_kernel(x, dwa, attended, weights, stream, past, block_out, dense_out, total):
-    step = pl.program_id(0)
-    across, _, depth, _ = weights.shape
-
-    @pl.when(step == 0)
-    def _():
-        total[...] = jnp.zeros(total.shape, jnp.float32)
-
-    pieces = attended.shape[2] // depth
-    for g in range(attended.shape[0]):
-        part = jnp.zeros(total.shape, jnp.float32)
-        for piece in range(pieces):
-            at = lax.rem(g * pieces + piece + across - x[0], across)
-            part += jnp.dot(
-                attended[g, :, piece * depth : (piece + 1) * depth],
-                weights[at, 0],
-                preferred_element_type=jnp.float32,
-            )
-        total[...] += part.astype(jnp.bfloat16).astype(jnp.float32)
-
-    @pl.when(step == pl.num_programs(0) - 1)
-    def _():
-        block = stream[...].astype(jnp.float32) + total[...]
-        block_out[...] = block.astype(block_out.dtype)
-        dense_out[...] = (dwa[dwa.shape[0] - 1] * block + past[...]).astype(dense_out.dtype)
-
-
-def finish(x, dwa, attended, weights, stream, past):
-    groups, rows, depth = attended.shape
-    across, along, cut, width = weights.shape
-    here = groups // along
-    scalars = pl.BlockSpec(memory_space=pltpu.SMEM)
-    whole = pl.BlockSpec(stream.shape, lambda i: (0, 0))
-    shape = jax.ShapeDtypeStruct(stream.shape, jnp.bfloat16)
-    return pl.pallas_call(
-        finish_kernel,
-        grid=(along,),
-        out_shape=(shape, shape),
-        in_specs=[
-            scalars,
-            scalars,
-            pl.BlockSpec((here, rows, depth), lambda i: (i, 0, 0)),
-            pl.BlockSpec((across, 1, cut, width), lambda i: (0, i, 0, 0)),
-            whole,
-            whole,
-        ],
-        out_specs=(whole, whole),
-        scratch_shapes=[pltpu.VMEM(stream.shape, jnp.float32)],
-        name="finish",
-    )(x, dwa, attended, weights, stream, past)
 
 
 def columns_here(w_out):
@@ -255,33 +279,34 @@
 
 
 def on_device(stream, history, dwa_weights, w_query, w_out, encoded_kv, neighbour_ids):
-    tok_rows, _ = stream.shape
+    tok_rows = stream.shape[0]
     local_heads = w_query.shape[1] // HDIM
     ctx_count = lax.axis_size(CTX)
     db_count = lax.axis_size(DB)
     slots = neighbour_ids.shape[0] // ctx_count
     slab_rows = 2 * encoded_kv.shape[2]
-    place = jnp.stack([lax.axis_index("z"), lax.axis_index("core")]).astype(jnp.int32)
     x = lax.axis_index("x").astype(jnp.int32).reshape(1)
-
-    w_in = lax.all_gather(w_query, CTX, axis=0)
+    y = lax.axis_index("y").astype(jnp.int32).reshape(1)
+
+    after = shifted(stream[:SPAN], -1)
+    own_spans = jnp.concatenate([stream[LEAD:], after[:LEAD]], 0)
     by_head = split_heads(encoded_kv, local_heads)
     store = lax.all_to_all(
         by_head.reshape(db_count, -1, HDIM), DB, split_axis=0, concat_axis=0, tiled=True
     )
-    after = shifted(stream[:SPAN], -1)
-    own_spans = jnp.concatenate([stream[LEAD:], after[:LEAD]], 0)
     turned = columns_here(w_out)
-    turned = lax.all_gather(turned, "y", axis=0)
-
+    w_in = lax.all_gather(w_query, "y", axis=0)
+    w_in = along_x(w_in)
+    own_spans, store, turned = lax.optimization_barrier((own_spans, store, turned))
+    features = lax.all_gather(own_spans, DB, axis=0)
     picked = pick(neighbour_ids, store.reshape(-1, local_heads * slab_rows, HDIM))
-    own_spans, turned, picked = lax.optimization_barrier((own_spans, turned, picked))
     arrived = lax.all_to_all(
         picked.reshape(ctx_count, -1, HDIM), CTX, split_axis=0, concat_axis=0, tiled=True
     ).reshape(ctx_count, slots, local_heads, slab_rows, HDIM)
-    mine = around(own_spans, "z")
+    w_in, turned = lax.optimization_barrier((w_in, turned))
+    turned = lax.all_gather(turned, "x", axis=0)
     past = jnp.sum(history.astype(jnp.float32) * dwa_weights[:-1, None, None], axis=0)
-    queries = project(place, mine, partner(mine), w_in)
+    queries = project(x, features, w_in)
     spans = tok_rows // SPAN
     last = attend(queries, arrived, spans - 1, 1)
     before = shifted(last, 1)
@@ -289,8 +314,8 @@
     attended = jnp.concatenate([before[1:], rest, last[:1]], 0)
     attended, turned = lax.optimization_barrier((attended, turned))
     everyone = lax.all_gather(attended, DB, axis=0)
-    columns = along_x(turned)
-    return finish(x, dwa_weights, everyone, columns, stream, past)
+    columns = around(turned, "y")
+    return finish(y, dwa_weights, everyone, columns, stream, past)
 
 
 def solution(mesh):

time: 238 us -> 247 us (1.038)
  the two profiles are of different devices: /device:TPU:1 before, /device:TPU:24 now
where the time goes in v3:
time: 247 us; the launch traced here: 246 us
  starting transfers between devices  77.2 us (31%)
  blocking collectives  70.1 us (28%)
  waiting for transfers between devices  55 us (22%)
  Pallas kernels  20.9 us (8%)
  between operations  14.5 us (6%)
  other arithmetic  4.22 us (2%)
  local copies, waits for them, and re-layouts  3.93 us (2%)
    all_gather x1, blocking collectives, on_device(): w_in = lax.all_gather(w_query, 'y', axis=0)  57.9 us
    all_to_all x1, waiting for transfers between devices, on_device(): lax.all_to_all(by_head.reshape(db_count, -1, HDIM), DB, split_axis=0, con...  20.8 us
    ppermute x4, waiting for transfers between devices, around(): right = lax.ppermute(right, axis, ring(count, 1))  15.1 us
    all_to_all x1, starting transfers between devices, on_device(): lax.all_to_all(picked.reshape(ctx_count, -1, HDIM), CTX, split_axis=0, co...  14.2 us
    all_gather x1, blocking collectives, on_device(): turned = lax.all_gather(turned, 'x', axis=0)  12.3 us
    ppermute x2, starting transfers between devices, columns_here(): pieces.append(lax.ppermute(send, CTX + DB, route))  11.3 us
    all_to_all x1, starting transfers between devices, on_device(): lax.all_to_all(by_head.reshape(db_count, -1, HDIM), DB, split_axis=0, con...  10.6 us
    ppermute x3, starting transfers between devices, around(): left = lax.ppermute(left, axis, ring(count, -1))  10.2 us
  transfers between devices with their start and end apart: 19, of which 11 were waited for; matrix products, arithmetic and copies ran while one was open for 2% of the time, Pallas kernels for 5%

profile of v3, /device:TPU:24, one launch (start us, length us, event | category | flops | bytes accessed | tf_op | source)
XLA Modules:
  0.0 245.8 jit_solution(4078550842463382070)
XLA Ops:
  7.2 0.0 copy-start.1
  7.2 1.4 copy-done.1
  8.6 3.2 %split_heads.1 = bf16[16,24,2,4,2,128]{5,4,3,2,1,0:T(2,128)(2,1)} custom-call(bf16[1,24,4,2,4096]{4,3,2,1,0:T(2,128)(2,1)S(1)} %copy-done.1), custom_call_target="tpu_custom_call" | custom-call | tf_op jit(solution)/shard_map/split_heads/pallas_call | solution.py:45
  11.7 0.0 copy-start.7
  11.8 0.0 copy-start.5
  11.8 0.0 copy-start.2
  11.8 10.6 %all-to-all-start = ((bf16[16,384,128]{2,1,0:T(8,128)(2,1)}), bf16[16,384,128]{2,1,0:T(8,128)(2,1)S(1)}, u32[]{:S(2)}, u32[]{:S(2)}) async-start(bf16[16,384,128]{2,1,0:T(8,128)(2,1)} %bitcast.2), calls=%async_computation | async-start | bytes 3145728 | tf_op jit(solution)/shard_map/all_to_all | solution.py:294
  22.3 0.0 all-gather.7.cloned.1.call-start
  22.4 0.0 copy-done.7
  22.5 5.3 %collective-permute-start.1 = (bf16[128,128]{1,0:T(8,128)(2,1)S(1)}, bf16[128,128]{1,0:T(8,128)(2,1)S(1)}, u32[]{:S(2)}, u32[]{:S(2)}) collective-permute-start(bf16[128,128]{1,0:T(8,128)(2,1)S(1)} %get-tuple-element.16), channel_id=1, source_target_pairs={{0,0},{1,32},{2,64},{3,96},{4,128},{5,160},{6,192},{7,224},{8,256}... | collective-permute-start | bytes 98312 | tf_op jit(solution)/shard_map/ppermute | solution.py:265
  27.8 6.0 %collective-permute-start.2 = (bf16[128,128]{1,0:T(8,128)(2,1)S(1)}, bf16[128,128]{1,0:T(8,128)(2,1)S(1)}, u32[]{:S(2)}, u32[]{:S(2)}) collective-permute-start(bf16[128,128]{1,0:T(8,128)(2,1)S(1)} %get-tuple-element.17), channel_id=1, source_target_pairs={{0,16},{1,48},{2,80},{3,112},{4,144},{5,176},{6,208},{7,240},{8,27... | collective-permute-start | bytes 98312 | tf_op jit(solution)/shard_map/ppermute | solution.py:265
  33.7 0.0 copy-done.5
  33.8 3.9 %collective-permute-start = (bf16[64,256]{1,0:T(8,128)(2,1)S(1)}, bf16[64,256]{1,0:T(8,128)(2,1)S(1)}, u32[]{:S(2)}, u32[]{:S(2)}) collective-permute-start(bf16[64,256]{1,0:T(8,128)(2,1)S(1)} %slice.25), channel_id=1, source_target_pairs={{16,0},{32,16},{48,32},{64,48},{80,64},{96,80},{112,96},{128,112},... | collective-permute-start | bytes 98312 | tf_op jit(solution)/shard_map/ppermute | solution.py:124
  37.8 0.0 collective-permute-done.1
  37.8 2.7 %collective-permute-done.2 = bf16[128,128]{1,0:T(8,128)(2,1)S(1)} collective-permute-done((bf16[128,128]{1,0:T(8,128)(2,1)S(1)}, bf16[128,128]{1,0:T(8,128)(2,1)S(1)}, u32[]{:S(2)}, u32[]{:S(2)}) %collective-permute-start.2) | collective-permute-done | bytes 32800 | tf_op jit(solution)/shard_map/ppermute | solution.py:265
  40.5 0.0 collective-permute-done
  40.5 0.7 pad_maximum_fusion.1
  41.2 20.8 %all-to-all-done = bf16[16,384,128]{2,1,0:T(8,128)(2,1)S(1)} async-done(((bf16[16,384,128]{2,1,0:T(8,128)(2,1)}), bf16[16,384,128]{2,1,0:T(8,128)(2,1)S(1)}, u32[]{:S(2)}, u32[]{:S(2)}) %all-to-all-start) | async-done | bytes 1572896 | tf_op jit(solution)/shard_map/all_to_all | solution.py:294
  62.0 0.0 all-gather.7.cloned.1.call-update
  62.0 0.0 copy-done.2
  62.0 2.4 pick.1
  64.4 14.2 %all-to-all-start.1 = ((bf16[32,192,128]{2,1,0:T(8,128)(2,1)}), bf16[32,192,128]{2,1,0:T(8,128)(2,1)S(1)}, u32[]{:S(2)}, u32[]{:S(2)}) async-start(bf16[32,192,128]{2,1,0:T(8,128)(2,1)} %bitcast.10), calls=%async_computation.1 | async-start | bytes 3145728 | tf_op jit(solution)/shard_map/all_to_all | solution.py:303
  78.6 0.0 all-gather.9.cloned.1.call-start
  78.6 0.0 copy-done.6
  78.6 57.9 %all-gather.1 = bf16[1024,256]{1,0:T(8,128)(2,1)S(1)} all-gather(bf16[128,256]{1,0:T(8,128)(2,1)S(1)} %copy-done.6), channel_id=3, replica_groups=mesh['y'=8,'x'=4,'z'=8,'core'=2] {'y'}, dimensions={0}, use_global_device_ids=true | all-gather | bytes 589824 | tf_op jit(solution)/shard_map/all_gather | solution.py:298
  136.5 3.5 %collective-permute-start.4 = (bf16[8,128,256]{2,1,0:T(8,128)(2,1)S(1)}, bf16[8,128,256]{2,1,0:T(8,128)(2,1)S(1)}, u32[]{:S(2)}, u32[]{:S(2)}) collective-permute-start(bf16[8,128,256]{2,1,0:T(8,128)(2,1)S(1)} %bitcast.39), channel_id=1, source_target_pairs={{0,16},{16,32},{32,48},{48,0},{1,17},{17,33},{33,49},{49,1},{2,18}... | collective-permute-start | bytes 1572872 | tf_op jit(solution)/shard_map/ppermute | solution.py:274
  140.0 3.6 %collective-permute-start.3 = (bf16[8,128,256]{2,1,0:T(8,128)(2,1)S(1)}, bf16[8,128,256]{2,1,0:T(8,128)(2,1)S(1)}, u32[]{:S(2)}, u32[]{:S(2)}) collective-permute-start(bf16[8,128,256]{2,1,0:T(8,128)(2,1)S(1)} %bitcast.40), channel_id=1, source_target_pairs={{0,48},{16,0},{32,16},{48,32},{1,49},{17,1},{33,17},{49,33},{2,50}... | collective-permute-start | bytes 1572872 | tf_op jit(solution)/shard_map/ppermute | solution.py:275
  143.6 6.0 %collective-permute-done.4 = bf16[8,128,256]{2,1,0:T(8,128)(2,1)S(1)} collective-permute-done((bf16[8,128,256]{2,1,0:T(8,128)(2,1)S(1)}, bf16[8,128,256]{2,1,0:T(8,128)(2,1)S(1)}, u32[]{:S(2)}, u32[]{:S(2)}) %collective-permute-start.4) | collective-permute-done | bytes 524320 | tf_op jit(solution)/shard_map/ppermute | solution.py:274
  149.6 3.6 %collective-permute-start.5 = (bf16[4,128,256]{2,1,0:T(8,128)(2,1)S(1)}, bf16[4,128,256]{2,1,0:T(8,128)(2,1)S(1)}, u32[]{:S(2)}, u32[]{:S(2)}) collective-permute-start(bf16[4,128,256]{2,1,0:T(8,128)(2,1)S(1)} %slice.33), channel_id=1, source_target_pairs={{0,16},{16,32},{32,48},{48,0},{1,17},{17,33},{33,49},{49,1},{2,18}... | collective-permute-start | bytes 786440 | tf_op jit(solution)/shard_map/ppermute | solution.py:276
  153.2 0.2 collective-permute-done.3
  153.4 3.5 %collective-permute-start.6 = (bf16[4,128,256]{2,1,0:T(8,128)(2,1)S(1)}, bf16[4,128,256]{2,1,0:T(8,128)(2,1)S(1)}, u32[]{:S(2)}, u32[]{:S(2)}) collective-permute-start(bf16[4,128,256]{2,1,0:T(8,128)(2,1)S(1)} %slice.34), channel_id=1, source_target_pairs={{0,48},{16,0},{32,16},{48,32},{1,49},{17,1},{33,17},{49,33},{2,50}... | collective-permute-start | bytes 786440 | tf_op jit(solution)/shard_map/ppermute | solution.py:277
  156.9 2.2 collective-permute-done.5
  159.1 2.6 %collective-permute-done.6 = bf16[4,128,256]{2,1,0:T(8,128)(2,1)S(1)} collective-permute-done((bf16[4,128,256]{2,1,0:T(8,128)(2,1)S(1)}, bf16[4,128,256]{2,1,0:T(8,128)(2,1)S(1)}, u32[]{:S(2)}, u32[]{:S(2)}) %collective-permute-start.6) | collective-permute-done | bytes 262176 | tf_op jit(solution)/shard_map/ppermute | solution.py:277
  161.8 1.6 pad_maximum_fusion.weights
  163.4 5.1 %project.1.q_ref = bf16[384,256]{1,0:T(8,128)(2,1)} custom-call(s32[1]{0:T(128)} %bitcast.1.x, bf16[16,384,256]{2,1,0:T(8,128)(2,1)} %bitcast.38, bf16[4,8,128,256]{3,2,1,0:T(8,128)(2,1)} %pad_maximum_fusion.weights), custom_call_target="tpu_custom_call" | custom-call | tf_op jit(solution)/shard_map/project/pallas_call | solution.py:166
  168.5 0.0 all-to-all-done.1
  168.5 0.9 copy-done
  169.4 1.0 shard_map.86
  170.4 3.7 %collective-permute-start.7 = (bf16[64,256]{1,0:T(8,128)(2,1)S(1)}, bf16[64,256]{1,0:T(8,128)(2,1)S(1)}, u32[]{:S(2)}, u32[]{:S(2)}) collective-permute-start(bf16[64,256]{1,0:T(8,128)(2,1)S(1)} %shard_map.86), channel_id=1, source_target_pairs={{0,16},{16,32},{32,48},{48,64},{64,80},{80,96},{96,112},{112,128},... | collective-permute-start | bytes 98312 | tf_op jit(solution)/shard_map/ppermute | solution.py:124
  174.1 12.3 %all-gather.2 = bf16[512,256]{1,0:T(8,128)(2,1)S(1)} all-gather(bf16[128,256]{1,0:T(8,128)(2,1)S(1)} %maximum_select_fusion), channel_id=4, replica_groups=mesh['y'=8,'x'=4,'z'=8,'core'=2] {'x'}, dimensions={0}, use_global_device_ids=true | all-gather | bytes 327680 | tf_op jit(solution)/shard_map/all_gather | solution.py:307
  186.3 4.2 %shard_map.87 = bf16[320,256]{1,0:T(8,128)(2,1)S(1)} custom-call(bf16[384,256]{1,0:T(8,128)(2,1)S(1)} %copy-done, bf16[32,12,2,8,128]{4,3,2,1,0:T(8,128)(2,1)S(1)} %bitcast.34), custom_call_target="tpu_custom_call" | custom-call | tf_op jit(solution)/shard_map/pallas_call | solution.py:112
  190.6 0.0 collective-permute-done.7
  190.6 0.7 pad_maximum_fusion.2
  191.3 0.0 all-gather.9.cloned.1.call-update
  191.3 1.9 collective-permute-start.8
  193.3 7.2 %collective-permute-done.8 = bf16[4,128,256]{2,1,0:T(8,128)(2,1)S(1)} collective-permute-done((bf16[4,128,256]{2,1,0:T(8,128)(2,1)S(1)}, bf16[4,128,256]{2,1,0:T(8,128)(2,1)S(1)}, u32[]{:S(2)}, u32[]{:S(2)}) %collective-permute-start.8) | collective-permute-done | bytes 262176 | tf_op jit(solution)/shard_map/ppermute | solution.py:244
  200.5 2.3 collective-permute-start.9
  202.8 3.6 %collective-permute-start.12 = (bf16[4,128,256]{2,1,0:T(8,128)(2,1)S(1)}, bf16[4,128,256]{2,1,0:T(8,128)(2,1)S(1)}, u32[]{:S(2)}, u32[]{:S(2)}) collective-permute-start(bf16[4,128,256]{2,1,0:T(8,128)(2,1)S(1)} %bitcast.45), channel_id=1, source_target_pairs={{0,448},{64,0},{128,64},{192,128},{256,192},{320,256},{384,320},{4... | collective-permute-start | bytes 786440 | tf_op jit(solution)/shard_map/ppermute | solution.py:247
  206.3 4.3 %collective-permute-done.9 = bf16[4,128,256]{2,1,0:T(8,128)(2,1)S(1)} collective-permute-done((bf16[4,128,256]{2,1,0:T(8,128)(2,1)S(1)}, bf16[4,128,256]{2,1,0:T(8,128)(2,1)S(1)}, u32[]{:S(2)}, u32[]{:S(2)}) %collective-permute-start.9) | collective-permute-done | bytes 262176 | tf_op jit(solution)/shard_map/ppermute | solution.py:244
  210.6 1.9 collective-permute-start.10
  212.5 0.0 collective-permute-done.12
  212.5 3.9 %collective-permute-start.13 = (bf16[4,128,256]{2,1,0:T(8,128)(2,1)S(1)}, bf16[4,128,256]{2,1,0:T(8,128)(2,1)S(1)}, u32[]{:S(2)}, u32[]{:S(2)}) collective-permute-start(bf16[4,128,256]{2,1,0:T(8,128)(2,1)S(1)} %collective-permute-done.12), channel_id=1, source_target_pairs={{0,448},{64,0},{128,64},{192,128},{256,192},{320,256},{384,320},{4... | collective-permute-start | bytes 786440 | tf_op jit(solution)/shard_map/ppermute | solution.py:247
  216.5 2.4 collective-permute-done.10
  218.9 3.1 %collective-permute-start.11 = (bf16[4,128,256]{2,1,0:T(8,128)(2,1)S(1)}, bf16[4,128,256]{2,1,0:T(8,128)(2,1)S(1)}, u32[]{:S(2)}, u32[]{:S(2)}) collective-permute-start(bf16[4,128,256]{2,1,0:T(8,128)(2,1)S(1)} %collective-permute-done.10), channel_id=1, source_target_pairs={{0,64},{64,128},{128,192},{192,256},{256,320},{320,384},{384,448},... | collective-permute-start | bytes 786440 | tf_op jit(solution)/shard_map/ppermute | solution.py:244
  222.0 0.0 copy-done.4
  222.0 0.0 copy-done.8
  222.0 1.1 multiply_reduce_fusion.past
  223.1 0.0 collective-permute-done.13
  223.1 2.7 %collective-permute-start.14 = (bf16[4,128,256]{2,1,0:T(8,128)(2,1)S(1)}, bf16[4,128,256]{2,1,0:T(8,128)(2,1)S(1)}, u32[]{:S(2)}, u32[]{:S(2)}) collective-permute-start(bf16[4,128,256]{2,1,0:T(8,128)(2,1)S(1)} %collective-permute-done.13), channel_id=1, source_target_pairs={{0,448},{64,0},{128,64},{192,128},{256,192},{320,256},{384,320},{4... | collective-permute-start | bytes 786440 | tf_op jit(solution)/shard_map/ppermute | solution.py:247
  225.8 1.3 collective-permute-done.11
  227.3 5.3 %collective-permute-done.14 = bf16[4,128,256]{2,1,0:T(8,128)(2,1)S(1)} collective-permute-done((bf16[4,128,256]{2,1,0:T(8,128)(2,1)S(1)}, bf16[4,128,256]{2,1,0:T(8,128)(2,1)S(1)}, u32[]{:S(2)}, u32[]{:S(2)}) %collective-permute-start.14) | collective-permute-done | bytes 262176 | tf_op jit(solution)/shard_map/ppermute | solution.py:247
  232.6 0.0 all-gather.9.cloned.1.call-done
  232.7 1.3 copy-done.3
  234.0 5.0 %finish.1 = (bf16[384,256]{1,0:T(8,128)(2,1)}, bf16[384,256]{1,0:T(8,128)(2,1)}) custom-call(s32[1]{0:T(128)} %bitcast.y, f32[9]{0:T(128)} %dwa.1, bf16[16,384,256]{2,1,0:T(8,128)(2,1)} %bitcast.36, bf16[16,384,256]{2,1,0:T(8,128)(2,1)} %bitcast.37, bf16[8,4,128,256]{3,2,1,0:T(8,128)(2,1)} %copy-done.3, bf16[384,256]{1,0:T(8,128)(2,1)} %stream.1, ...), custom_call_target="tpu_custom_call" | custom-call | tf_op jit(solution)/shard_map/finish/pallas_call | solution.py:218
  (23 shorter events, 0.3 us)
Async XLA Ops:
  7.2 1.4 copy-start.1
  11.7 10.7 %copy-start.7 = (bf16[256,128]{1,0:T(8,128)(2,1)S(1)}, bf16[256,128]{1,0:T(8,128)(2,1)}, u32[]{:S(2)}) copy-start(bf16[256,128]{1,0:T(8,128)(2,1)} %param.11) | copy-start | bytes 196612
  11.8 22.0 %copy-start.5 = (bf16[384,256]{1,0:T(8,128)(2,1)S(1)}, bf16[384,256]{1,0:T(8,128)(2,1)}, u32[]{:S(2)}) copy-start(bf16[384,256]{1,0:T(8,128)(2,1)} %stream.1) | copy-start | bytes 589828
  11.8 50.2 %copy-start.2 = (s32[384]{0:T(512)S(1)}, s32[384]{0:T(512)}, u32[]{:S(2)}) copy-start(s32[384]{0:T(512)} %ids.1) | copy-start | bytes 4612
  11.8 50.2 %all-to-all-start = ((bf16[16,384,128]{2,1,0:T(8,128)(2,1)}), bf16[16,384,128]{2,1,0:T(8,128)(2,1)S(1)}, u32[]{:S(2)}, u32[]{:S(2)}) async-start(bf16[16,384,128]{2,1,0:T(8,128)(2,1)} %bitcast.2), calls=%async_computation | async-start | bytes 3145728 | tf_op jit(solution)/shard_map/all_to_all | solution.py:294
  22.3 141.0 %all-gather.7.cloned.1.call-start = ((), (), s32[]{:S(2)}) async-start(), calls=%async_computation.2 | async-start | bytes 3342336 | tf_op jit(solution)/shard_map/all_gather | solution.py:301
  22.5 15.3 %collective-permute-start.1 = (bf16[128,128]{1,0:T(8,128)(2,1)S(1)}, bf16[128,128]{1,0:T(8,128)(2,1)S(1)}, u32[]{:S(2)}, u32[]{:S(2)}) collective-permute-start(bf16[128,128]{1,0:T(8,128)(2,1)S(1)} %get-tuple-element.16), channel_id=1, source_target_pairs={{0,0},{1,32},{2,64},{3,96},{4,128},{5,160},{6,192},{7,224},{8,256}... | collective-permute-start | bytes 98312 | tf_op jit(solution)/shard_map/ppermute | solution.py:265
  27.8 12.7 %collective-permute-start.2 = (bf16[128,128]{1,0:T(8,128)(2,1)S(1)}, bf16[128,128]{1,0:T(8,128)(2,1)S(1)}, u32[]{:S(2)}, u32[]{:S(2)}) collective-permute-start(bf16[128,128]{1,0:T(8,128)(2,1)S(1)} %get-tuple-element.17), channel_id=1, source_target_pairs={{0,16},{1,48},{2,80},{3,112},{4,144},{5,176},{6,208},{7,240},{8,27... | collective-permute-start | bytes 98312 | tf_op jit(solution)/shard_map/ppermute | solution.py:265
  33.8 6.7 %collective-permute-start = (bf16[64,256]{1,0:T(8,128)(2,1)S(1)}, bf16[64,256]{1,0:T(8,128)(2,1)S(1)}, u32[]{:S(2)}, u32[]{:S(2)}) collective-permute-start(bf16[64,256]{1,0:T(8,128)(2,1)S(1)} %slice.25), channel_id=1, source_target_pairs={{16,0},{32,16},{48,32},{64,48},{80,64},{96,80},{112,96},{128,112},... | collective-permute-start | bytes 98312 | tf_op jit(solution)/shard_map/ppermute | solution.py:124
  64.4 14.2 %copy-start.6 = (bf16[128,256]{1,0:T(8,128)(2,1)S(1)}, bf16[128,256]{1,0:T(8,128)(2,1)}, u32[]{:S(2)}) copy-start(bf16[128,256]{1,0:T(8,128)(2,1)} %param.10) | copy-start | bytes 196612
  64.4 104.1 %all-to-all-start.1 = ((bf16[32,192,128]{2,1,0:T(8,128)(2,1)}), bf16[32,192,128]{2,1,0:T(8,128)(2,1)S(1)}, u32[]{:S(2)}, u32[]{:S(2)}) async-start(bf16[32,192,128]{2,1,0:T(8,128)(2,1)} %bitcast.10), calls=%async_computation.1 | async-start | bytes 3145728 | tf_op jit(solution)/shard_map/all_to_all | solution.py:303
  78.6 154.1 %all-gather.9.cloned.1.call-start = ((), (), s32[]{:S(2)}) async-start(), calls=%async_computation.3 | async-start | bytes 3342336 | tf_op jit(solution)/shard_map/all_gather | solution.py:316
  136.5 13.1 %collective-permute-start.4 = (bf16[8,128,256]{2,1,0:T(8,128)(2,1)S(1)}, bf16[8,128,256]{2,1,0:T(8,128)(2,1)S(1)}, u32[]{:S(2)}, u32[]{:S(2)}) collective-permute-start(bf16[8,128,256]{2,1,0:T(8,128)(2,1)S(1)} %bitcast.39), channel_id=1, source_target_pairs={{0,16},{16,32},{32,48},{48,0},{1,17},{17,33},{33,49},{49,1},{2,18}... | collective-permute-start | bytes 1572872 | tf_op jit(solution)/shard_map/ppermute | solution.py:274
  140.0 13.4 %collective-permute-start.3 = (bf16[8,128,256]{2,1,0:T(8,128)(2,1)S(1)}, bf16[8,128,256]{2,1,0:T(8,128)(2,1)S(1)}, u32[]{:S(2)}, u32[]{:S(2)}) collective-permute-start(bf16[8,128,256]{2,1,0:T(8,128)(2,1)S(1)} %bitcast.40), channel_id=1, source_target_pairs={{0,48},{16,0},{32,16},{48,32},{1,49},{17,1},{33,17},{49,33},{2,50}... | collective-permute-start | bytes 1572872 | tf_op jit(solution)/shard_map/ppermute | solution.py:275
  149.6 9.5 %collective-permute-start.5 = (bf16[4,128,256]{2,1,0:T(8,128)(2,1)S(1)}, bf16[4,128,256]{2,1,0:T(8,128)(2,1)S(1)}, u32[]{:S(2)}, u32[]{:S(2)}) collective-permute-start(bf16[4,128,256]{2,1,0:T(8,128)(2,1)S(1)} %slice.33), channel_id=1, source_target_pairs={{0,16},{16,32},{32,48},{48,0},{1,17},{17,33},{33,49},{49,1},{2,18}... | collective-permute-start | bytes 786440 | tf_op jit(solution)/shard_map/ppermute | solution.py:276
  153.4 8.3 %collective-permute-start.6 = (bf16[4,128,256]{2,1,0:T(8,128)(2,1)S(1)}, bf16[4,128,256]{2,1,0:T(8,128)(2,1)S(1)}, u32[]{:S(2)}, u32[]{:S(2)}) collective-permute-start(bf16[4,128,256]{2,1,0:T(8,128)(2,1)S(1)} %slice.34), channel_id=1, source_target_pairs={{0,48},{16,0},{32,16},{48,32},{1,49},{17,1},{33,17},{49,33},{2,50}... | collective-permute-start | bytes 786440 | tf_op jit(solution)/shard_map/ppermute | solution.py:277
  168.5 0.9 copy-start
  169.4 52.6 %copy-start.4 = (bf16[8,384,256]{2,1,0:T(8,128)(2,1)S(1)}, bf16[8,384,256]{2,1,0:T(8,128)(2,1)}, u32[]{:S(2)}) copy-start(bf16[8,384,256]{2,1,0:T(8,128)(2,1)} %param.8) | copy-start | bytes 4718596
  169.4 52.6 %copy-start.8 = (f32[9]{0:T(128)S(1)}, f32[9]{0:T(128)}, u32[]{:S(2)}) copy-start(f32[9]{0:T(128)} %dwa.1) | copy-start | bytes 112
  170.4 20.2 %collective-permute-start.7 = (bf16[64,256]{1,0:T(8,128)(2,1)S(1)}, bf16[64,256]{1,0:T(8,128)(2,1)S(1)}, u32[]{:S(2)}, u32[]{:S(2)}) collective-permute-start(bf16[64,256]{1,0:T(8,128)(2,1)S(1)} %shard_map.86), channel_id=1, source_target_pairs={{0,16},{16,32},{32,48},{48,64},{64,80},{80,96},{96,112},{112,128},... | collective-permute-start | bytes 98312 | tf_op jit(solution)/shard_map/ppermute | solution.py:124
  191.3 9.1 %collective-permute-start.8 = (bf16[4,128,256]{2,1,0:T(8,128)(2,1)S(1)}, bf16[4,128,256]{2,1,0:T(8,128)(2,1)S(1)}, u32[]{:S(2)}, u32[]{:S(2)}) collective-permute-start(bf16[4,128,256]{2,1,0:T(8,128)(2,1)S(1)} %bitcast.44), channel_id=1, source_target_pairs={{0,64},{64,128},{128,192},{192,256},{256,320},{320,384},{384,448},... | collective-permute-start | bytes 786440 | tf_op jit(solution)/shard_map/ppermute | solution.py:244
  200.5 10.1 %collective-permute-start.9 = (bf16[4,128,256]{2,1,0:T(8,128)(2,1)S(1)}, bf16[4,128,256]{2,1,0:T(8,128)(2,1)S(1)}, u32[]{:S(2)}, u32[]{:S(2)}) collective-permute-start(bf16[4,128,256]{2,1,0:T(8,128)(2,1)S(1)} %collective-permute-done.8), channel_id=1, source_target_pairs={{0,64},{64,128},{128,192},{192,256},{256,320},{320,384},{384,448},... | collective-permute-start | bytes 786440 | tf_op jit(solution)/shard_map/ppermute | solution.py:244
  202.8 9.8 %collective-permute-start.12 = (bf16[4,128,256]{2,1,0:T(8,128)(2,1)S(1)}, bf16[4,128,256]{2,1,0:T(8,128)(2,1)S(1)}, u32[]{:S(2)}, u32[]{:S(2)}) collective-permute-start(bf16[4,128,256]{2,1,0:T(8,128)(2,1)S(1)} %bitcast.45), channel_id=1, source_target_pairs={{0,448},{64,0},{128,64},{192,128},{256,192},{320,256},{384,320},{4... | collective-permute-start | bytes 786440 | tf_op jit(solution)/shard_map/ppermute | solution.py:247
  210.6 8.3 %collective-permute-start.10 = (bf16[4,128,256]{2,1,0:T(8,128)(2,1)S(1)}, bf16[4,128,256]{2,1,0:T(8,128)(2,1)S(1)}, u32[]{:S(2)}, u32[]{:S(2)}) collective-permute-start(bf16[4,128,256]{2,1,0:T(8,128)(2,1)S(1)} %collective-permute-done.9), channel_id=1, source_target_pairs={{0,64},{64,128},{128,192},{192,256},{256,320},{320,384},{384,448},... | collective-permute-start | bytes 786440 | tf_op jit(solution)/shard_map/ppermute | solution.py:244
  212.5 10.6 %collective-permute-start.13 = (bf16[4,128,256]{2,1,0:T(8,128)(2,1)S(1)}, bf16[4,128,256]{2,1,0:T(8,128)(2,1)S(1)}, u32[]{:S(2)}, u32[]{:S(2)}) collective-permute-start(bf16[4,128,256]{2,1,0:T(8,128)(2,1)S(1)} %collective-permute-done.12), channel_id=1, source_target_pairs={{0,448},{64,0},{128,64},{192,128},{256,192},{320,256},{384,320},{4... | collective-permute-start | bytes 786440 | tf_op jit(solution)/shard_map/ppermute | solution.py:247
  218.9 8.3 %collective-permute-start.11 = (bf16[4,128,256]{2,1,0:T(8,128)(2,1)S(1)}, bf16[4,128,256]{2,1,0:T(8,128)(2,1)S(1)}, u32[]{:S(2)}, u32[]{:S(2)}) collective-permute-start(bf16[4,128,256]{2,1,0:T(8,128)(2,1)S(1)} %collective-permute-done.10), channel_id=1, source_target_pairs={{0,64},{64,128},{128,192},{192,256},{256,320},{320,384},{384,448},... | collective-permute-start | bytes 786440 | tf_op jit(solution)/shard_map/ppermute | solution.py:244
  223.1 9.5 %collective-permute-start.14 = (bf16[4,128,256]{2,1,0:T(8,128)(2,1)S(1)}, bf16[4,128,256]{2,1,0:T(8,128)(2,1)S(1)}, u32[]{:S(2)}, u32[]{:S(2)}) collective-permute-start(bf16[4,128,256]{2,1,0:T(8,128)(2,1)S(1)} %collective-permute-done.13), channel_id=1, source_target_pairs={{0,448},{64,0},{128,64},{192,128},{256,192},{320,256},{384,320},{4... | collective-permute-start | bytes 786440 | tf_op jit(solution)/shard_map/ppermute | solution.py:247
  232.6 1.3 copy-start.3
Sparse Core Ops, SparseCore 0:
  62.1 46.5 all-gather.6
  191.5 38.8 all-gather.8

commit v4 on v3

--- a/solution.py
+++ b/solution.py
@@ -50,7 +50,6 @@
         in_specs=[any_space()],
         out_specs=vmem_space(),
         scratch_shapes=[pltpu.SemaphoreType.DMA((heads,))],
-        compiler_params=ROOM,
         name="split_heads",
     )(encoded)
 
@@ -132,10 +131,8 @@
 BAND = 128
 
 
-def project_kernel(x, blocks, weights, out, total):
+def project_kernel(blocks, weights, out, total):
     step = pl.program_id(0)
-    across, _, depth, _ = weights.shape
-    pieces = blocks.shape[2] // depth
 
     @pl.when(step == 0)
     def _():
@@ -145,14 +142,7 @@
         rows = slice(row, row + BAND)
         value = total[rows, :]
         for g in range(blocks.shape[0]):
-            for piece in range(pieces):
-                column = g * pieces + piece
-                at = lax.rem(column % across + across - x[0], across)
-                value += jnp.dot(
-                    blocks[g, rows, piece * depth : (piece + 1) * depth],
-                    weights[at, column // across],
-                    preferred_element_type=jnp.float32,
-                )
+            value += jnp.dot(blocks[g, rows, :], weights[g], preferred_element_type=jnp.float32)
         total[rows, :] = value
 
     @pl.when(step == pl.num_programs(0) - 1)
@@ -160,22 +150,21 @@
         out[...] = total[...].astype(out.dtype)
 
 
-def project(x, blocks, weights):
+def project(blocks, weights):
     groups, rows, depth = blocks.shape
-    across, along, cut, width = weights.shape
+    width = weights.shape[2]
     return pl.pallas_call(
         project_kernel,
         grid=(STEPS,),
         out_shape=jax.ShapeDtypeStruct((rows, width), jnp.bfloat16),
         in_specs=[
-            pl.BlockSpec(memory_space=pltpu.SMEM),
             pl.BlockSpec((groups // STEPS, rows, depth), lambda i: (i, 0, 0)),
-            pl.BlockSpec((across, along // STEPS, cut, width), lambda i: (0, i, 0, 0)),
+            pl.BlockSpec((groups // STEPS, depth, width), lambda i: (i, 0, 0)),
         ],
         out_specs=pl.BlockSpec((rows, width), lambda i: (0, 0)),
         scratch_shapes=[pltpu.VMEM((rows, width), jnp.float32)],
         name="project",
-    )(x, blocks, weights)
+    )(blocks, weights)
 
 
 def finish_kernel(y, dwa, first, second, weights, stream, past, block_out, dense_out, total):
@@ -268,16 +257,6 @@
     return jnp.where(odd == 0, straight, crossed)
 
 
-def along_x(block):
-    count = lax.axis_size("x")
-    half = block.shape[0] // 2
-    before = lax.ppermute(block, "x", ring(count, 1))
-    after = lax.ppermute(block, "x", ring(count, -1))
-    low = lax.ppermute(before[:half], "x", ring(count, 1))
-    high = lax.ppermute(after[half:], "x", ring(count, -1))
-    return jnp.stack([block, after, jnp.concatenate([low, high], 0), before])
-
-
 def on_device(stream, history, dwa_weights, w_query, w_out, encoded_kv, neighbour_ids):
     tok_rows = stream.shape[0]
     local_heads = w_query.shape[1] // HDIM
@@ -285,28 +264,28 @@
     db_count = lax.axis_size(DB)
     slots = neighbour_ids.shape[0] // ctx_count
     slab_rows = 2 * encoded_kv.shape[2]
-    x = lax.axis_index("x").astype(jnp.int32).reshape(1)
     y = lax.axis_index("y").astype(jnp.int32).reshape(1)
-
-    after = shifted(stream[:SPAN], -1)
-    own_spans = jnp.concatenate([stream[LEAD:], after[:LEAD]], 0)
+    width = stream.shape[1]
+
+    features = lax.all_gather(stream, DB, axis=0)
     by_head = split_heads(encoded_kv, local_heads)
     store = lax.all_to_all(
         by_head.reshape(db_count, -1, HDIM), DB, split_axis=0, concat_axis=0, tiled=True
     )
+    w_in = lax.all_gather(w_query, "x", axis=0)
+    w_in = lax.all_gather(w_in, "y", axis=0)
     turned = columns_here(w_out)
-    w_in = lax.all_gather(w_query, "y", axis=0)
-    w_in = along_x(w_in)
-    own_spans, store, turned = lax.optimization_barrier((own_spans, store, turned))
-    features = lax.all_gather(own_spans, DB, axis=0)
     picked = pick(neighbour_ids, store.reshape(-1, local_heads * slab_rows, HDIM))
+    turned, picked = lax.optimization_barrier((turned, picked))
     arrived = lax.all_to_all(
         picked.reshape(ctx_count, -1, HDIM), CTX, split_axis=0, concat_axis=0, tiled=True
     ).reshape(ctx_count, slots, local_heads, slab_rows, HDIM)
+    turned = lax.all_gather(turned, "x", axis=0)
     w_in, turned = lax.optimization_barrier((w_in, turned))
-    turned = lax.all_gather(turned, "x", axis=0)
     past = jnp.sum(history.astype(jnp.float32) * dwa_weights[:-1, None, None], axis=0)
-    queries = project(x, features, w_in)
+    queries = project(features, w_in.reshape(db_count, width, -1))
+    after = shifted(queries[:SPAN], -1)
+    queries = jnp.concatenate([queries[LEAD:], after[:LEAD]], 0)
     spans = tok_rows // SPAN
     last = attend(queries, arrived, spans - 1, 1)
     before = shifted(last, 1)

time: 247 us -> 197 us (0.80)
  the two profiles are of different devices: /device:TPU:24 before, /device:TPU:28 now
where the time goes in v4:
time: 197 us; the launch traced here: 196 us
  starting transfers between devices  70.8 us (36%)
  waiting for transfers between devices  57.7 us (29%)
  blocking collectives  28.1 us (14%)
  Pallas kernels  20.2 us (10%)
  between operations  14.1 us (7%)
  local copies, waits for them, and re-layouts  3.26 us (2%)
    all_to_all x1, waiting for transfers between devices, on_device(): lax.all_to_all(by_head.reshape(db_count, -1, HDIM), DB, split_axis=0, con...  20.6 us
    ppermute x4, starting transfers between devices, around(): right = lax.ppermute(right, axis, ring(count, 1))  19.3 us
    all_gather x1, blocking collectives, on_device(): turned = lax.all_gather(turned, 'x', axis=0)  15.4 us
    all_to_all x1, starting transfers between devices, on_device(): lax.all_to_all(picked.reshape(ctx_count, -1, HDIM), CTX, split_axis=0, co...  14.3 us
    all_gather x1, blocking collectives, on_device(): w_in = lax.all_gather(w_query, 'x', axis=0)  12.6 us
    ppermute x2, starting transfers between devices, columns_here(): pieces.append(lax.ppermute(send, CTX + DB, route))  12.2 us
    all_to_all x1, starting transfers between devices, on_device(): lax.all_to_all(by_head.reshape(db_count, -1, HDIM), DB, split_axis=0, con...  10.6 us
    all_gather x1, waiting for transfers between devices, on_device(): features = lax.all_gather(stream, DB, axis=0)  10.2 us
  transfers between devices with their start and end apart: 16, of which 11 were waited for; matrix products, arithmetic and copies ran while one was open for 2% of the time, Pallas kernels for 7%

profile of v4, /device:TPU:28, one launch (start us, length us, event | category | flops | bytes accessed | tf_op | source)
XLA Modules:
  0.0 196.1 jit_solution(4666311181350804945)
XLA Ops:
  7.2 0.0 all-gather.11.cloned.1.call-start
  7.2 12.6 %all-gather.1 = bf16[512,256]{1,0:T(8,128)(2,1)} all-gather(bf16[128,256]{1,0:T(8,128)(2,1)} %param.10), channel_id=3, replica_groups=mesh['y'=8,'x'=4,'z'=8,'core'=2] {'x'}, dimensions={0}, use_global_device_ids=true | all-gather | bytes 327680 | tf_op jit(solution)/shard_map/all_gather | solution.py:275
  19.8 0.0 all-gather.11.cloned.1.call-update
  19.9 0.0 all-gather.9.cloned.1.call-start
  19.9 0.7 all-gather.9.cloned.1.call-update
  20.6 3.1 %split_heads.1 = bf16[16,24,2,4,2,128]{5,4,3,2,1,0:T(2,128)(2,1)} custom-call(bf16[1,24,4,2,4096]{4,3,2,1,0:T(2,128)(2,1)} %source.1), custom_call_target="tpu_custom_call" | custom-call | tf_op jit(solution)/shard_map/split_heads/pallas_call | solution.py:45
  23.7 0.0 copy-start.4
  23.7 0.0 copy-start
  23.7 10.6 %all-to-all-start = ((bf16[16,384,128]{2,1,0:T(8,128)(2,1)}), bf16[16,384,128]{2,1,0:T(8,128)(2,1)S(1)}, u32[]{:S(2)}, u32[]{:S(2)}) async-start(bf16[16,384,128]{2,1,0:T(8,128)(2,1)} %bitcast.34), calls=%async_computation | async-start | bytes 3145728 | tf_op jit(solution)/shard_map/all_to_all | solution.py:272
  34.3 0.0 copy-done.4
  34.4 6.5 %collective-permute-start = (bf16[128,128]{1,0:T(8,128)(2,1)S(1)}, bf16[128,128]{1,0:T(8,128)(2,1)S(1)}, u32[]{:S(2)}, u32[]{:S(2)}) collective-permute-start(bf16[128,128]{1,0:T(8,128)(2,1)S(1)} %get-tuple-element.14), channel_id=1, source_target_pairs={{0,0},{1,32},{2,64},{3,96},{4,128},{5,160},{6,192},{7,224},{8,256}... | collective-permute-start | bytes 98312 | tf_op jit(solution)/shard_map/ppermute | solution.py:254
  40.8 5.7 %collective-permute-start.1 = (bf16[128,128]{1,0:T(8,128)(2,1)S(1)}, bf16[128,128]{1,0:T(8,128)(2,1)S(1)}, u32[]{:S(2)}, u32[]{:S(2)}) collective-permute-start(bf16[128,128]{1,0:T(8,128)(2,1)S(1)} %get-tuple-element.15), channel_id=1, source_target_pairs={{0,16},{1,48},{2,80},{3,112},{4,144},{5,176},{6,208},{7,240},{8,27... | collective-permute-start | bytes 98312 | tf_op jit(solution)/shard_map/ppermute | solution.py:254
  46.5 0.1 collective-permute-done
  46.6 6.6 %collective-permute-done.1 = bf16[128,128]{1,0:T(8,128)(2,1)S(1)} collective-permute-done((bf16[128,128]{1,0:T(8,128)(2,1)S(1)}, bf16[128,128]{1,0:T(8,128)(2,1)S(1)}, u32[]{:S(2)}, u32[]{:S(2)}) %collective-permute-start.1) | collective-permute-done | bytes 32800 | tf_op jit(solution)/shard_map/ppermute | solution.py:254
  53.2 20.6 %all-to-all-done = bf16[16,384,128]{2,1,0:T(8,128)(2,1)S(1)} async-done(((bf16[16,384,128]{2,1,0:T(8,128)(2,1)}), bf16[16,384,128]{2,1,0:T(8,128)(2,1)S(1)}, u32[]{:S(2)}, u32[]{:S(2)}) %all-to-all-start) | async-done | bytes 1572896 | tf_op jit(solution)/shard_map/all_to_all | solution.py:272
  73.9 0.0 copy-done
  73.9 2.4 %pick.1 = bf16[384,16,128]{2,1,0:T(8,128)(2,1)} custom-call(s32[384]{0:T(512)S(1)} %copy-done, bf16[384,16,128]{2,1,0:T(8,128)(2,1)S(1)} %bitcast.31), custom_call_target="tpu_custom_call" | custom-call | tf_op jit(solution)/shard_map/pick/pallas_call | solution.py:68
  76.3 14.3 %all-to-all-start.1 = ((bf16[32,192,128]{2,1,0:T(8,128)(2,1)}), bf16[32,192,128]{2,1,0:T(8,128)(2,1)S(1)}, u32[]{:S(2)}, u32[]{:S(2)}) async-start(bf16[32,192,128]{2,1,0:T(8,128)(2,1)} %bitcast.8), calls=%async_computation.1 | async-start | bytes 3145728 | tf_op jit(solution)/shard_map/all_to_all | solution.py:280
  90.6 0.0 all-gather.13.cloned.1.call-start
  90.6 15.4 %all-gather.3 = bf16[512,256]{1,0:T(8,128)(2,1)} all-gather(bf16[128,256]{1,0:T(8,128)(2,1)S(1)} %maximum_select_fusion), channel_id=5, replica_groups=mesh['y'=8,'x'=4,'z'=8,'core'=2] {'x'}, dimensions={0}, use_global_device_ids=true | all-gather | bytes 327680 | tf_op jit(solution)/shard_map/all_gather | solution.py:283
  106.1 0.0 all-gather.11.cloned.1.call-done
  106.1 10.2 %all-gather.9.cloned.1.call-done = bf16[6144,256]{1,0:T(8,128)(2,1)} async-done(((bf16[384,256]{1,0:T(8,128)(2,1)}), bf16[6144,256]{1,0:T(8,128)(2,1)}) %all-gather.9.cloned.1.call-update) | async-done | bytes 3145744 | tf_op jit(solution)/shard_map/all_gather | solution.py:270
  116.3 4.5 %project.1 = bf16[384,256]{1,0:T(8,128)(2,1)} custom-call(bf16[16,384,256]{2,1,0:T(8,128)(2,1)} %bitcast.35, bf16[16,256,256]{2,1,0:T(8,128)(2,1)} %bitcast.36), custom_call_target="tpu_custom_call" | custom-call | tf_op jit(solution)/shard_map/project/pallas_call | solution.py:156
  120.8 0.8 slice.25
  121.6 2.3 %collective-permute-start.2 = (bf16[64,256]{1,0:T(8,128)(2,1)S(1)}, bf16[64,256]{1,0:T(8,128)(2,1)S(1)}, u32[]{:S(2)}, u32[]{:S(2)}) collective-permute-start(bf16[64,256]{1,0:T(8,128)(2,1)S(1)} %slice.25), channel_id=1, source_target_pairs={{16,0},{32,16},{48,32},{64,48},{80,64},{96,80},{112,96},{128,112},... | collective-permute-start | bytes 98312 | tf_op jit(solution)/shard_map/ppermute | solution.py:123
  123.9 1.0 slice.24
  124.9 2.5 %collective-permute-done.2 = bf16[64,256]{1,0:T(8,128)(2,1)S(1)} collective-permute-done((bf16[64,256]{1,0:T(8,128)(2,1)S(1)}, bf16[64,256]{1,0:T(8,128)(2,1)S(1)}, u32[]{:S(2)}, u32[]{:S(2)}) %collective-permute-start.2) | collective-permute-done | bytes 32800 | tf_op jit(solution)/shard_map/ppermute | solution.py:123
  127.4 0.0 all-to-all-done.1
  127.4 0.0 copy-start.2
  127.4 0.0 copy-start.5
  127.4 1.0 shard_map.86
  128.4 6.3 %collective-permute-start.3 = (bf16[64,256]{1,0:T(8,128)(2,1)S(1)}, bf16[64,256]{1,0:T(8,128)(2,1)S(1)}, u32[]{:S(2)}, u32[]{:S(2)}) collective-permute-start(bf16[64,256]{1,0:T(8,128)(2,1)S(1)} %shard_map.86), channel_id=1, source_target_pairs={{0,16},{16,32},{32,48},{48,64},{64,80},{80,96},{96,112},{112,128},... | collective-permute-start | bytes 98312 | tf_op jit(solution)/shard_map/ppermute | solution.py:123
  134.7 4.2 %shard_map.87 = bf16[320,256]{1,0:T(8,128)(2,1)S(1)} custom-call(bf16[384,256]{1,0:T(8,128)(2,1)S(1)} %pad_maximum_fusion.q_ref, bf16[32,12,2,8,128]{4,3,2,1,0:T(8,128)(2,1)S(1)} %bitcast.30), custom_call_target="tpu_custom_call" | custom-call | tf_op jit(solution)/shard_map/pallas_call | solution.py:111
  139.0 0.0 collective-permute-done.3
  139.0 0.7 pad_maximum_fusion.1
  139.7 0.0 copy-start.3
  139.7 0.0 all-gather.13.cloned.1.call-update
  139.7 3.5 %collective-permute-start.4 = (bf16[4,128,256]{2,1,0:T(8,128)(2,1)}, bf16[4,128,256]{2,1,0:T(8,128)(2,1)S(1)}, u32[]{:S(2)}, u32[]{:S(2)}) collective-permute-start(bf16[4,128,256]{2,1,0:T(8,128)(2,1)} %bitcast.38), channel_id=1, source_target_pairs={{0,64},{64,128},{128,192},{192,256},{256,320},{320,384},{384,448},... | collective-permute-start | bytes 786440 | tf_op jit(solution)/shard_map/ppermute | solution.py:233
  143.3 5.7 %collective-permute-done.4 = bf16[4,128,256]{2,1,0:T(8,128)(2,1)S(1)} collective-permute-done((bf16[4,128,256]{2,1,0:T(8,128)(2,1)}, bf16[4,128,256]{2,1,0:T(8,128)(2,1)S(1)}, u32[]{:S(2)}, u32[]{:S(2)}) %collective-permute-start.4) | collective-permute-done | bytes 262176 | tf_op jit(solution)/shard_map/ppermute | solution.py:233
  149.0 4.6 %collective-permute-start.5 = (bf16[4,128,256]{2,1,0:T(8,128)(2,1)S(1)}, bf16[4,128,256]{2,1,0:T(8,128)(2,1)S(1)}, u32[]{:S(2)}, u32[]{:S(2)}) collective-permute-start(bf16[4,128,256]{2,1,0:T(8,128)(2,1)S(1)} %collective-permute-done.4), channel_id=1, source_target_pairs={{0,64},{64,128},{128,192},{192,256},{256,320},{320,384},{384,448},... | collective-permute-start | bytes 786440 | tf_op jit(solution)/shard_map/ppermute | solution.py:233
  153.6 1.9 collective-permute-start.8
  155.5 1.9 collective-permute-done.5
  157.4 5.6 %collective-permute-start.6 = (bf16[4,128,256]{2,1,0:T(8,128)(2,1)S(1)}, bf16[4,128,256]{2,1,0:T(8,128)(2,1)S(1)}, u32[]{:S(2)}, u32[]{:S(2)}) collective-permute-start(bf16[4,128,256]{2,1,0:T(8,128)(2,1)S(1)} %collective-permute-done.5), channel_id=1, source_target_pairs={{0,64},{64,128},{128,192},{192,256},{256,320},{320,384},{384,448},... | collective-permute-start | bytes 786440 | tf_op jit(solution)/shard_map/ppermute | solution.py:233
  163.0 0.2 collective-permute-done.8
  163.3 1.9 collective-permute-start.9
  165.2 1.7 collective-permute-done.6
  166.9 5.6 %collective-permute-start.7 = (bf16[4,128,256]{2,1,0:T(8,128)(2,1)S(1)}, bf16[4,128,256]{2,1,0:T(8,128)(2,1)S(1)}, u32[]{:S(2)}, u32[]{:S(2)}) collective-permute-start(bf16[4,128,256]{2,1,0:T(8,128)(2,1)S(1)} %collective-permute-done.6), channel_id=1, source_target_pairs={{0,64},{64,128},{128,192},{192,256},{256,320},{320,384},{384,448},... | collective-permute-start | bytes 786440 | tf_op jit(solution)/shard_map/ppermute | solution.py:233
  172.5 0.0 copy-done.2
  172.5 0.0 copy-done.5
  172.5 1.1 multiply_reduce_fusion.past
  173.7 0.0 collective-permute-done.9
  173.7 1.9 collective-permute-start.10
  175.6 0.8 collective-permute-done.7
  176.5 0.0 copy-done.3
  176.6 6.6 %collective-permute-done.10 = bf16[4,128,256]{2,1,0:T(8,128)(2,1)S(1)} collective-permute-done((bf16[4,128,256]{2,1,0:T(8,128)(2,1)S(1)}, bf16[4,128,256]{2,1,0:T(8,128)(2,1)S(1)}, u32[]{:S(2)}, u32[]{:S(2)}) %collective-permute-start.10) | collective-permute-done | bytes 262176 | tf_op jit(solution)/shard_map/ppermute | solution.py:236
  183.2 0.0 copy-start.1
  183.2 0.0 all-gather.13.cloned.1.call-done
  183.2 1.3 copy-done.1
  184.5 5.0 %finish.1 = (bf16[384,256]{1,0:T(8,128)(2,1)}, bf16[384,256]{1,0:T(8,128)(2,1)}) custom-call(s32[1]{0:T(128)} %bitcast.y, f32[9]{0:T(128)} %dwa.1, bf16[16,384,256]{2,1,0:T(8,128)(2,1)} %bitcast.32, bf16[16,384,256]{2,1,0:T(8,128)(2,1)} %bitcast.33, bf16[8,4,128,256]{3,2,1,0:T(8,128)(2,1)} %copy-done.1, bf16[384,256]{1,0:T(8,128)(2,1)} %stream.1, ...), custom_call_target="tpu_custom_call" | custom-call | tf_op jit(solution)/shard_map/finish/pallas_call | solution.py:207
  (13 shorter events, 0.2 us)
Async XLA Ops:
  7.2 98.9 %all-gather.11.cloned.1.call-start = ((), (), s32[]{:S(2)}) async-start(), calls=%async_computation.3 | async-start | bytes 2359296 | tf_op jit(solution)/shard_map/all_gather | solution.py:276
  19.9 96.4 %all-gather.9.cloned.1.call-start = ((), (), s32[]{:S(2)}) async-start(), calls=%async_computation.2 | async-start | bytes 3342336 | tf_op jit(solution)/shard_map/all_gather | solution.py:270
  23.7 10.6 %copy-start.4 = (bf16[256,128]{1,0:T(8,128)(2,1)S(1)}, bf16[256,128]{1,0:T(8,128)(2,1)}, u32[]{:S(2)}) copy-start(bf16[256,128]{1,0:T(8,128)(2,1)} %param.11) | copy-start | bytes 196612
  23.7 50.2 %copy-start = (s32[384]{0:T(512)S(1)}, s32[384]{0:T(512)}, u32[]{:S(2)}) copy-start(s32[384]{0:T(512)} %ids.1) | copy-start | bytes 4612
  23.7 50.1 %all-to-all-start = ((bf16[16,384,128]{2,1,0:T(8,128)(2,1)}), bf16[16,384,128]{2,1,0:T(8,128)(2,1)S(1)}, u32[]{:S(2)}, u32[]{:S(2)}) async-start(bf16[16,384,128]{2,1,0:T(8,128)(2,1)} %bitcast.34), calls=%async_computation | async-start | bytes 3145728 | tf_op jit(solution)/shard_map/all_to_all | solution.py:272
  34.4 12.3 %collective-permute-start = (bf16[128,128]{1,0:T(8,128)(2,1)S(1)}, bf16[128,128]{1,0:T(8,128)(2,1)S(1)}, u32[]{:S(2)}, u32[]{:S(2)}) collective-permute-start(bf16[128,128]{1,0:T(8,128)(2,1)S(1)} %get-tuple-element.14), channel_id=1, source_target_pairs={{0,0},{1,32},{2,64},{3,96},{4,128},{5,160},{6,192},{7,224},{8,256}... | collective-permute-start | bytes 98312 | tf_op jit(solution)/shard_map/ppermute | solution.py:254
  40.8 12.4 %collective-permute-start.1 = (bf16[128,128]{1,0:T(8,128)(2,1)S(1)}, bf16[128,128]{1,0:T(8,128)(2,1)S(1)}, u32[]{:S(2)}, u32[]{:S(2)}) collective-permute-start(bf16[128,128]{1,0:T(8,128)(2,1)S(1)} %get-tuple-element.15), channel_id=1, source_target_pairs={{0,16},{1,48},{2,80},{3,112},{4,144},{5,176},{6,208},{7,240},{8,27... | collective-permute-start | bytes 98312 | tf_op jit(solution)/shard_map/ppermute | solution.py:254
  76.3 51.2 %all-to-all-start.1 = ((bf16[32,192,128]{2,1,0:T(8,128)(2,1)}), bf16[32,192,128]{2,1,0:T(8,128)(2,1)S(1)}, u32[]{:S(2)}, u32[]{:S(2)}) async-start(bf16[32,192,128]{2,1,0:T(8,128)(2,1)} %bitcast.8), calls=%async_computation.1 | async-start | bytes 3145728 | tf_op jit(solution)/shard_map/all_to_all | solution.py:280
  90.6 92.6 %all-gather.13.cloned.1.call-start = ((), (), s32[]{:S(2)}) async-start(), calls=%async_computation.4 | async-start | bytes 3342336 | tf_op jit(solution)/shard_map/all_gather | solution.py:295
  121.6 5.8 %collective-permute-start.2 = (bf16[64,256]{1,0:T(8,128)(2,1)S(1)}, bf16[64,256]{1,0:T(8,128)(2,1)S(1)}, u32[]{:S(2)}, u32[]{:S(2)}) collective-permute-start(bf16[64,256]{1,0:T(8,128)(2,1)S(1)} %slice.25), channel_id=1, source_target_pairs={{16,0},{32,16},{48,32},{64,48},{80,64},{96,80},{112,96},{128,112},... | collective-permute-start | bytes 98312 | tf_op jit(solution)/shard_map/ppermute | solution.py:123
  127.4 45.1 %copy-start.2 = (bf16[8,384,256]{2,1,0:T(8,128)(2,1)S(1)}, bf16[8,384,256]{2,1,0:T(8,128)(2,1)}, u32[]{:S(2)}) copy-start(bf16[8,384,256]{2,1,0:T(8,128)(2,1)} %param.8) | copy-start | bytes 4718596
  127.4 45.1 %copy-start.5 = (f32[9]{0:T(128)S(1)}, f32[9]{0:T(128)}, u32[]{:S(2)}) copy-start(f32[9]{0:T(128)} %dwa.1) | copy-start | bytes 112
  128.4 10.6 %collective-permute-start.3 = (bf16[64,256]{1,0:T(8,128)(2,1)S(1)}, bf16[64,256]{1,0:T(8,128)(2,1)S(1)}, u32[]{:S(2)}, u32[]{:S(2)}) collective-permute-start(bf16[64,256]{1,0:T(8,128)(2,1)S(1)} %shard_map.86), channel_id=1, source_target_pairs={{0,16},{16,32},{32,48},{48,64},{64,80},{80,96},{96,112},{112,128},... | collective-permute-start | bytes 98312 | tf_op jit(solution)/shard_map/ppermute | solution.py:123
  139.7 36.8 %copy-start.3 = (bf16[512,256]{1,0:T(8,128)(2,1)S(1)}, bf16[512,256]{1,0:T(8,128)(2,1)}, u32[]{:S(2)}) copy-start(bf16[512,256]{1,0:T(8,128)(2,1)} %all-gather.3) | copy-start | bytes 786436
  139.7 9.2 %collective-permute-start.4 = (bf16[4,128,256]{2,1,0:T(8,128)(2,1)}, bf16[4,128,256]{2,1,0:T(8,128)(2,1)S(1)}, u32[]{:S(2)}, u32[]{:S(2)}) collective-permute-start(bf16[4,128,256]{2,1,0:T(8,128)(2,1)} %bitcast.38), channel_id=1, source_target_pairs={{0,64},{64,128},{128,192},{192,256},{256,320},{320,384},{384,448},... | collective-permute-start | bytes 786440 | tf_op jit(solution)/shard_map/ppermute | solution.py:233
  149.0 8.5 %collective-permute-start.5 = (bf16[4,128,256]{2,1,0:T(8,128)(2,1)S(1)}, bf16[4,128,256]{2,1,0:T(8,128)(2,1)S(1)}, u32[]{:S(2)}, u32[]{:S(2)}) collective-permute-start(bf16[4,128,256]{2,1,0:T(8,128)(2,1)S(1)} %collective-permute-done.4), channel_id=1, source_target_pairs={{0,64},{64,128},{128,192},{192,256},{256,320},{320,384},{384,448},... | collective-permute-start | bytes 786440 | tf_op jit(solution)/shard_map/ppermute | solution.py:233
  153.6 9.7 %collective-permute-start.8 = (bf16[4,128,256]{2,1,0:T(8,128)(2,1)}, bf16[4,128,256]{2,1,0:T(8,128)(2,1)S(1)}, u32[]{:S(2)}, u32[]{:S(2)}) collective-permute-start(bf16[4,128,256]{2,1,0:T(8,128)(2,1)} %bitcast.39), channel_id=1, source_target_pairs={{0,448},{64,0},{128,64},{192,128},{256,192},{320,256},{384,320},{4... | collective-permute-start | bytes 786440 | tf_op jit(solution)/shard_map/ppermute | solution.py:236
  157.4 9.5 %collective-permute-start.6 = (bf16[4,128,256]{2,1,0:T(8,128)(2,1)S(1)}, bf16[4,128,256]{2,1,0:T(8,128)(2,1)S(1)}, u32[]{:S(2)}, u32[]{:S(2)}) collective-permute-start(bf16[4,128,256]{2,1,0:T(8,128)(2,1)S(1)} %collective-permute-done.5), channel_id=1, source_target_pairs={{0,64},{64,128},{128,192},{192,256},{256,320},{320,384},{384,448},... | collective-permute-start | bytes 786440 | tf_op jit(solution)/shard_map/ppermute | solution.py:233
  163.3 10.4 %collective-permute-start.9 = (bf16[4,128,256]{2,1,0:T(8,128)(2,1)S(1)}, bf16[4,128,256]{2,1,0:T(8,128)(2,1)S(1)}, u32[]{:S(2)}, u32[]{:S(2)}) collective-permute-start(bf16[4,128,256]{2,1,0:T(8,128)(2,1)S(1)} %collective-permute-done.8), channel_id=1, source_target_pairs={{0,448},{64,0},{128,64},{192,128},{256,192},{320,256},{384,320},{4... | collective-permute-start | bytes 786440 | tf_op jit(solution)/shard_map/ppermute | solution.py:236
  166.9 9.5 %collective-permute-start.7 = (bf16[4,128,256]{2,1,0:T(8,128)(2,1)S(1)}, bf16[4,128,256]{2,1,0:T(8,128)(2,1)S(1)}, u32[]{:S(2)}, u32[]{:S(2)}) collective-permute-start(bf16[4,128,256]{2,1,0:T(8,128)(2,1)S(1)} %collective-permute-done.6), channel_id=1, source_target_pairs={{0,64},{64,128},{128,192},{192,256},{256,320},{320,384},{384,448},... | collective-permute-start | bytes 786440 | tf_op jit(solution)/shard_map/ppermute | solution.py:233
  173.7 9.5 %collective-permute-start.10 = (bf16[4,128,256]{2,1,0:T(8,128)(2,1)S(1)}, bf16[4,128,256]{2,1,0:T(8,128)(2,1)S(1)}, u32[]{:S(2)}, u32[]{:S(2)}) collective-permute-start(bf16[4,128,256]{2,1,0:T(8,128)(2,1)S(1)} %collective-permute-done.9), channel_id=1, source_target_pairs={{0,448},{64,0},{128,64},{192,128},{256,192},{320,256},{384,320},{4... | collective-permute-start | bytes 786440 | tf_op jit(solution)/shard_map/ppermute | solution.py:236
  183.2 1.4 copy-start.1
Sparse Core Ops, SparseCore 0:
  20.0 48.8 all-gather.10
  71.0 45.2 all-gather.8
  139.9 40.8 all-gather.12

commit v5 on v2

--- a/solution.py
+++ b/solution.py
@@ -50,7 +50,6 @@
         in_specs=[any_space()],
         out_specs=vmem_space(),
         scratch_shapes=[pltpu.SemaphoreType.DMA((heads,))],
-        compiler_params=ROOM,
         name="split_heads",
     )(encoded)
 
@@ -173,25 +172,27 @@
     )(place, mine, other, weights)
 
 
-def finish_kernel(x, dwa, attended, weights, stream, past, block_out, dense_out, total):
+BAND = 128
+
+
+def finish_kernel(y, dwa, first, second, weights, stream, past, block_out, dense_out, total):
     step = pl.program_id(0)
-    across, _, depth, _ = weights.shape
+    width = weights.shape[3]
 
     @pl.when(step == 0)
     def _():
         total[...] = jnp.zeros(total.shape, jnp.float32)
 
-    pieces = attended.shape[2] // depth
-    for g in range(attended.shape[0]):
-        part = jnp.zeros(total.shape, jnp.float32)
-        for piece in range(pieces):
-            at = lax.rem(g * pieces + piece + across - x[0], across)
-            part += jnp.dot(
-                attended[g, :, piece * depth : (piece + 1) * depth],
-                weights[at, 0],
-                preferred_element_type=jnp.float32,
-            )
-        total[...] += part.astype(jnp.bfloat16).astype(jnp.float32)
+    for row in range(0, total.shape[0], BAND):
+        rows = slice(row, row + BAND)
+        value = total[rows, :]
+        for which, blocks in enumerate((first, second)):
+            groups, _, depth = blocks.shape
+            matching = weights[which].reshape(groups, depth, width)
+            for g in range(groups):
+                part = jnp.dot(blocks[g, rows, :], matching[g], preferred_element_type=jnp.float32)
+                value += part.astype(jnp.bfloat16).astype(jnp.float32)
+        total[rows, :] = value
 
     @pl.when(step == pl.num_programs(0) - 1)
     def _():
@@ -200,29 +201,36 @@
         dense_out[...] = (dwa[dwa.shape[0] - 1] * block + past[...]).astype(dense_out.dtype)
 
 
-def finish(x, dwa, attended, weights, stream, past):
-    groups, rows, depth = attended.shape
-    across, along, cut, width = weights.shape
+def finish(y, dwa, blocks, weights, stream, past):
+    groups, rows, depth = blocks.shape
+    along, across, cut, width = weights.shape
+    steps = along // 2
     here = groups // along
-    scalars = pl.BlockSpec(memory_space=pltpu.SMEM)
-    whole = pl.BlockSpec(stream.shape, lambda i: (0, 0))
+
+    def at(which):
+        return lambda i, y: (lax.rem(y[0] + 2 * i + which + along - along // 2, along), 0, 0)
+
+    whole = pl.BlockSpec((rows, width), lambda i, y: (0, 0))
     shape = jax.ShapeDtypeStruct(stream.shape, jnp.bfloat16)
     return pl.pallas_call(
         finish_kernel,
-        grid=(along,),
         out_shape=(shape, shape),
-        in_specs=[
-            scalars,
-            scalars,
-            pl.BlockSpec((here, rows, depth), lambda i: (i, 0, 0)),
-            pl.BlockSpec((across, 1, cut, width), lambda i: (0, i, 0, 0)),
-            whole,
-            whole,
-        ],
-        out_specs=(whole, whole),
-        scratch_shapes=[pltpu.VMEM(stream.shape, jnp.float32)],
+        grid_spec=pltpu.PrefetchScalarGridSpec(
+            num_scalar_prefetch=1,
+            grid=(steps,),
+            in_specs=[
+                pl.BlockSpec(memory_space=pltpu.SMEM),
+                pl.BlockSpec((here, rows, depth), at(0)),
+                pl.BlockSpec((here, rows, depth), at(1)),
+                pl.BlockSpec((2, across, cut, width), lambda i, y: (i, 0, 0, 0)),
+                whole,
+                whole,
+            ],
+            out_specs=(whole, whole),
+            scratch_shapes=[pltpu.VMEM(stream.shape, jnp.float32)],
+        ),
         name="finish",
-    )(x, dwa, attended, weights, stream, past)
+    )(y, dwa, blocks, blocks, weights, stream, past)
 
 
 def columns_here(w_out):
@@ -244,25 +252,15 @@
     return jnp.where(odd == 0, straight, crossed)
 
 
-def along_x(block):
-    count = lax.axis_size("x")
-    half = block.shape[0] // 2
-    before = lax.ppermute(block, "x", ring(count, 1))
-    after = lax.ppermute(block, "x", ring(count, -1))
-    low = lax.ppermute(before[:half], "x", ring(count, 1))
-    high = lax.ppermute(after[half:], "x", ring(count, -1))
-    return jnp.stack([block, after, jnp.concatenate([low, high], 0), before])
-
-
 def on_device(stream, history, dwa_weights, w_query, w_out, encoded_kv, neighbour_ids):
-    tok_rows, _ = stream.shape
+    tok_rows = stream.shape[0]
     local_heads = w_query.shape[1] // HDIM
     ctx_count = lax.axis_size(CTX)
     db_count = lax.axis_size(DB)
     slots = neighbour_ids.shape[0] // ctx_count
     slab_rows = 2 * encoded_kv.shape[2]
     place = jnp.stack([lax.axis_index("z"), lax.axis_index("core")]).astype(jnp.int32)
-    x = lax.axis_index("x").astype(jnp.int32).reshape(1)
+    y = lax.axis_index("y").astype(jnp.int32).reshape(1)
 
     w_in = lax.all_gather(w_query, CTX, axis=0)
     by_head = split_heads(encoded_kv, local_heads)
@@ -272,7 +270,7 @@
     after = shifted(stream[:SPAN], -1)
     own_spans = jnp.concatenate([stream[LEAD:], after[:LEAD]], 0)
     turned = columns_here(w_out)
-    turned = lax.all_gather(turned, "y", axis=0)
+    turned = lax.all_gather(turned, "x", axis=0)
 
     picked = pick(neighbour_ids, store.reshape(-1, local_heads * slab_rows, HDIM))
     own_spans, turned, picked = lax.optimization_barrier((own_spans, turned, picked))
@@ -289,8 +287,8 @@
     attended = jnp.concatenate([before[1:], rest, last[:1]], 0)
     attended, turned = lax.optimization_barrier((attended, turned))
     everyone = lax.all_gather(attended, DB, axis=0)
-    columns = along_x(turned)
-    return finish(x, dwa_weights, everyone, columns, stream, past)
+    columns = around(turned, "y")
+    return finish(y, dwa_weights, everyone, columns, stream, past)
 
 
 def solution(mesh):

time: 238 us -> 233 us (0.979)
  the two profiles are of different devices: /device:TPU:1 before, /device:TPU:24 now
where the time goes in v5:
time: 233 us; the launch traced here: 232 us
  starting transfers between devices  95.4 us (41%)
  waiting for transfers between devices  78.5 us (34%)
  Pallas kernels  19.3 us (8%)
  between operations  14.6 us (6%)
  blocking collectives  13.7 us (6%)
  local copies, waits for them, and re-layouts  7 us (3%)
  other arithmetic  3.43 us (1%)
    all_gather x1, waiting for transfers between devices, on_device(): w_in = lax.all_gather(w_query, CTX, axis=0)  39.2 us
    ppermute x8, starting transfers between devices, around(): right = lax.ppermute(right, axis, ring(count, 1))  31.2 us
    ppermute x8, waiting for transfers between devices, around(): right = lax.ppermute(right, axis, ring(count, 1))  20.6 us
    ppermute x6, starting transfers between devices, around(): left = lax.ppermute(left, axis, ring(count, -1))  19.6 us
    all_to_all x1, starting transfers between devices, on_device(): lax.all_to_all(picked.reshape(ctx_count, -1, HDIM), CTX, split_axis=0, co...  13.8 us
    all_gather x1, blocking collectives, on_device(): turned = lax.all_gather(turned, 'x', axis=0)  13.7 us
    ppermute x2, starting transfers between devices, columns_here(): pieces.append(lax.ppermute(send, CTX + DB, route))  11.3 us
    all_to_all x1, starting transfers between devices, on_device(): lax.all_to_all(by_head.reshape(db_count, -1, HDIM), DB, split_axis=0, con...  10.6 us
  transfers between devices with their start and end apart: 23, of which 11 were waited for; matrix products, arithmetic and copies ran while one was open for 3% of the time, Pallas kernels for 3%

profile of v5, /device:TPU:24, one launch (start us, length us, event | category | flops | bytes accessed | tf_op | source)
XLA Modules:
  0.0 231.9 jit_solution(8453312068584714355)
XLA Ops:
  7.2 3.1 %split_heads.1 = bf16[16,24,2,4,2,128]{5,4,3,2,1,0:T(2,128)(2,1)} custom-call(bf16[1,24,4,2,4096]{4,3,2,1,0:T(2,128)(2,1)} %source.1), custom_call_target="tpu_custom_call" | custom-call | tf_op jit(solution)/shard_map/split_heads/pallas_call | solution.py:45
  10.2 0.0 copy-start.9
  10.3 0.0 copy-start.4
  10.3 0.0 copy-start.1
  10.3 10.6 %all-to-all-start = ((bf16[16,384,128]{2,1,0:T(8,128)(2,1)}), bf16[16,384,128]{2,1,0:T(8,128)(2,1)S(1)}, u32[]{:S(2)}, u32[]{:S(2)}) async-start(bf16[16,384,128]{2,1,0:T(8,128)(2,1)} %bitcast.51), calls=%async_computation | async-start | bytes 3145728 | tf_op jit(solution)/shard_map/all_to_all | solution.py:267
  20.8 0.0 all-gather.5.cloned.1.call-start
  21.0 5.3 %collective-permute-start.1 = (bf16[128,128]{1,0:T(8,128)(2,1)S(1)}, bf16[128,128]{1,0:T(8,128)(2,1)S(1)}, u32[]{:S(2)}, u32[]{:S(2)}) collective-permute-start(bf16[128,128]{1,0:T(8,128)(2,1)S(1)} %get-tuple-element.12), channel_id=1, source_target_pairs={{0,0},{1,32},{2,64},{3,96},{4,128},{5,160},{6,192},{7,224},{8,256}... | collective-permute-start | bytes 98312 | tf_op jit(solution)/shard_map/ppermute | solution.py:249
  26.3 6.0 %collective-permute-start.2 = (bf16[128,128]{1,0:T(8,128)(2,1)S(1)}, bf16[128,128]{1,0:T(8,128)(2,1)S(1)}, u32[]{:S(2)}, u32[]{:S(2)}) collective-permute-start(bf16[128,128]{1,0:T(8,128)(2,1)S(1)} %get-tuple-element.13), channel_id=1, source_target_pairs={{0,16},{1,48},{2,80},{3,112},{4,144},{5,176},{6,208},{7,240},{8,27... | collective-permute-start | bytes 98312 | tf_op jit(solution)/shard_map/ppermute | solution.py:249
  32.3 3.9 %collective-permute-start = (bf16[64,256]{1,0:T(8,128)(2,1)S(1)}, bf16[64,256]{1,0:T(8,128)(2,1)S(1)}, u32[]{:S(2)}, u32[]{:S(2)}) collective-permute-start(bf16[64,256]{1,0:T(8,128)(2,1)S(1)} %slice.19), channel_id=1, source_target_pairs={{16,0},{32,16},{48,32},{64,48},{80,64},{96,80},{112,96},{128,112},... | collective-permute-start | bytes 98312 | tf_op jit(solution)/shard_map/ppermute | solution.py:123
  36.3 0.0 collective-permute-done.1
  36.3 2.7 %collective-permute-done.2 = bf16[128,128]{1,0:T(8,128)(2,1)S(1)} collective-permute-done((bf16[128,128]{1,0:T(8,128)(2,1)S(1)}, bf16[128,128]{1,0:T(8,128)(2,1)S(1)}, u32[]{:S(2)}, u32[]{:S(2)}) %collective-permute-start.2) | collective-permute-done | bytes 32800 | tf_op jit(solution)/shard_map/ppermute | solution.py:249
  39.0 13.7 %all_gather.16 = bf16[4,128,256]{2,1,0:T(8,128)(2,1)} all-gather(bf16[1,128,256]{2,1,0:T(8,128)(2,1)S(1)} %maximum_select_fusion), channel_id=1, replica_groups=mesh['y'=8,'x'=4,'z'=8,'core'=2] {'x'}, dimensions={0}, use_global_device_ids=true | all-gather | bytes 327680 | tf_op jit(solution)/shard_map/all_gather | solution.py:273
  52.7 7.7 %all-to-all-done = bf16[16,384,128]{2,1,0:T(8,128)(2,1)S(1)} async-done(((bf16[16,384,128]{2,1,0:T(8,128)(2,1)}), bf16[16,384,128]{2,1,0:T(8,128)(2,1)S(1)}, u32[]{:S(2)}, u32[]{:S(2)}) %all-to-all-start) | async-done | bytes 1572896 | tf_op jit(solution)/shard_map/all_to_all | solution.py:267
  60.5 2.4 %pick.1 = bf16[384,16,128]{2,1,0:T(8,128)(2,1)} custom-call(s32[384]{0:T(512)S(1)} %copy-done.1, bf16[384,16,128]{2,1,0:T(8,128)(2,1)S(1)} %bitcast.47), custom_call_target="tpu_custom_call" | custom-call | tf_op jit(solution)/shard_map/pick/pallas_call | solution.py:68
  62.8 4.6 %collective-permute-start.3 = (bf16[384,256]{1,0:T(8,128)(2,1)S(1)}, bf16[384,256]{1,0:T(8,128)(2,1)S(1)}, u32[]{:S(2)}, u32[]{:S(2)}) collective-permute-start(bf16[384,256]{1,0:T(8,128)(2,1)S(1)} %pad_maximum_fusion), channel_id=1, source_target_pairs={{0,2},{2,4},{4,6},{6,8},{8,10},{10,12},{12,14},{14,0},{1,3},{3,5},... | collective-permute-start | bytes 589832 | tf_op jit(solution)/shard_map/ppermute | solution.py:135
  67.4 0.0 all-gather.5.cloned.1.call-update
  67.4 6.3 %collective-permute-done.3 = bf16[384,256]{1,0:T(8,128)(2,1)S(1)} collective-permute-done((bf16[384,256]{1,0:T(8,128)(2,1)S(1)}, bf16[384,256]{1,0:T(8,128)(2,1)S(1)}, u32[]{:S(2)}, u32[]{:S(2)}) %collective-permute-start.3) | collective-permute-done | bytes 196640 | tf_op jit(solution)/shard_map/ppermute | solution.py:135
  73.7 3.4 %collective-permute-start.4 = (bf16[384,256]{1,0:T(8,128)(2,1)S(1)}, bf16[384,256]{1,0:T(8,128)(2,1)S(1)}, u32[]{:S(2)}, u32[]{:S(2)}) collective-permute-start(bf16[384,256]{1,0:T(8,128)(2,1)S(1)} %collective-permute-done.3), channel_id=1, source_target_pairs={{0,2},{2,4},{4,6},{6,8},{8,10},{10,12},{12,14},{14,0},{1,3},{3,5},... | collective-permute-start | bytes 589832 | tf_op jit(solution)/shard_map/ppermute | solution.py:135
  77.0 3.7 %collective-permute-start.7 = (bf16[384,256]{1,0:T(8,128)(2,1)S(1)}, bf16[384,256]{1,0:T(8,128)(2,1)S(1)}, u32[]{:S(2)}, u32[]{:S(2)}) collective-permute-start(bf16[384,256]{1,0:T(8,128)(2,1)S(1)} %pad_maximum_fusion), channel_id=1, source_target_pairs={{0,14},{2,0},{4,2},{6,4},{8,6},{10,8},{12,10},{14,12},{1,15},{3,1}... | collective-permute-start | bytes 589832 | tf_op jit(solution)/shard_map/ppermute | solution.py:138
  80.7 3.0 %collective-permute-done.4 = bf16[384,256]{1,0:T(8,128)(2,1)S(1)} collective-permute-done((bf16[384,256]{1,0:T(8,128)(2,1)S(1)}, bf16[384,256]{1,0:T(8,128)(2,1)S(1)}, u32[]{:S(2)}, u32[]{:S(2)}) %collective-permute-start.4) | collective-permute-done | bytes 196640 | tf_op jit(solution)/shard_map/ppermute | solution.py:135
  83.7 2.1 collective-permute-start.5
  85.9 0.0 collective-permute-done.7
  85.9 4.9 %collective-permute-start.8 = (bf16[384,256]{1,0:T(8,128)(2,1)S(1)}, bf16[384,256]{1,0:T(8,128)(2,1)}, u32[]{:S(2)}, u32[]{:S(2)}) collective-permute-start(bf16[384,256]{1,0:T(8,128)(2,1)S(1)} %collective-permute-done.7), channel_id=1, source_target_pairs={{0,14},{2,0},{4,2},{6,4},{8,6},{10,8},{12,10},{14,12},{1,15},{3,1}... | collective-permute-start | bytes 589832 | tf_op jit(solution)/shard_map/ppermute | solution.py:138
  90.8 2.1 collective-permute-done.5
  92.9 1.9 collective-permute-start.6
  94.8 13.8 %all-to-all-start.1 = ((bf16[32,192,128]{2,1,0:T(8,128)(2,1)}), bf16[32,192,128]{2,1,0:T(8,128)(2,1)S(1)}, u32[]{:S(2)}, u32[]{:S(2)}) async-start(bf16[32,192,128]{2,1,0:T(8,128)(2,1)} %bitcast.16), calls=%async_computation.1 | async-start | bytes 3145728 | tf_op jit(solution)/shard_map/all_to_all | solution.py:277
  108.6 0.0 all-gather.7.cloned.1.call-start
  108.7 5.3 %collective-permute-start.9 = (bf16[384,256]{1,0:T(8,128)(2,1)}, bf16[384,256]{1,0:T(8,128)(2,1)S(1)}, u32[]{:S(2)}, u32[]{:S(2)}) collective-permute-start(bf16[384,256]{1,0:T(8,128)(2,1)} %collective-permute-done.8), channel_id=1, source_target_pairs={{0,14},{2,0},{4,2},{6,4},{8,6},{10,8},{12,10},{14,12},{1,15},{3,1}... | collective-permute-start | bytes 589832 | tf_op jit(solution)/shard_map/ppermute | solution.py:138
  114.0 0.0 collective-permute-done.6
  114.0 0.9 bitcast_dynamic-update-slice_fusion.15
  114.9 0.9 bitcast_dynamic-update-slice_fusion.14
  115.9 0.9 bitcast_dynamic-update-slice_fusion.13
  116.9 0.9 bitcast_dynamic-update-slice_fusion.9
  117.8 0.0 collective-permute-done.9
  117.9 1.9 collective-permute-start.10
  119.8 0.1 pad_add_fusion.place
  119.9 39.2 %all-gather.5.cloned.1.call-done = bf16[4096,256]{1,0:T(8,128)(2,1)} async-done(((bf16[128,256]{1,0:T(8,128)(2,1)}), bf16[4096,256]{1,0:T(8,128)(2,1)}) %all-gather.5.cloned.1.call-update) | async-done | bytes 2097168 | tf_op jit(solution)/shard_map/all_gather | solution.py:265
  159.1 1.6 copy-done
  160.7 3.7 %project.1.q_ref = bf16[384,256]{1,0:T(8,128)(2,1)S(1)} custom-call(s32[2]{0:T(128)S(1)} %pad_add_fusion.place, bf16[8,384,256]{2,1,0:T(8,128)(2,1)S(1)} %bitcast_dynamic-update-slice_fusion.8.mine, bf16[8,384,256]{2,1,0:T(8,128)(2,1)} %collective-permute-done.10.other, bf16[32,128,256]{2,1,0:T(8,128)(2,1)S(1)} %bitcast.48), custom_call_target="tpu_custom_call" | custom-call | tf_op jit(solution)/shard_map/project/pallas_call | solution.py:165
  164.4 0.0 all-to-all-done.1
  164.4 1.0 shard_map.86
  165.3 0.0 copy-start.10
  165.4 3.0 %collective-permute-start.11 = (bf16[64,256]{1,0:T(8,128)(2,1)S(1)}, bf16[64,256]{1,0:T(8,128)(2,1)S(1)}, u32[]{:S(2)}, u32[]{:S(2)}) collective-permute-start(bf16[64,256]{1,0:T(8,128)(2,1)S(1)} %shard_map.86), channel_id=1, source_target_pairs={{0,16},{16,32},{32,48},{48,64},{64,80},{80,96},{96,112},{112,128},... | collective-permute-start | bytes 98312 | tf_op jit(solution)/shard_map/ppermute | solution.py:123
  168.4 4.2 %shard_map.87 = bf16[320,256]{1,0:T(8,128)(2,1)S(1)} custom-call(bf16[384,256]{1,0:T(8,128)(2,1)S(1)} %project.1.q_ref, bf16[32,12,2,8,128]{4,3,2,1,0:T(8,128)(2,1)S(1)} %bitcast.46), custom_call_target="tpu_custom_call" | custom-call | tf_op jit(solution)/shard_map/pallas_call | solution.py:111
  172.6 0.8 collective-permute-done.11
  173.4 0.7 pad_maximum_fusion.1
  174.1 0.0 all-gather.7.cloned.1.call-update
  174.2 3.4 %collective-permute-start.12 = (bf16[4,128,256]{2,1,0:T(8,128)(2,1)S(1)}, bf16[4,128,256]{2,1,0:T(8,128)(2,1)S(1)}, u32[]{:S(2)}, u32[]{:S(2)}) collective-permute-start(bf16[4,128,256]{2,1,0:T(8,128)(2,1)S(1)} %copy-done.3), channel_id=1, source_target_pairs={{0,64},{64,128},{128,192},{192,256},{256,320},{320,384},{384,448},... | collective-permute-start | bytes 786440 | tf_op jit(solution)/shard_map/ppermute | solution.py:135
  177.6 4.8 %collective-permute-done.12 = bf16[4,128,256]{2,1,0:T(8,128)(2,1)S(1)} collective-permute-done((bf16[4,128,256]{2,1,0:T(8,128)(2,1)S(1)}, bf16[4,128,256]{2,1,0:T(8,128)(2,1)S(1)}, u32[]{:S(2)}, u32[]{:S(2)}) %collective-permute-start.12) | collective-permute-done | bytes 262176 | tf_op jit(solution)/shard_map/ppermute | solution.py:135
  182.4 4.6 %collective-permute-start.13 = (bf16[4,128,256]{2,1,0:T(8,128)(2,1)S(1)}, bf16[4,128,256]{2,1,0:T(8,128)(2,1)S(1)}, u32[]{:S(2)}, u32[]{:S(2)}) collective-permute-start(bf16[4,128,256]{2,1,0:T(8,128)(2,1)S(1)} %collective-permute-done.12), channel_id=1, source_target_pairs={{0,64},{64,128},{128,192},{192,256},{256,320},{320,384},{384,448},... | collective-permute-start | bytes 786440 | tf_op jit(solution)/shard_map/ppermute | solution.py:135
  187.1 1.9 collective-permute-start.16
  189.0 1.9 collective-permute-done.13
  190.9 5.6 %collective-permute-start.14 = (bf16[4,128,256]{2,1,0:T(8,128)(2,1)S(1)}, bf16[4,128,256]{2,1,0:T(8,128)(2,1)S(1)}, u32[]{:S(2)}, u32[]{:S(2)}) collective-permute-start(bf16[4,128,256]{2,1,0:T(8,128)(2,1)S(1)} %collective-permute-done.13), channel_id=1, source_target_pairs={{0,64},{64,128},{128,192},{192,256},{256,320},{320,384},{384,448},... | collective-permute-start | bytes 786440 | tf_op jit(solution)/shard_map/ppermute | solution.py:135
  196.5 0.0 collective-permute-done.16
  196.6 1.9 collective-permute-start.17
  198.5 2.5 %collective-permute-done.14 = bf16[4,128,256]{2,1,0:T(8,128)(2,1)S(1)} collective-permute-done((bf16[4,128,256]{2,1,0:T(8,128)(2,1)S(1)}, bf16[4,128,256]{2,1,0:T(8,128)(2,1)S(1)}, u32[]{:S(2)}, u32[]{:S(2)}) %collective-permute-start.14) | collective-permute-done | bytes 262176 | tf_op jit(solution)/shard_map/ppermute | solution.py:135
  201.0 5.6 %collective-permute-start.15 = (bf16[4,128,256]{2,1,0:T(8,128)(2,1)S(1)}, bf16[4,128,256]{2,1,0:T(8,128)(2,1)S(1)}, u32[]{:S(2)}, u32[]{:S(2)}) collective-permute-start(bf16[4,128,256]{2,1,0:T(8,128)(2,1)S(1)} %collective-permute-done.14), channel_id=1, source_target_pairs={{0,64},{64,128},{128,192},{192,256},{256,320},{320,384},{384,448},... | collective-permute-start | bytes 786440 | tf_op jit(solution)/shard_map/ppermute | solution.py:135
  206.6 2.6 %multiply_reduce_fusion.past = f32[384,256]{1,0:T(8,128)} fusion(bf16[8,384,256]{2,1,0:T(8,128)(2,1)} %param.8, f32[8]{0:T(128)S(1)} %bitcast.55), kind=kLoop, calls=%fused_computation | loop fusion | flops 2260992 | bytes 1966112 | tf_op jit(solution)/shard_map/reduce_sum | solution.py:281
  209.2 1.9 collective-permute-start.18
  211.2 0.0 collective-permute-done.15
  211.4 7.3 %collective-permute-done.18 = bf16[4,128,256]{2,1,0:T(8,128)(2,1)S(1)} collective-permute-done((bf16[4,128,256]{2,1,0:T(8,128)(2,1)S(1)}, bf16[4,128,256]{2,1,0:T(8,128)(2,1)S(1)}, u32[]{:S(2)}, u32[]{:S(2)}) %collective-permute-start.18) | collective-permute-done | bytes 262176 | tf_op jit(solution)/shard_map/ppermute | solution.py:138
  218.7 0.0 all-gather.7.cloned.1.call-done
  218.8 1.3 copy-done.2
  220.1 5.0 %finish.1 = (bf16[384,256]{1,0:T(8,128)(2,1)}, bf16[384,256]{1,0:T(8,128)(2,1)}) custom-call(s32[1]{0:T(128)} %bitcast.y, f32[9]{0:T(128)} %dwa.1, bf16[16,384,256]{2,1,0:T(8,128)(2,1)} %bitcast.49, bf16[16,384,256]{2,1,0:T(8,128)(2,1)} %bitcast.50, bf16[8,4,128,256]{3,2,1,0:T(8,128)(2,1)} %copy-done.2, bf16[384,256]{1,0:T(8,128)(2,1)} %stream.1, ...), custom_call_target="tpu_custom_call" | custom-call | tf_op jit(solution)/shard_map/finish/pallas_call | solution.py:215
  (39 shorter events, 0.4 us)
Async XLA Ops:
  10.2 10.7 %copy-start.9 = (bf16[256,128]{1,0:T(8,128)(2,1)S(1)}, bf16[256,128]{1,0:T(8,128)(2,1)}, u32[]{:S(2)}) copy-start(bf16[256,128]{1,0:T(8,128)(2,1)} %param.11) | copy-start | bytes 196612
  10.3 22.0 %copy-start.4 = (bf16[384,256]{1,0:T(8,128)(2,1)S(1)}, bf16[384,256]{1,0:T(8,128)(2,1)}, u32[]{:S(2)}) copy-start(bf16[384,256]{1,0:T(8,128)(2,1)} %stream.1) | copy-start | bytes 589828
  10.3 50.2 %copy-start.1 = (s32[384]{0:T(512)S(1)}, s32[384]{0:T(512)}, u32[]{:S(2)}) copy-start(s32[384]{0:T(512)} %ids.1) | copy-start | bytes 4612
  10.3 50.2 %all-to-all-start = ((bf16[16,384,128]{2,1,0:T(8,128)(2,1)}), bf16[16,384,128]{2,1,0:T(8,128)(2,1)S(1)}, u32[]{:S(2)}, u32[]{:S(2)}) async-start(bf16[16,384,128]{2,1,0:T(8,128)(2,1)} %bitcast.51), calls=%async_computation | async-start | bytes 3145728 | tf_op jit(solution)/shard_map/all_to_all | solution.py:267
  20.8 138.3 %all-gather.5.cloned.1.call-start = ((), (), s32[]{:S(2)}) async-start(), calls=%async_computation.2 | async-start | bytes 2162688 | tf_op jit(solution)/shard_map/all_gather | solution.py:265
  21.0 15.3 %collective-permute-start.1 = (bf16[128,128]{1,0:T(8,128)(2,1)S(1)}, bf16[128,128]{1,0:T(8,128)(2,1)S(1)}, u32[]{:S(2)}, u32[]{:S(2)}) collective-permute-start(bf16[128,128]{1,0:T(8,128)(2,1)S(1)} %get-tuple-element.12), channel_id=1, source_target_pairs={{0,0},{1,32},{2,64},{3,96},{4,128},{5,160},{6,192},{7,224},{8,256}... | collective-permute-start | bytes 98312 | tf_op jit(solution)/shard_map/ppermute | solution.py:249
  26.3 12.7 %collective-permute-start.2 = (bf16[128,128]{1,0:T(8,128)(2,1)S(1)}, bf16[128,128]{1,0:T(8,128)(2,1)S(1)}, u32[]{:S(2)}, u32[]{:S(2)}) collective-permute-start(bf16[128,128]{1,0:T(8,128)(2,1)S(1)} %get-tuple-element.13), channel_id=1, source_target_pairs={{0,16},{1,48},{2,80},{3,112},{4,144},{5,176},{6,208},{7,240},{8,27... | collective-permute-start | bytes 98312 | tf_op jit(solution)/shard_map/ppermute | solution.py:249
  32.3 20.4 %collective-permute-start = (bf16[64,256]{1,0:T(8,128)(2,1)S(1)}, bf16[64,256]{1,0:T(8,128)(2,1)S(1)}, u32[]{:S(2)}, u32[]{:S(2)}) collective-permute-start(bf16[64,256]{1,0:T(8,128)(2,1)S(1)} %slice.19), channel_id=1, source_target_pairs={{16,0},{32,16},{48,32},{64,48},{80,64},{96,80},{112,96},{128,112},... | collective-permute-start | bytes 98312 | tf_op jit(solution)/shard_map/ppermute | solution.py:123
  62.8 10.9 %collective-permute-start.3 = (bf16[384,256]{1,0:T(8,128)(2,1)S(1)}, bf16[384,256]{1,0:T(8,128)(2,1)S(1)}, u32[]{:S(2)}, u32[]{:S(2)}) collective-permute-start(bf16[384,256]{1,0:T(8,128)(2,1)S(1)} %pad_maximum_fusion), channel_id=1, source_target_pairs={{0,2},{2,4},{4,6},{6,8},{8,10},{10,12},{12,14},{14,0},{1,3},{3,5},... | collective-permute-start | bytes 589832 | tf_op jit(solution)/shard_map/ppermute | solution.py:135
  73.7 10.0 %collective-permute-start.4 = (bf16[384,256]{1,0:T(8,128)(2,1)S(1)}, bf16[384,256]{1,0:T(8,128)(2,1)S(1)}, u32[]{:S(2)}, u32[]{:S(2)}) collective-permute-start(bf16[384,256]{1,0:T(8,128)(2,1)S(1)} %collective-permute-done.3), channel_id=1, source_target_pairs={{0,2},{2,4},{4,6},{6,8},{8,10},{10,12},{12,14},{14,0},{1,3},{3,5},... | collective-permute-start | bytes 589832 | tf_op jit(solution)/shard_map/ppermute | solution.py:135
  77.0 8.8 %collective-permute-start.7 = (bf16[384,256]{1,0:T(8,128)(2,1)S(1)}, bf16[384,256]{1,0:T(8,128)(2,1)S(1)}, u32[]{:S(2)}, u32[]{:S(2)}) collective-permute-start(bf16[384,256]{1,0:T(8,128)(2,1)S(1)} %pad_maximum_fusion), channel_id=1, source_target_pairs={{0,14},{2,0},{4,2},{6,4},{8,6},{10,8},{12,10},{14,12},{1,15},{3,1}... | collective-permute-start | bytes 589832 | tf_op jit(solution)/shard_map/ppermute | solution.py:138
  83.7 30.3 %copy-start.7 = (bf16[384,256]{1,0:T(8,128)(2,1)}, bf16[384,256]{1,0:T(8,128)(2,1)S(1)}, u32[]{:S(2)}) copy-start(bf16[384,256]{1,0:T(8,128)(2,1)S(1)} %collective-permute-done.4) | copy-start | bytes 589828
  83.7 9.2 %collective-permute-start.5 = (bf16[384,256]{1,0:T(8,128)(2,1)S(1)}, bf16[384,256]{1,0:T(8,128)(2,1)S(1)}, u32[]{:S(2)}, u32[]{:S(2)}) collective-permute-start(bf16[384,256]{1,0:T(8,128)(2,1)S(1)} %collective-permute-done.4), channel_id=1, source_target_pairs={{0,2},{2,4},{4,6},{6,8},{8,10},{10,12},{12,14},{14,0},{1,3},{3,5},... | collective-permute-start | bytes 589832 | tf_op jit(solution)/shard_map/ppermute | solution.py:135
  85.9 8.9 %copy-start.5 = (bf16[384,256]{1,0:T(8,128)(2,1)}, bf16[384,256]{1,0:T(8,128)(2,1)S(1)}, u32[]{:S(2)}) copy-start(bf16[384,256]{1,0:T(8,128)(2,1)S(1)} %collective-permute-done.7) | copy-start | bytes 589828
  85.9 22.8 %collective-permute-start.8 = (bf16[384,256]{1,0:T(8,128)(2,1)S(1)}, bf16[384,256]{1,0:T(8,128)(2,1)}, u32[]{:S(2)}, u32[]{:S(2)}) collective-permute-start(bf16[384,256]{1,0:T(8,128)(2,1)S(1)} %collective-permute-done.7), channel_id=1, source_target_pairs={{0,14},{2,0},{4,2},{6,4},{8,6},{10,8},{12,10},{14,12},{1,15},{3,1}... | collective-permute-start | bytes 589832 | tf_op jit(solution)/shard_map/ppermute | solution.py:138
  92.9 21.1 %copy-start.8 = (bf16[384,256]{1,0:T(8,128)(2,1)}, bf16[384,256]{1,0:T(8,128)(2,1)S(1)}, u32[]{:S(2)}) copy-start(bf16[384,256]{1,0:T(8,128)(2,1)S(1)} %collective-permute-done.5) | copy-start | bytes 589828
  92.9 21.1 %collective-permute-start.6 = (bf16[384,256]{1,0:T(8,128)(2,1)S(1)}, bf16[384,256]{1,0:T(8,128)(2,1)}, u32[]{:S(2)}, u32[]{:S(2)}) collective-permute-start(bf16[384,256]{1,0:T(8,128)(2,1)S(1)} %collective-permute-done.5), channel_id=1, source_target_pairs={{0,2},{2,4},{4,6},{6,8},{8,10},{10,12},{12,14},{14,0},{1,3},{3,5},... | collective-permute-start | bytes 589832 | tf_op jit(solution)/shard_map/ppermute | solution.py:135
  94.8 69.6 %all-to-all-start.1 = ((bf16[32,192,128]{2,1,0:T(8,128)(2,1)}), bf16[32,192,128]{2,1,0:T(8,128)(2,1)S(1)}, u32[]{:S(2)}, u32[]{:S(2)}) async-start(bf16[32,192,128]{2,1,0:T(8,128)(2,1)} %bitcast.16), calls=%async_computation.1 | async-start | bytes 3145728 | tf_op jit(solution)/shard_map/all_to_all | solution.py:277
  108.6 110.1 %all-gather.7.cloned.1.call-start = ((), (), s32[]{:S(2)}) async-start(), calls=%async_computation.3 | async-start | bytes 3342336 | tf_op jit(solution)/shard_map/all_gather | solution.py:289
  108.7 8.2 %copy-start.6 = (bf16[384,256]{1,0:T(8,128)(2,1)S(1)}, bf16[384,256]{1,0:T(8,128)(2,1)}, u32[]{:S(2)}) copy-start(bf16[384,256]{1,0:T(8,128)(2,1)} %copy-done.5) | copy-start | bytes 589828
  108.7 9.2 %collective-permute-start.9 = (bf16[384,256]{1,0:T(8,128)(2,1)}, bf16[384,256]{1,0:T(8,128)(2,1)S(1)}, u32[]{:S(2)}, u32[]{:S(2)}) collective-permute-start(bf16[384,256]{1,0:T(8,128)(2,1)} %collective-permute-done.8), channel_id=1, source_target_pairs={{0,14},{2,0},{4,2},{6,4},{8,6},{10,8},{12,10},{14,12},{1,15},{3,1}... | collective-permute-start | bytes 589832 | tf_op jit(solution)/shard_map/ppermute | solution.py:138
  117.9 41.2 %collective-permute-start.10 = (bf16[8,384,256]{2,1,0:T(8,128)(2,1)S(1)}, bf16[8,384,256]{2,1,0:T(8,128)(2,1)}, u32[]{:S(2)}, u32[]{:S(2)}) collective-permute-start(bf16[8,384,256]{2,1,0:T(8,128)(2,1)S(1)} %bitcast_dynamic-update-slice_fusion.8.mine), channel_id=1, source_target_pairs={{0,1},{1,0},{2,3},{3,2},{4,5},{5,4},{6,7},{7,6},{8,9},{9,8},{10,11... | collective-permute-start | bytes 4718600 | tf_op jit(solution)/shard_map/ppermute | solution.py:144
  159.1 1.6 copy-start
  165.3 8.8 %copy-start.3 = (bf16[4,128,256]{2,1,0:T(8,128)(2,1)S(1)}, bf16[4,128,256]{2,1,0:T(8,128)(2,1)}, u32[]{:S(2)}) copy-start(bf16[4,128,256]{2,1,0:T(8,128)(2,1)} %all_gather.16) | copy-start | bytes 786436
  165.3 41.3 %copy-start.10 = (f32[9]{0:T(128)S(1)}, f32[9]{0:T(128)}, u32[]{:S(2)}) copy-start(f32[9]{0:T(128)} %dwa.1) | copy-start | bytes 112
  165.4 8.0 %collective-permute-start.11 = (bf16[64,256]{1,0:T(8,128)(2,1)S(1)}, bf16[64,256]{1,0:T(8,128)(2,1)S(1)}, u32[]{:S(2)}, u32[]{:S(2)}) collective-permute-start(bf16[64,256]{1,0:T(8,128)(2,1)S(1)} %shard_map.86), channel_id=1, source_target_pairs={{0,16},{16,32},{32,48},{48,64},{64,80},{80,96},{96,112},{112,128},... | collective-permute-start | bytes 98312 | tf_op jit(solution)/shard_map/ppermute | solution.py:123
  174.2 8.3 %collective-permute-start.12 = (bf16[4,128,256]{2,1,0:T(8,128)(2,1)S(1)}, bf16[4,128,256]{2,1,0:T(8,128)(2,1)S(1)}, u32[]{:S(2)}, u32[]{:S(2)}) collective-permute-start(bf16[4,128,256]{2,1,0:T(8,128)(2,1)S(1)} %copy-done.3), channel_id=1, source_target_pairs={{0,64},{64,128},{128,192},{192,256},{256,320},{320,384},{384,448},... | collective-permute-start | bytes 786440 | tf_op jit(solution)/shard_map/ppermute | solution.py:135
  182.4 8.5 %collective-permute-start.13 = (bf16[4,128,256]{2,1,0:T(8,128)(2,1)S(1)}, bf16[4,128,256]{2,1,0:T(8,128)(2,1)S(1)}, u32[]{:S(2)}, u32[]{:S(2)}) collective-permute-start(bf16[4,128,256]{2,1,0:T(8,128)(2,1)S(1)} %collective-permute-done.12), channel_id=1, source_target_pairs={{0,64},{64,128},{128,192},{192,256},{256,320},{320,384},{384,448},... | collective-permute-start | bytes 786440 | tf_op jit(solution)/shard_map/ppermute | solution.py:135
  187.1 9.5 %collective-permute-start.16 = (bf16[4,128,256]{2,1,0:T(8,128)(2,1)S(1)}, bf16[4,128,256]{2,1,0:T(8,128)(2,1)S(1)}, u32[]{:S(2)}, u32[]{:S(2)}) collective-permute-start(bf16[4,128,256]{2,1,0:T(8,128)(2,1)S(1)} %copy-done.3), channel_id=1, source_target_pairs={{0,448},{64,0},{128,64},{192,128},{256,192},{320,256},{384,320},{4... | collective-permute-start | bytes 786440 | tf_op jit(solution)/shard_map/ppermute | solution.py:138
  190.9 10.1 %collective-permute-start.14 = (bf16[4,128,256]{2,1,0:T(8,128)(2,1)S(1)}, bf16[4,128,256]{2,1,0:T(8,128)(2,1)S(1)}, u32[]{:S(2)}, u32[]{:S(2)}) collective-permute-start(bf16[4,128,256]{2,1,0:T(8,128)(2,1)S(1)} %collective-permute-done.13), channel_id=1, source_target_pairs={{0,64},{64,128},{128,192},{192,256},{256,320},{320,384},{384,448},... | collective-permute-start | bytes 786440 | tf_op jit(solution)/shard_map/ppermute | solution.py:135
  196.6 12.7 %collective-permute-start.17 = (bf16[4,128,256]{2,1,0:T(8,128)(2,1)S(1)}, bf16[4,128,256]{2,1,0:T(8,128)(2,1)S(1)}, u32[]{:S(2)}, u32[]{:S(2)}) collective-permute-start(bf16[4,128,256]{2,1,0:T(8,128)(2,1)S(1)} %collective-permute-done.16), channel_id=1, source_target_pairs={{0,448},{64,0},{128,64},{192,128},{256,192},{320,256},{384,320},{4... | collective-permute-start | bytes 786440 | tf_op jit(solution)/shard_map/ppermute | solution.py:138
  201.0 10.1 %collective-permute-start.15 = (bf16[4,128,256]{2,1,0:T(8,128)(2,1)S(1)}, bf16[4,128,256]{2,1,0:T(8,128)(2,1)S(1)}, u32[]{:S(2)}, u32[]{:S(2)}) collective-permute-start(bf16[4,128,256]{2,1,0:T(8,128)(2,1)S(1)} %collective-permute-done.14), channel_id=1, source_target_pairs={{0,64},{64,128},{128,192},{192,256},{256,320},{320,384},{384,448},... | collective-permute-start | bytes 786440 | tf_op jit(solution)/shard_map/ppermute | solution.py:135
  209.2 9.5 %collective-permute-start.18 = (bf16[4,128,256]{2,1,0:T(8,128)(2,1)S(1)}, bf16[4,128,256]{2,1,0:T(8,128)(2,1)S(1)}, u32[]{:S(2)}, u32[]{:S(2)}) collective-permute-start(bf16[4,128,256]{2,1,0:T(8,128)(2,1)S(1)} %collective-permute-done.17), channel_id=1, source_target_pairs={{0,448},{64,0},{128,64},{192,128},{256,192},{320,256},{384,320},{4... | collective-permute-start | bytes 786440 | tf_op jit(solution)/shard_map/ppermute | solution.py:138
  218.7 1.3 copy-start.2
Sparse Core Ops, SparseCore 0:
  67.5 91.5 all-gather.4
  174.3 39.8 all-gather.6

commit v6 on v5

--- a/solution.py
+++ b/solution.py
@@ -144,32 +144,36 @@
     return lax.ppermute(block, "core", [(0, 1), (1, 0)])
 
 
-def project_kernel(place, mine, other, weights, out):
-    steps, _, depth = mine.shape
-    z, core = place[0], place[1]
-
-    def body(i, total):
-        at = lax.rem(z + i + steps - steps // 2, steps) * 2
-        w_mine = weights[pl.ds((at + core) * 2, 2)].reshape(depth, -1)
-        w_other = weights[pl.ds((at + 1 - core) * 2, 2)].reshape(depth, -1)
-        total += jnp.dot(mine[i], w_mine, preferred_element_type=jnp.float32)
-        total += jnp.dot(other[i], w_other, preferred_element_type=jnp.float32)
-        return total
-
-    total = lax.fori_loop(0, steps, body, jnp.zeros(out.shape, jnp.float32))
-    out[...] = total.astype(out.dtype)
-
-
-def project(place, mine, other, weights):
-    rows, width = mine.shape[1], weights.shape[2]
-    return pl.pallas_call(
-        project_kernel,
-        out_shape=jax.ShapeDtypeStruct((rows, width), jnp.bfloat16),
-        in_specs=[pl.BlockSpec(memory_space=pltpu.SMEM)] + [vmem_space()] * 3,
+def project_kernel(swapped, place, blocks, weights, *rest):
+    out = rest[-1]
+    steps, rows, depth = blocks.shape
+    which = place[1] if not swapped else 1 - place[1]
+    for row in range(0, rows, BAND):
+        band = slice(row, row + BAND)
+
+        def body(i, total):
+            at = lax.rem(place[0] + i + steps - steps // 2, steps) * 2 + which
+            matching = weights[pl.ds(at * 2, 2)].reshape(depth, -1)
+            return total + jnp.dot(
+                blocks[i, band, :], matching, preferred_element_type=jnp.float32
+            )
+
+        total = rest[0][band, :] if swapped else jnp.zeros((BAND, out.shape[1]), jnp.float32)
+        out[band, :] = lax.fori_loop(0, steps, body, total, unroll=True).astype(out.dtype)
+
+
+def project(place, blocks, weights, so_far=None):
+    rows, width = blocks.shape[1], weights.shape[2]
+    swapped = so_far is not None
+    terms = (place, blocks, weights) + ((so_far,) if swapped else ())
+    return pl.pallas_call(
+        functools.partial(project_kernel, swapped),
+        out_shape=jax.ShapeDtypeStruct((rows, width), jnp.bfloat16 if swapped else jnp.float32),
+        in_specs=[pl.BlockSpec(memory_space=pltpu.SMEM)] + [vmem_space()] * (len(terms) - 1),
         out_specs=vmem_space(),
         compiler_params=ROOM,
-        name="project",
-    )(place, mine, other, weights)
+        name="project_other" if swapped else "project_own",
+    )(*terms)
 
 
 BAND = 128
@@ -273,19 +277,20 @@
     turned = lax.all_gather(turned, "x", axis=0)
 
     picked = pick(neighbour_ids, store.reshape(-1, local_heads * slab_rows, HDIM))
-    own_spans, turned, picked = lax.optimization_barrier((own_spans, turned, picked))
+    turned, picked = lax.optimization_barrier((turned, picked))
     arrived = lax.all_to_all(
         picked.reshape(ctx_count, -1, HDIM), CTX, split_axis=0, concat_axis=0, tiled=True
     ).reshape(ctx_count, slots, local_heads, slab_rows, HDIM)
     mine = around(own_spans, "z")
     past = jnp.sum(history.astype(jnp.float32) * dwa_weights[:-1, None, None], axis=0)
-    queries = project(place, mine, partner(mine), w_in)
+    other = partner(mine)
+    queries = project(place, mine, w_in)
+    queries = project(place, other, w_in, queries)
     spans = tok_rows // SPAN
     last = attend(queries, arrived, spans - 1, 1)
     before = shifted(last, 1)
     rest = attend(queries, arrived, 0, spans - 1)
     attended = jnp.concatenate([before[1:], rest, last[:1]], 0)
-    attended, turned = lax.optimization_barrier((attended, turned))
     everyone = lax.all_gather(attended, DB, axis=0)
     columns = around(turned, "y")
     return finish(y, dwa_weights, everyone, columns, stream, past)

time: 233 us -> 234 us (level)
  waiting for transfers between devices: 78.5 us -> 83 us
  starting transfers between devices: 95.4 us -> 92.6 us
    all_gather x1, waiting for transfers between devices: 39.2 us -> 0.01 us  [on_device(): w_in = lax.all_gather(w_query, CTX, axis=0)]
    all_to_all x1, waiting for transfers between devices: 0.01 us -> 26.3 us  [on_device(): lax.all_to_all(picked.reshape(ctx_count, -1, HDIM), CTX, split_axis=0, co...]
    ppermute x8, waiting for transfers between devices: 20.6 us -> 46 us  [around(): right = lax.ppermute(right, axis, ring(count, 1))]
    all_to_all x1, waiting for transfers between devices: 7.71 us -> 0.01 us  [on_device(): lax.all_to_all(by_head.reshape(db_count, -1, HDIM), DB, split_axis=0, con...]
    all_to_all x1, starting transfers between devices: 13.8 us -> 7.02 us  [on_device(): lax.all_to_all(picked.reshape(ctx_count, -1, HDIM), CTX, split_axis=0, co...]
    ppermute x6, starting transfers between devices: 19.6 us -> 25.3 us  [around(): left = lax.ppermute(left, axis, ring(count, -1))]
    ppermute x2, waiting for transfers between devices: 2.71 us -> 0.01 us  [columns_here(): pieces.append(lax.ppermute(send, CTX + DB, route))]
    ppermute x2, waiting for transfers between devices: 0.78 us -> 3.27 us  [shifted(): return lax.ppermute(block, CTX, route)]
  transfers between devices with their start and end apart: 23 -> 23, of which waited for: 11 -> 12; matrix products, arithmetic and copies ran while one was open for 3% -> 2% of each run, Pallas kernels for 3% -> 4%
where the time goes in v6:
time: 234 us; the launch traced here: 232 us
  starting transfers between devices  92.6 us (40%)
  waiting for transfers between devices  83 us (35%)
  Pallas kernels  18.7 us (8%)
  between operations  14.7 us (6%)
  blocking collectives  14.5 us (6%)
  local copies, waits for them, and re-layouts  7.01 us (3%)
    ppermute x8, waiting for transfers between devices, around(): right = lax.ppermute(right, axis, ring(count, 1))  46 us
    ppermute x8, starting transfers between devices, around(): right = lax.ppermute(right, axis, ring(count, 1))  29.7 us
    all_to_all x1, waiting for transfers between devices, on_device(): lax.all_to_all(picked.reshape(ctx_count, -1, HDIM), CTX, split_axis=0, co...  26.3 us
    ppermute x6, starting transfers between devices, around(): left = lax.ppermute(left, axis, ring(count, -1))  25.3 us
    all_gather x1, blocking collectives, on_device(): turned = lax.all_gather(turned, 'x', axis=0)  14.5 us
    ppermute x2, starting transfers between devices, columns_here(): pieces.append(lax.ppermute(send, CTX + DB, route))  11.4 us
    all_to_all x1, starting transfers between devices, on_device(): lax.all_to_all(by_head.reshape(db_count, -1, HDIM), DB, split_axis=0, con...  10.6 us
    all_to_all x1, starting transfers between devices, on_device(): lax.all_to_all(picked.reshape(ctx_count, -1, HDIM), CTX, split_axis=0, co...  7.02 us
  transfers between devices with their start and end apart: 23, of which 12 were waited for; matrix products, arithmetic and copies ran while one was open for 2% of the time, Pallas kernels for 4%

profile of v6, /device:TPU:24, one launch (start us, length us, event | category | flops | bytes accessed | tf_op | source)
XLA Modules:
  0.0 232.4 jit_solution(3856889838616243932)
XLA Ops:
  7.2 3.0 %split_heads.1 = bf16[16,24,2,4,2,128]{5,4,3,2,1,0:T(2,128)(2,1)} custom-call(bf16[1,24,4,2,4096]{4,3,2,1,0:T(2,128)(2,1)} %source.1), custom_call_target="tpu_custom_call" | custom-call | tf_op jit(solution)/shard_map/split_heads/pallas_call | solution.py:45
  10.2 0.0 copy-start.6
  10.2 0.0 copy-start.11
  10.2 10.6 %all-to-all-start = ((bf16[16,384,128]{2,1,0:T(8,128)(2,1)}), bf16[16,384,128]{2,1,0:T(8,128)(2,1)S(1)}, u32[]{:S(2)}, u32[]{:S(2)}) async-start(bf16[16,384,128]{2,1,0:T(8,128)(2,1)} %bitcast.52), calls=%async_computation | async-start | bytes 3145728 | tf_op jit(solution)/shard_map/all_to_all | solution.py:271
  20.8 0.0 copy-start.2
  20.8 0.0 all-gather.5.cloned.1.call-start
  20.9 4.6 %collective-permute-start = (bf16[64,256]{1,0:T(8,128)(2,1)S(1)}, bf16[64,256]{1,0:T(8,128)(2,1)S(1)}, u32[]{:S(2)}, u32[]{:S(2)}) collective-permute-start(bf16[64,256]{1,0:T(8,128)(2,1)S(1)} %slice.19), channel_id=1, source_target_pairs={{16,0},{32,16},{48,32},{64,48},{80,64},{96,80},{112,96},{128,112},... | collective-permute-start | bytes 98312 | tf_op jit(solution)/shard_map/ppermute | solution.py:123
  25.5 1.5 collective-permute-done
  27.0 3.8 %collective-permute-start.1 = (bf16[384,256]{1,0:T(8,128)(2,1)S(1)}, bf16[384,256]{1,0:T(8,128)(2,1)S(1)}, u32[]{:S(2)}, u32[]{:S(2)}) collective-permute-start(bf16[384,256]{1,0:T(8,128)(2,1)S(1)} %pad_maximum_fusion), channel_id=1, source_target_pairs={{0,2},{2,4},{4,6},{6,8},{8,10},{10,12},{12,14},{14,0},{1,3},{3,5},... | collective-permute-start | bytes 589832 | tf_op jit(solution)/shard_map/ppermute | solution.py:135
  30.9 0.0 all-gather.5.cloned.1.call-update
  30.9 32.2 %collective-permute-done.1 = bf16[384,256]{1,0:T(8,128)(2,1)S(1)} collective-permute-done((bf16[384,256]{1,0:T(8,128)(2,1)S(1)}, bf16[384,256]{1,0:T(8,128)(2,1)S(1)}, u32[]{:S(2)}, u32[]{:S(2)}) %collective-permute-start.1) | collective-permute-done | bytes 196640 | tf_op jit(solution)/shard_map/ppermute | solution.py:135
  63.1 1.9 collective-permute-start.2
  65.0 5.1 %collective-permute-start.5 = (bf16[384,256]{1,0:T(8,128)(2,1)S(1)}, bf16[384,256]{1,0:T(8,128)(2,1)S(1)}, u32[]{:S(2)}, u32[]{:S(2)}) collective-permute-start(bf16[384,256]{1,0:T(8,128)(2,1)S(1)} %pad_maximum_fusion), channel_id=1, source_target_pairs={{0,14},{2,0},{4,2},{6,4},{8,6},{10,8},{12,10},{14,12},{1,15},{3,1}... | collective-permute-start | bytes 589832 | tf_op jit(solution)/shard_map/ppermute | solution.py:138
  70.2 2.4 %collective-permute-done.2 = bf16[384,256]{1,0:T(8,128)(2,1)S(1)} collective-permute-done((bf16[384,256]{1,0:T(8,128)(2,1)S(1)}, bf16[384,256]{1,0:T(8,128)(2,1)S(1)}, u32[]{:S(2)}, u32[]{:S(2)}) %collective-permute-start.2) | collective-permute-done | bytes 196640 | tf_op jit(solution)/shard_map/ppermute | solution.py:135
  72.6 1.9 collective-permute-start.3
  74.5 6.7 %collective-permute-start.10 = (bf16[128,128]{1,0:T(8,128)(2,1)S(1)}, bf16[128,128]{1,0:T(8,128)(2,1)S(1)}, u32[]{:S(2)}, u32[]{:S(2)}) collective-permute-start(bf16[128,128]{1,0:T(8,128)(2,1)S(1)} %get-tuple-element.7), channel_id=1, source_target_pairs={{0,16},{1,48},{2,80},{3,112},{4,144},{5,176},{6,208},{7,240},{8,27... | collective-permute-start | bytes 98312 | tf_op jit(solution)/shard_map/ppermute | solution.py:253
  81.3 4.6 %collective-permute-start.9 = (bf16[128,128]{1,0:T(8,128)(2,1)S(1)}, bf16[128,128]{1,0:T(8,128)(2,1)S(1)}, u32[]{:S(2)}, u32[]{:S(2)}) collective-permute-start(bf16[128,128]{1,0:T(8,128)(2,1)S(1)} %get-tuple-element.6), channel_id=1, source_target_pairs={{0,0},{1,32},{2,64},{3,96},{4,128},{5,160},{6,192},{7,224},{8,256}... | collective-permute-start | bytes 98312 | tf_op jit(solution)/shard_map/ppermute | solution.py:253
  85.9 0.0 collective-permute-done.5
  85.9 9.4 %collective-permute-start.6 = (bf16[384,256]{1,0:T(8,128)(2,1)S(1)}, bf16[384,256]{1,0:T(8,128)(2,1)}, u32[]{:S(2)}, u32[]{:S(2)}) collective-permute-start(bf16[384,256]{1,0:T(8,128)(2,1)S(1)} %collective-permute-done.5), channel_id=1, source_target_pairs={{0,14},{2,0},{4,2},{6,4},{8,6},{10,8},{12,10},{14,12},{1,15},{3,1}... | collective-permute-start | bytes 589832 | tf_op jit(solution)/shard_map/ppermute | solution.py:138
  95.3 0.0 collective-permute-done.3
  95.3 0.0 copy-start.10
  95.3 1.9 collective-permute-start.4
  97.3 0.0 collective-permute-done.9
  97.3 14.5 %all_gather.18 = bf16[4,128,256]{2,1,0:T(8,128)(2,1)} all-gather(bf16[1,128,256]{2,1,0:T(8,128)(2,1)S(1)} %maximum_select_fusion), channel_id=1, replica_groups=mesh['y'=8,'x'=4,'z'=8,'core'=2] {'x'}, dimensions={0}, use_global_device_ids=true | all-gather | bytes 327680 | tf_op jit(solution)/shard_map/all_gather | solution.py:277
  111.8 5.1 %collective-permute-start.7 = (bf16[384,256]{1,0:T(8,128)(2,1)}, bf16[384,256]{1,0:T(8,128)(2,1)}, u32[]{:S(2)}, u32[]{:S(2)}) collective-permute-start(bf16[384,256]{1,0:T(8,128)(2,1)} %collective-permute-done.6), channel_id=1, source_target_pairs={{0,14},{2,0},{4,2},{6,4},{8,6},{10,8},{12,10},{14,12},{1,15},{3,1}... | collective-permute-start | bytes 589832 | tf_op jit(solution)/shard_map/ppermute | solution.py:138
  117.0 2.4 %pick.1 = bf16[384,16,128]{2,1,0:T(8,128)(2,1)} custom-call(s32[384]{0:T(512)S(1)} %copy-done.2, bf16[384,16,128]{2,1,0:T(8,128)(2,1)S(1)} %bitcast.49), custom_call_target="tpu_custom_call" | custom-call | tf_op jit(solution)/shard_map/pick/pallas_call | solution.py:68
  119.4 7.0 %all-to-all-start.1 = ((bf16[32,192,128]{2,1,0:T(8,128)(2,1)}), bf16[32,192,128]{2,1,0:T(8,128)(2,1)S(1)}, u32[]{:S(2)}, u32[]{:S(2)}) async-start(bf16[32,192,128]{2,1,0:T(8,128)(2,1)} %bitcast.16), calls=%async_computation.1 | async-start | bytes 3145728 | tf_op jit(solution)/shard_map/all_to_all | solution.py:281
  126.4 0.0 all-gather.7.cloned.1.call-start
  126.5 1.0 bitcast_dynamic-update-slice_fusion.14
  127.5 0.9 bitcast_dynamic-update-slice_fusion.13
  128.5 0.9 bitcast_dynamic-update-slice_fusion.9
  129.4 0.0 collective-permute-done.7
  129.4 0.9 bitcast_dynamic-update-slice_fusion.8.blocks
  130.4 1.9 collective-permute-start.8
  132.3 0.1 pad_add_fusion.place
  132.4 1.6 copy-done
  134.0 1.1 project_own.1.rest_0_
  135.1 0.7 collective-permute-done.8.blocks
  135.8 2.0 project_other.1.q_ref
  137.8 26.3 %all-to-all-done.1 = bf16[32,192,128]{2,1,0:T(8,128)(2,1)S(1)} async-done(((bf16[32,192,128]{2,1,0:T(8,128)(2,1)}), bf16[32,192,128]{2,1,0:T(8,128)(2,1)S(1)}, u32[]{:S(2)}, u32[]{:S(2)}) %all-to-all-start.1) | async-done | bytes 1572896 | tf_op jit(solution)/shard_map/all_to_all | solution.py:281
  164.1 1.0 shard_map.86
  165.1 0.0 copy-start.12
  165.1 2.1 collective-permute-start.11
  167.2 4.2 %shard_map.87 = bf16[320,256]{1,0:T(8,128)(2,1)S(1)} custom-call(bf16[384,256]{1,0:T(8,128)(2,1)S(1)} %project_other.1.q_ref, bf16[32,12,2,8,128]{4,3,2,1,0:T(8,128)(2,1)S(1)} %bitcast.46), custom_call_target="tpu_custom_call" | custom-call | tf_op jit(solution)/shard_map/pallas_call | solution.py:111
  171.4 1.7 collective-permute-done.11
  173.1 0.7 pad_maximum_fusion.1
  173.9 0.0 all-gather.7.cloned.1.call-update
  173.9 4.0 %collective-permute-start.12 = (bf16[4,128,256]{2,1,0:T(8,128)(2,1)}, bf16[4,128,256]{2,1,0:T(8,128)(2,1)S(1)}, u32[]{:S(2)}, u32[]{:S(2)}) collective-permute-start(bf16[4,128,256]{2,1,0:T(8,128)(2,1)} %all_gather.18), channel_id=1, source_target_pairs={{0,64},{64,128},{128,192},{192,256},{256,320},{320,384},{384,448},... | collective-permute-start | bytes 786440 | tf_op jit(solution)/shard_map/ppermute | solution.py:135
  177.9 4.7 %collective-permute-done.12 = bf16[4,128,256]{2,1,0:T(8,128)(2,1)S(1)} collective-permute-done((bf16[4,128,256]{2,1,0:T(8,128)(2,1)}, bf16[4,128,256]{2,1,0:T(8,128)(2,1)S(1)}, u32[]{:S(2)}, u32[]{:S(2)}) %collective-permute-start.12) | collective-permute-done | bytes 262176 | tf_op jit(solution)/shard_map/ppermute | solution.py:135
  182.5 5.0 %collective-permute-start.13 = (bf16[4,128,256]{2,1,0:T(8,128)(2,1)S(1)}, bf16[4,128,256]{2,1,0:T(8,128)(2,1)S(1)}, u32[]{:S(2)}, u32[]{:S(2)}) collective-permute-start(bf16[4,128,256]{2,1,0:T(8,128)(2,1)S(1)} %collective-permute-done.12), channel_id=1, source_target_pairs={{0,64},{64,128},{128,192},{192,256},{256,320},{320,384},{384,448},... | collective-permute-start | bytes 786440 | tf_op jit(solution)/shard_map/ppermute | solution.py:135
  187.5 1.9 collective-permute-start.16
  189.5 2.6 %collective-permute-done.13 = bf16[4,128,256]{2,1,0:T(8,128)(2,1)S(1)} collective-permute-done((bf16[4,128,256]{2,1,0:T(8,128)(2,1)S(1)}, bf16[4,128,256]{2,1,0:T(8,128)(2,1)S(1)}, u32[]{:S(2)}, u32[]{:S(2)}) %collective-permute-start.13) | collective-permute-done | bytes 262176 | tf_op jit(solution)/shard_map/ppermute | solution.py:135
  192.1 5.6 %collective-permute-start.14 = (bf16[4,128,256]{2,1,0:T(8,128)(2,1)S(1)}, bf16[4,128,256]{2,1,0:T(8,128)(2,1)S(1)}, u32[]{:S(2)}, u32[]{:S(2)}) collective-permute-start(bf16[4,128,256]{2,1,0:T(8,128)(2,1)S(1)} %collective-permute-done.13), channel_id=1, source_target_pairs={{0,64},{64,128},{128,192},{192,256},{256,320},{320,384},{384,448},... | collective-permute-start | bytes 786440 | tf_op jit(solution)/shard_map/ppermute | solution.py:135
  197.7 0.1 collective-permute-done.16
  197.8 1.9 collective-permute-start.17
  199.7 3.3 %collective-permute-done.14 = bf16[4,128,256]{2,1,0:T(8,128)(2,1)S(1)} collective-permute-done((bf16[4,128,256]{2,1,0:T(8,128)(2,1)S(1)}, bf16[4,128,256]{2,1,0:T(8,128)(2,1)S(1)}, u32[]{:S(2)}, u32[]{:S(2)}) %collective-permute-start.14) | collective-permute-done | bytes 262176 | tf_op jit(solution)/shard_map/ppermute | solution.py:135
  203.0 5.6 %collective-permute-start.15 = (bf16[4,128,256]{2,1,0:T(8,128)(2,1)S(1)}, bf16[4,128,256]{2,1,0:T(8,128)(2,1)S(1)}, u32[]{:S(2)}, u32[]{:S(2)}) collective-permute-start(bf16[4,128,256]{2,1,0:T(8,128)(2,1)S(1)} %collective-permute-done.14), channel_id=1, source_target_pairs={{0,64},{64,128},{128,192},{192,256},{256,320},{320,384},{384,448},... | collective-permute-start | bytes 786440 | tf_op jit(solution)/shard_map/ppermute | solution.py:135
  208.6 1.1 multiply_reduce_fusion.past
  209.8 1.9 collective-permute-start.18
  211.7 0.8 collective-permute-done.15
  212.7 6.6 %collective-permute-done.18 = bf16[4,128,256]{2,1,0:T(8,128)(2,1)S(1)} collective-permute-done((bf16[4,128,256]{2,1,0:T(8,128)(2,1)S(1)}, bf16[4,128,256]{2,1,0:T(8,128)(2,1)S(1)}, u32[]{:S(2)}, u32[]{:S(2)}) %collective-permute-start.18) | collective-permute-done | bytes 262176 | tf_op jit(solution)/shard_map/ppermute | solution.py:138
  219.3 0.0 all-gather.7.cloned.1.call-done
  219.3 1.3 copy-done.3
  220.6 5.0 %finish.1 = (bf16[384,256]{1,0:T(8,128)(2,1)}, bf16[384,256]{1,0:T(8,128)(2,1)}) custom-call(s32[1]{0:T(128)} %bitcast.y, f32[9]{0:T(128)} %dwa.1, bf16[16,384,256]{2,1,0:T(8,128)(2,1)} %bitcast.50, bf16[16,384,256]{2,1,0:T(8,128)(2,1)} %bitcast.51, bf16[8,4,128,256]{3,2,1,0:T(8,128)(2,1)} %copy-done.3, bf16[384,256]{1,0:T(8,128)(2,1)} %stream.1, ...), custom_call_target="tpu_custom_call" | custom-call | tf_op jit(solution)/shard_map/finish/pallas_call | solution.py:219
  (44 shorter events, 0.4 us)
Async XLA Ops:
  10.2 10.7 %copy-start.6 = (bf16[384,256]{1,0:T(8,128)(2,1)S(1)}, bf16[384,256]{1,0:T(8,128)(2,1)}, u32[]{:S(2)}) copy-start(bf16[384,256]{1,0:T(8,128)(2,1)} %stream.1) | copy-start | bytes 589828
  10.2 64.3 %copy-start.11 = (bf16[256,128]{1,0:T(8,128)(2,1)S(1)}, bf16[256,128]{1,0:T(8,128)(2,1)}, u32[]{:S(2)}) copy-start(bf16[256,128]{1,0:T(8,128)(2,1)} %param.11) | copy-start | bytes 196612
  10.2 106.8 %all-to-all-start = ((bf16[16,384,128]{2,1,0:T(8,128)(2,1)}), bf16[16,384,128]{2,1,0:T(8,128)(2,1)S(1)}, u32[]{:S(2)}, u32[]{:S(2)}) async-start(bf16[16,384,128]{2,1,0:T(8,128)(2,1)} %bitcast.52), calls=%async_computation | async-start | bytes 3145728 | tf_op jit(solution)/shard_map/all_to_all | solution.py:271
  20.8 96.2 %copy-start.2 = (s32[384]{0:T(512)S(1)}, s32[384]{0:T(512)}, u32[]{:S(2)}) copy-start(s32[384]{0:T(512)} %ids.1) | copy-start | bytes 4612
  20.8 111.6 %all-gather.5.cloned.1.call-start = ((), (), s32[]{:S(2)}) async-start(), calls=%async_computation.2 | async-start | bytes 2162688 | tf_op jit(solution)/shard_map/all_gather | solution.py:269
  20.9 6.1 %collective-permute-start = (bf16[64,256]{1,0:T(8,128)(2,1)S(1)}, bf16[64,256]{1,0:T(8,128)(2,1)S(1)}, u32[]{:S(2)}, u32[]{:S(2)}) collective-permute-start(bf16[64,256]{1,0:T(8,128)(2,1)S(1)} %slice.19), channel_id=1, source_target_pairs={{16,0},{32,16},{48,32},{64,48},{80,64},{96,80},{112,96},{128,112},... | collective-permute-start | bytes 98312 | tf_op jit(solution)/shard_map/ppermute | solution.py:123
  27.0 36.1 %collective-permute-start.1 = (bf16[384,256]{1,0:T(8,128)(2,1)S(1)}, bf16[384,256]{1,0:T(8,128)(2,1)S(1)}, u32[]{:S(2)}, u32[]{:S(2)}) collective-permute-start(bf16[384,256]{1,0:T(8,128)(2,1)S(1)} %pad_maximum_fusion), channel_id=1, source_target_pairs={{0,2},{2,4},{4,6},{6,8},{8,10},{10,12},{12,14},{14,0},{1,3},{3,5},... | collective-permute-start | bytes 589832 | tf_op jit(solution)/shard_map/ppermute | solution.py:135
  63.1 9.5 %collective-permute-start.2 = (bf16[384,256]{1,0:T(8,128)(2,1)S(1)}, bf16[384,256]{1,0:T(8,128)(2,1)S(1)}, u32[]{:S(2)}, u32[]{:S(2)}) collective-permute-start(bf16[384,256]{1,0:T(8,128)(2,1)S(1)} %collective-permute-done.1), channel_id=1, source_target_pairs={{0,2},{2,4},{4,6},{6,8},{8,10},{10,12},{12,14},{14,0},{1,3},{3,5},... | collective-permute-start | bytes 589832 | tf_op jit(solution)/shard_map/ppermute | solution.py:135
  65.0 20.9 %collective-permute-start.5 = (bf16[384,256]{1,0:T(8,128)(2,1)S(1)}, bf16[384,256]{1,0:T(8,128)(2,1)S(1)}, u32[]{:S(2)}, u32[]{:S(2)}) collective-permute-start(bf16[384,256]{1,0:T(8,128)(2,1)S(1)} %pad_maximum_fusion), channel_id=1, source_target_pairs={{0,14},{2,0},{4,2},{6,4},{8,6},{10,8},{12,10},{14,12},{1,15},{3,1}... | collective-permute-start | bytes 589832 | tf_op jit(solution)/shard_map/ppermute | solution.py:138
  72.5 44.4 %copy-start.9 = (bf16[384,256]{1,0:T(8,128)(2,1)}, bf16[384,256]{1,0:T(8,128)(2,1)S(1)}, u32[]{:S(2)}) copy-start(bf16[384,256]{1,0:T(8,128)(2,1)S(1)} %collective-permute-done.2) | copy-start | bytes 589828
  72.6 22.7 %collective-permute-start.3 = (bf16[384,256]{1,0:T(8,128)(2,1)S(1)}, bf16[384,256]{1,0:T(8,128)(2,1)S(1)}, u32[]{:S(2)}, u32[]{:S(2)}) collective-permute-start(bf16[384,256]{1,0:T(8,128)(2,1)S(1)} %collective-permute-done.2), channel_id=1, source_target_pairs={{0,2},{2,4},{4,6},{6,8},{8,10},{10,12},{12,14},{14,0},{1,3},{3,5},... | collective-permute-start | bytes 589832 | tf_op jit(solution)/shard_map/ppermute | solution.py:135
  74.5 22.7 %collective-permute-start.10 = (bf16[128,128]{1,0:T(8,128)(2,1)S(1)}, bf16[128,128]{1,0:T(8,128)(2,1)S(1)}, u32[]{:S(2)}, u32[]{:S(2)}) collective-permute-start(bf16[128,128]{1,0:T(8,128)(2,1)S(1)} %get-tuple-element.7), channel_id=1, source_target_pairs={{0,16},{1,48},{2,80},{3,112},{4,144},{5,176},{6,208},{7,240},{8,27... | collective-permute-start | bytes 98312 | tf_op jit(solution)/shard_map/ppermute | solution.py:253
  81.3 16.0 %collective-permute-start.9 = (bf16[128,128]{1,0:T(8,128)(2,1)S(1)}, bf16[128,128]{1,0:T(8,128)(2,1)S(1)}, u32[]{:S(2)}, u32[]{:S(2)}) collective-permute-start(bf16[128,128]{1,0:T(8,128)(2,1)S(1)} %get-tuple-element.6), channel_id=1, source_target_pairs={{0,0},{1,32},{2,64},{3,96},{4,128},{5,160},{6,192},{7,224},{8,256}... | collective-permute-start | bytes 98312 | tf_op jit(solution)/shard_map/ppermute | solution.py:253
  85.9 31.0 %copy-start.7 = (bf16[384,256]{1,0:T(8,128)(2,1)}, bf16[384,256]{1,0:T(8,128)(2,1)S(1)}, u32[]{:S(2)}) copy-start(bf16[384,256]{1,0:T(8,128)(2,1)S(1)} %collective-permute-done.5) | copy-start | bytes 589828
  85.9 25.9 %collective-permute-start.6 = (bf16[384,256]{1,0:T(8,128)(2,1)S(1)}, bf16[384,256]{1,0:T(8,128)(2,1)}, u32[]{:S(2)}, u32[]{:S(2)}) collective-permute-start(bf16[384,256]{1,0:T(8,128)(2,1)S(1)} %collective-permute-done.5), channel_id=1, source_target_pairs={{0,14},{2,0},{4,2},{6,4},{8,6},{10,8},{12,10},{14,12},{1,15},{3,1}... | collective-permute-start | bytes 589832 | tf_op jit(solution)/shard_map/ppermute | solution.py:138
  95.3 21.7 %copy-start.10 = (bf16[384,256]{1,0:T(8,128)(2,1)}, bf16[384,256]{1,0:T(8,128)(2,1)S(1)}, u32[]{:S(2)}) copy-start(bf16[384,256]{1,0:T(8,128)(2,1)S(1)} %collective-permute-done.3) | copy-start | bytes 589828
  95.3 21.7 %collective-permute-start.4 = (bf16[384,256]{1,0:T(8,128)(2,1)S(1)}, bf16[384,256]{1,0:T(8,128)(2,1)S(1)}, u32[]{:S(2)}, u32[]{:S(2)}) collective-permute-start(bf16[384,256]{1,0:T(8,128)(2,1)S(1)} %collective-permute-done.3), channel_id=1, source_target_pairs={{0,2},{2,4},{4,6},{6,8},{8,10},{10,12},{12,14},{14,0},{1,3},{3,5},... | collective-permute-start | bytes 589832 | tf_op jit(solution)/shard_map/ppermute | solution.py:135
  111.8 17.6 %collective-permute-start.7 = (bf16[384,256]{1,0:T(8,128)(2,1)}, bf16[384,256]{1,0:T(8,128)(2,1)}, u32[]{:S(2)}, u32[]{:S(2)}) collective-permute-start(bf16[384,256]{1,0:T(8,128)(2,1)} %collective-permute-done.6), channel_id=1, source_target_pairs={{0,14},{2,0},{4,2},{6,4},{8,6},{10,8},{12,10},{14,12},{1,15},{3,1}... | collective-permute-start | bytes 589832 | tf_op jit(solution)/shard_map/ppermute | solution.py:138
  119.4 44.7 %all-to-all-start.1 = ((bf16[32,192,128]{2,1,0:T(8,128)(2,1)}), bf16[32,192,128]{2,1,0:T(8,128)(2,1)S(1)}, u32[]{:S(2)}, u32[]{:S(2)}) async-start(bf16[32,192,128]{2,1,0:T(8,128)(2,1)} %bitcast.16), calls=%async_computation.1 | async-start | bytes 3145728 | tf_op jit(solution)/shard_map/all_to_all | solution.py:281
  126.4 92.9 %all-gather.7.cloned.1.call-start = ((), (), s32[]{:S(2)}) async-start(), calls=%async_computation.3 | async-start | bytes 3342336 | tf_op jit(solution)/shard_map/all_gather | solution.py:294
  126.5 2.0 copy-start.8
  130.4 5.4 %collective-permute-start.8 = (bf16[8,384,256]{2,1,0:T(8,128)(2,1)S(1)}, bf16[8,384,256]{2,1,0:T(8,128)(2,1)}, u32[]{:S(2)}, u32[]{:S(2)}) collective-permute-start(bf16[8,384,256]{2,1,0:T(8,128)(2,1)S(1)} %bitcast_dynamic-update-slice_fusion.8.blocks), channel_id=1, source_target_pairs={{0,1},{1,0},{2,3},{3,2},{4,5},{5,4},{6,7},{7,6},{8,9},{9,8},{10,11... | collective-permute-start | bytes 4718600 | tf_op jit(solution)/shard_map/ppermute | solution.py:144
  132.4 1.6 copy-start
  134.0 1.8 copy-start.1
  165.1 43.5 %copy-start.4 = (bf16[8,384,256]{2,1,0:T(8,128)(2,1)S(1)}, bf16[8,384,256]{2,1,0:T(8,128)(2,1)}, u32[]{:S(2)}) copy-start(bf16[8,384,256]{2,1,0:T(8,128)(2,1)} %param.8) | copy-start | bytes 4718596
  165.1 43.5 %copy-start.12 = (f32[9]{0:T(128)S(1)}, f32[9]{0:T(128)}, u32[]{:S(2)}) copy-start(f32[9]{0:T(128)} %dwa.1) | copy-start | bytes 112
  165.1 8.0 %collective-permute-start.11 = (bf16[64,256]{1,0:T(8,128)(2,1)S(1)}, bf16[64,256]{1,0:T(8,128)(2,1)S(1)}, u32[]{:S(2)}, u32[]{:S(2)}) collective-permute-start(bf16[64,256]{1,0:T(8,128)(2,1)S(1)} %shard_map.86), channel_id=1, source_target_pairs={{0,16},{16,32},{32,48},{48,64},{64,80},{80,96},{96,112},{112,128},... | collective-permute-start | bytes 98312 | tf_op jit(solution)/shard_map/ppermute | solution.py:123
  173.9 8.6 %collective-permute-start.12 = (bf16[4,128,256]{2,1,0:T(8,128)(2,1)}, bf16[4,128,256]{2,1,0:T(8,128)(2,1)S(1)}, u32[]{:S(2)}, u32[]{:S(2)}) collective-permute-start(bf16[4,128,256]{2,1,0:T(8,128)(2,1)} %all_gather.18), channel_id=1, source_target_pairs={{0,64},{64,128},{128,192},{192,256},{256,320},{320,384},{384,448},... | collective-permute-start | bytes 786440 | tf_op jit(solution)/shard_map/ppermute | solution.py:135
  182.5 9.6 %collective-permute-start.13 = (bf16[4,128,256]{2,1,0:T(8,128)(2,1)S(1)}, bf16[4,128,256]{2,1,0:T(8,128)(2,1)S(1)}, u32[]{:S(2)}, u32[]{:S(2)}) collective-permute-start(bf16[4,128,256]{2,1,0:T(8,128)(2,1)S(1)} %collective-permute-done.12), channel_id=1, source_target_pairs={{0,64},{64,128},{128,192},{192,256},{256,320},{320,384},{384,448},... | collective-permute-start | bytes 786440 | tf_op jit(solution)/shard_map/ppermute | solution.py:135
  187.5 10.3 %collective-permute-start.16 = (bf16[4,128,256]{2,1,0:T(8,128)(2,1)}, bf16[4,128,256]{2,1,0:T(8,128)(2,1)S(1)}, u32[]{:S(2)}, u32[]{:S(2)}) collective-permute-start(bf16[4,128,256]{2,1,0:T(8,128)(2,1)} %all_gather.18), channel_id=1, source_target_pairs={{0,448},{64,0},{128,64},{192,128},{256,192},{320,256},{384,320},{4... | collective-permute-start | bytes 786440 | tf_op jit(solution)/shard_map/ppermute | solution.py:138
  192.1 10.9 %collective-permute-start.14 = (bf16[4,128,256]{2,1,0:T(8,128)(2,1)S(1)}, bf16[4,128,256]{2,1,0:T(8,128)(2,1)S(1)}, u32[]{:S(2)}, u32[]{:S(2)}) collective-permute-start(bf16[4,128,256]{2,1,0:T(8,128)(2,1)S(1)} %collective-permute-done.13), channel_id=1, source_target_pairs={{0,64},{64,128},{128,192},{192,256},{256,320},{320,384},{384,448},... | collective-permute-start | bytes 786440 | tf_op jit(solution)/shard_map/ppermute | solution.py:135
  197.8 12.0 %collective-permute-start.17 = (bf16[4,128,256]{2,1,0:T(8,128)(2,1)S(1)}, bf16[4,128,256]{2,1,0:T(8,128)(2,1)S(1)}, u32[]{:S(2)}, u32[]{:S(2)}) collective-permute-start(bf16[4,128,256]{2,1,0:T(8,128)(2,1)S(1)} %collective-permute-done.16), channel_id=1, source_target_pairs={{0,448},{64,0},{128,64},{192,128},{256,192},{320,256},{384,320},{4... | collective-permute-start | bytes 786440 | tf_op jit(solution)/shard_map/ppermute | solution.py:138
  203.0 9.5 %collective-permute-start.15 = (bf16[4,128,256]{2,1,0:T(8,128)(2,1)S(1)}, bf16[4,128,256]{2,1,0:T(8,128)(2,1)S(1)}, u32[]{:S(2)}, u32[]{:S(2)}) collective-permute-start(bf16[4,128,256]{2,1,0:T(8,128)(2,1)S(1)} %collective-permute-done.14), channel_id=1, source_target_pairs={{0,64},{64,128},{128,192},{192,256},{256,320},{320,384},{384,448},... | collective-permute-start | bytes 786440 | tf_op jit(solution)/shard_map/ppermute | solution.py:135
  208.6 4.0 %copy-start.5 = (bf16[4,128,256]{2,1,0:T(8,128)(2,1)S(1)}, bf16[4,128,256]{2,1,0:T(8,128)(2,1)}, u32[]{:S(2)}) copy-start(bf16[4,128,256]{2,1,0:T(8,128)(2,1)} %all_gather.18) | copy-start | bytes 786436
  209.8 9.5 %collective-permute-start.18 = (bf16[4,128,256]{2,1,0:T(8,128)(2,1)S(1)}, bf16[4,128,256]{2,1,0:T(8,128)(2,1)S(1)}, u32[]{:S(2)}, u32[]{:S(2)}) collective-permute-start(bf16[4,128,256]{2,1,0:T(8,128)(2,1)S(1)} %collective-permute-done.17), channel_id=1, source_target_pairs={{0,448},{64,0},{128,64},{192,128},{256,192},{320,256},{384,320},{4... | collective-permute-start | bytes 786440 | tf_op jit(solution)/shard_map/ppermute | solution.py:138
  219.3 1.3 copy-start.3
Sparse Core Ops, SparseCore 0:
  31.0 83.2 all-gather.4
  174.0 37.9 all-gather.6

commit v7 on v6

--- a/solution.py
+++ b/solution.py
@@ -54,26 +54,32 @@
     )(encoded)
 
 
-def pick_kernel(ids, store, out):
+def pick_kernel(ids, store, out, picked, sems):
+    parts = sems.shape[0]
+    count = out.shape[0] // parts
+
     def body(i, carry):
-        out[i] = store[ids[i]]
+        picked[i] = store[ids[i]]
         return carry
 
-    lax.fori_loop(0, out.shape[0], body, 0, unroll=8)
+    copies = []
+    for part in range(parts):
+        here = pl.ds(part * count, count)
+        lax.fori_loop(part * count, (part + 1) * count, body, 0, unroll=16)
+        copies.append(pltpu.make_async_copy(picked.at[here], out.at[here], sems.at[part]))
+        copies[-1].start()
+    for copy in copies:
+        copy.wait()
 
 
 def pick(ids, store):
-    count = ids.shape[0]
-    block = store.shape[1:]
+    shape = (ids.shape[0],) + store.shape[1:]
     return pl.pallas_call(
         pick_kernel,
-        out_shape=jax.ShapeDtypeStruct((count,) + block, store.dtype),
-        grid_spec=pltpu.PrefetchScalarGridSpec(
-            num_scalar_prefetch=1,
-            grid=(1,),
-            in_specs=[pl.BlockSpec(store.shape, lambda i, s: (0, 0, 0))],
-            out_specs=pl.BlockSpec((count,) + block, lambda i, s: (0, 0, 0)),
-        ),
+        out_shape=jax.ShapeDtypeStruct(shape, store.dtype),
+        in_specs=[pl.BlockSpec(memory_space=pltpu.SMEM), vmem_space()],
+        out_specs=pl.BlockSpec(memory_space=pltpu.HBM),
+        scratch_shapes=[pltpu.VMEM(shape, store.dtype), pltpu.SemaphoreType.DMA((4,))],
         compiler_params=ROOM,
         name="pick",
     )(ids, store)
@@ -179,62 +185,51 @@
 BAND = 128
 
 
-def finish_kernel(y, dwa, first, second, weights, stream, past, block_out, dense_out, total):
-    step = pl.program_id(0)
-    width = weights.shape[3]
-
-    @pl.when(step == 0)
-    def _():
-        total[...] = jnp.zeros(total.shape, jnp.float32)
-
-    for row in range(0, total.shape[0], BAND):
+def finish_kernel(y, dwa, gathered, weights, stream, past, block_out, dense_out, blocks, sems):
+    along, _, _, width = weights.shape
+    here = gathered.shape[0] // along
+    depth = gathered.shape[2]
+    copies = []
+    for k in range(along):
+        source = lax.rem(y[0] + k + along - along // 2, along) * here
+        copies.append(
+            pltpu.make_async_copy(
+                gathered.at[pl.ds(source, here)], blocks.at[pl.ds(k * here, here)], sems.at[k]
+            )
+        )
+        copies[-1].start()
+    for row in range(0, stream.shape[0], BAND):
         rows = slice(row, row + BAND)
-        value = total[rows, :]
-        for which, blocks in enumerate((first, second)):
-            groups, _, depth = blocks.shape
-            matching = weights[which].reshape(groups, depth, width)
-            for g in range(groups):
-                part = jnp.dot(blocks[g, rows, :], matching[g], preferred_element_type=jnp.float32)
-                value += part.astype(jnp.bfloat16).astype(jnp.float32)
-        total[rows, :] = value
-
-    @pl.when(step == pl.num_programs(0) - 1)
-    def _():
-        block = stream[...].astype(jnp.float32) + total[...]
-        block_out[...] = block.astype(block_out.dtype)
-        dense_out[...] = (dwa[dwa.shape[0] - 1] * block + past[...]).astype(dense_out.dtype)
-
-
-def finish(y, dwa, blocks, weights, stream, past):
-    groups, rows, depth = blocks.shape
-    along, across, cut, width = weights.shape
-    steps = along // 2
-    here = groups // along
-
-    def at(which):
-        return lambda i, y: (lax.rem(y[0] + 2 * i + which + along - along // 2, along), 0, 0)
-
-    whole = pl.BlockSpec((rows, width), lambda i, y: (0, 0))
+        total = jnp.zeros((BAND, width), jnp.float32)
+        for k in range(along):
+            if row == 0:
+                copies[k].wait()
+            matching = weights[k].reshape(here, depth, width)
+            for g in range(here):
+                part = jnp.dot(
+                    blocks[k * here + g, rows, :], matching[g], preferred_element_type=jnp.float32
+                )
+                total += part.astype(jnp.bfloat16).astype(jnp.float32)
+        block = stream[rows, :].astype(jnp.float32) + total
+        block_out[rows, :] = block.astype(block_out.dtype)
+        dense_out[rows, :] = (dwa[dwa.shape[0] - 1] * block + past[rows, :]).astype(dense_out.dtype)
+
+
+def finish(y, dwa, gathered, columns, stream, past):
     shape = jax.ShapeDtypeStruct(stream.shape, jnp.bfloat16)
+    scalars = pl.BlockSpec(memory_space=pltpu.SMEM)
     return pl.pallas_call(
         finish_kernel,
         out_shape=(shape, shape),
-        grid_spec=pltpu.PrefetchScalarGridSpec(
-            num_scalar_prefetch=1,
-            grid=(steps,),
-            in_specs=[
-                pl.BlockSpec(memory_space=pltpu.SMEM),
-                pl.BlockSpec((here, rows, depth), at(0)),
-                pl.BlockSpec((here, rows, depth), at(1)),
-                pl.BlockSpec((2, across, cut, width), lambda i, y: (i, 0, 0, 0)),
-                whole,
-                whole,
-            ],
-            out_specs=(whole, whole),
-            scratch_shapes=[pltpu.VMEM(stream.shape, jnp.float32)],
-        ),
+        in_specs=[scalars] * 2 + [pl.BlockSpec(memory_space=pltpu.HBM)] + [vmem_space()] * 3,
+        out_specs=(vmem_space(), vmem_space()),
+        scratch_shapes=[
+            pltpu.VMEM(gathered.shape, gathered.dtype),
+            pltpu.SemaphoreType.DMA((columns.shape[0],)),
+        ],
+        compiler_params=pltpu.CompilerParams(vmem_limit_bytes=50 * 1024 * 1024),
         name="finish",
-    )(y, dwa, blocks, blocks, weights, stream, past)
+    )(y, dwa, gathered, columns, stream, past)
 
 
 def columns_here(w_out):

time: 234 us -> 231 us (0.987)
  no operation moved by 1% of the time
where the time goes in v7:
time: 231 us; the launch traced here: 230 us
  starting transfers between devices  92.5 us (40%)
  waiting for transfers between devices  82.2 us (36%)
  Pallas kernels  17.7 us (8%)
  between operations  14.7 us (6%)
  blocking collectives  14.5 us (6%)
  local copies, waits for them, and re-layouts  6.66 us (3%)
    ppermute x8, waiting for transfers between devices, around(): right = lax.ppermute(right, axis, ring(count, 1))  46.8 us
    ppermute x8, starting transfers between devices, around(): right = lax.ppermute(right, axis, ring(count, 1))  29.6 us
    ppermute x6, starting transfers between devices, around(): left = lax.ppermute(left, axis, ring(count, -1))  25.4 us
    all_to_all x1, waiting for transfers between devices, on_device(): lax.all_to_all(picked.reshape(ctx_count, -1, HDIM), CTX, split_axis=0, co...  25.3 us
    all_gather x1, blocking collectives, on_device(): turned = lax.all_gather(turned, 'x', axis=0)  14.5 us
    ppermute x2, starting transfers between devices, columns_here(): pieces.append(lax.ppermute(send, CTX + DB, route))  11.4 us
    all_to_all x1, starting transfers between devices, on_device(): lax.all_to_all(by_head.reshape(db_count, -1, HDIM), DB, split_axis=0, con...  10.6 us
    all_to_all x1, starting transfers between devices, on_device(): lax.all_to_all(picked.reshape(ctx_count, -1, HDIM), CTX, split_axis=0, co...  7.06 us
  transfers between devices with their start and end apart: 23, of which 12 were waited for; matrix products, arithmetic and copies ran while one was open for 2% of the time, Pallas kernels for 4%

profile of v7, /device:TPU:24, one launch (start us, length us, event | category | flops | bytes accessed | tf_op | source)
XLA Modules:
  0.0 229.5 jit_solution(13283027208273582463)
XLA Ops:
  7.2 3.0 %split_heads.1 = bf16[16,24,2,4,2,128]{5,4,3,2,1,0:T(2,128)(2,1)} custom-call(bf16[1,24,4,2,4096]{4,3,2,1,0:T(2,128)(2,1)} %source.1), custom_call_target="tpu_custom_call" | custom-call | tf_op jit(solution)/shard_map/split_heads/pallas_call | solution.py:45
  10.2 0.0 copy-start.2
  10.2 0.0 copy-start.12
  10.2 10.6 %all-to-all-start = ((bf16[16,384,128]{2,1,0:T(8,128)(2,1)}), bf16[16,384,128]{2,1,0:T(8,128)(2,1)S(1)}, u32[]{:S(2)}, u32[]{:S(2)}) async-start(bf16[16,384,128]{2,1,0:T(8,128)(2,1)} %bitcast.51), calls=%async_computation | async-start | bytes 3145728 | tf_op jit(solution)/shard_map/all_to_all | solution.py:266
  20.8 0.0 copy-start.4
  20.8 0.0 all-gather.5.cloned.1.call-start
  20.9 4.6 %collective-permute-start = (bf16[64,256]{1,0:T(8,128)(2,1)S(1)}, bf16[64,256]{1,0:T(8,128)(2,1)S(1)}, u32[]{:S(2)}, u32[]{:S(2)}) collective-permute-start(bf16[64,256]{1,0:T(8,128)(2,1)S(1)} %slice.19), channel_id=1, source_target_pairs={{16,0},{32,16},{48,32},{64,48},{80,64},{96,80},{112,96},{128,112},... | collective-permute-start | bytes 98312 | tf_op jit(solution)/shard_map/ppermute | solution.py:129
  25.5 1.5 collective-permute-done
  27.0 3.8 %collective-permute-start.1 = (bf16[384,256]{1,0:T(8,128)(2,1)S(1)}, bf16[384,256]{1,0:T(8,128)(2,1)S(1)}, u32[]{:S(2)}, u32[]{:S(2)}) collective-permute-start(bf16[384,256]{1,0:T(8,128)(2,1)S(1)} %pad_maximum_fusion), channel_id=1, source_target_pairs={{0,2},{2,4},{4,6},{6,8},{8,10},{10,12},{12,14},{14,0},{1,3},{3,5},... | collective-permute-start | bytes 589832 | tf_op jit(solution)/shard_map/ppermute | solution.py:141
  30.9 0.0 all-gather.5.cloned.1.call-update
  30.9 32.2 %collective-permute-done.1 = bf16[384,256]{1,0:T(8,128)(2,1)S(1)} collective-permute-done((bf16[384,256]{1,0:T(8,128)(2,1)S(1)}, bf16[384,256]{1,0:T(8,128)(2,1)S(1)}, u32[]{:S(2)}, u32[]{:S(2)}) %collective-permute-start.1) | collective-permute-done | bytes 196640 | tf_op jit(solution)/shard_map/ppermute | solution.py:141
  63.1 1.9 collective-permute-start.2
  65.0 5.1 %collective-permute-start.5 = (bf16[384,256]{1,0:T(8,128)(2,1)S(1)}, bf16[384,256]{1,0:T(8,128)(2,1)S(1)}, u32[]{:S(2)}, u32[]{:S(2)}) collective-permute-start(bf16[384,256]{1,0:T(8,128)(2,1)S(1)} %pad_maximum_fusion), channel_id=1, source_target_pairs={{0,14},{2,0},{4,2},{6,4},{8,6},{10,8},{12,10},{14,12},{1,15},{3,1}... | collective-permute-start | bytes 589832 | tf_op jit(solution)/shard_map/ppermute | solution.py:144
  70.2 2.4 %collective-permute-done.2 = bf16[384,256]{1,0:T(8,128)(2,1)S(1)} collective-permute-done((bf16[384,256]{1,0:T(8,128)(2,1)S(1)}, bf16[384,256]{1,0:T(8,128)(2,1)S(1)}, u32[]{:S(2)}, u32[]{:S(2)}) %collective-permute-start.2) | collective-permute-done | bytes 196640 | tf_op jit(solution)/shard_map/ppermute | solution.py:141
  72.6 1.9 collective-permute-start.3
  74.5 6.7 %collective-permute-start.10 = (bf16[128,128]{1,0:T(8,128)(2,1)S(1)}, bf16[128,128]{1,0:T(8,128)(2,1)S(1)}, u32[]{:S(2)}, u32[]{:S(2)}) collective-permute-start(bf16[128,128]{1,0:T(8,128)(2,1)S(1)} %get-tuple-element.7), channel_id=1, source_target_pairs={{0,16},{1,48},{2,80},{3,112},{4,144},{5,176},{6,208},{7,240},{8,27... | collective-permute-start | bytes 98312 | tf_op jit(solution)/shard_map/ppermute | solution.py:248
  81.3 4.6 %collective-permute-start.9 = (bf16[128,128]{1,0:T(8,128)(2,1)S(1)}, bf16[128,128]{1,0:T(8,128)(2,1)S(1)}, u32[]{:S(2)}, u32[]{:S(2)}) collective-permute-start(bf16[128,128]{1,0:T(8,128)(2,1)S(1)} %get-tuple-element.6), channel_id=1, source_target_pairs={{0,0},{1,32},{2,64},{3,96},{4,128},{5,160},{6,192},{7,224},{8,256}... | collective-permute-start | bytes 98312 | tf_op jit(solution)/shard_map/ppermute | solution.py:248
  85.9 0.0 collective-permute-done.5
  85.9 9.4 %collective-permute-start.6 = (bf16[384,256]{1,0:T(8,128)(2,1)S(1)}, bf16[384,256]{1,0:T(8,128)(2,1)}, u32[]{:S(2)}, u32[]{:S(2)}) collective-permute-start(bf16[384,256]{1,0:T(8,128)(2,1)S(1)} %collective-permute-done.5), channel_id=1, source_target_pairs={{0,14},{2,0},{4,2},{6,4},{8,6},{10,8},{12,10},{14,12},{1,15},{3,1}... | collective-permute-start | bytes 589832 | tf_op jit(solution)/shard_map/ppermute | solution.py:144
  95.3 0.0 copy-start.11
  95.3 1.9 collective-permute-start.4
  97.2 0.0 collective-permute-done.10
  97.3 14.5 %all_gather.18 = bf16[4,128,256]{2,1,0:T(8,128)(2,1)} all-gather(bf16[1,128,256]{2,1,0:T(8,128)(2,1)S(1)} %maximum_select_fusion), channel_id=1, replica_groups=mesh['y'=8,'x'=4,'z'=8,'core'=2] {'x'}, dimensions={0}, use_global_device_ids=true | all-gather | bytes 327680 | tf_op jit(solution)/shard_map/all_gather | solution.py:272
  111.8 0.0 collective-permute-done.6
  111.8 5.1 %collective-permute-start.7 = (bf16[384,256]{1,0:T(8,128)(2,1)}, bf16[384,256]{1,0:T(8,128)(2,1)}, u32[]{:S(2)}, u32[]{:S(2)}) collective-permute-start(bf16[384,256]{1,0:T(8,128)(2,1)} %collective-permute-done.6), channel_id=1, source_target_pairs={{0,14},{2,0},{4,2},{6,4},{8,6},{10,8},{12,10},{14,12},{1,15},{3,1}... | collective-permute-start | bytes 589832 | tf_op jit(solution)/shard_map/ppermute | solution.py:144
  117.0 1.9 pick.1
  118.9 7.1 %all-to-all-start.1 = ((bf16[32,192,128]{2,1,0:T(8,128)(2,1)}), bf16[32,192,128]{2,1,0:T(8,128)(2,1)S(1)}, u32[]{:S(2)}, u32[]{:S(2)}) async-start(bf16[32,192,128]{2,1,0:T(8,128)(2,1)} %bitcast.16), calls=%async_computation.1 | async-start | bytes 3145728 | tf_op jit(solution)/shard_map/all_to_all | solution.py:276
  126.0 0.0 all-gather.7.cloned.1.call-start
  126.0 1.0 bitcast_dynamic-update-slice_fusion.14
  127.0 0.9 bitcast_dynamic-update-slice_fusion.13
  128.0 0.9 bitcast_dynamic-update-slice_fusion.12
  129.0 0.9 bitcast_dynamic-update-slice_fusion.9
  129.9 0.9 bitcast_dynamic-update-slice_fusion.8.blocks
  130.9 1.9 collective-permute-start.8
  132.8 0.1 pad_add_fusion.place
  132.9 1.6 copy-done
  134.5 1.1 project_own.1.rest_0_
  135.6 0.7 collective-permute-done.8.blocks
  136.3 2.0 project_other.1.q_ref
  138.3 25.3 %all-to-all-done.1 = bf16[32,192,128]{2,1,0:T(8,128)(2,1)S(1)} async-done(((bf16[32,192,128]{2,1,0:T(8,128)(2,1)}), bf16[32,192,128]{2,1,0:T(8,128)(2,1)S(1)}, u32[]{:S(2)}, u32[]{:S(2)}) %all-to-all-start.1) | async-done | bytes 1572896 | tf_op jit(solution)/shard_map/all_to_all | solution.py:276
  163.6 1.0 shard_map.86
  164.6 0.0 copy-start.3
  164.6 0.0 copy-start.5
  164.6 2.1 collective-permute-start.11
  166.7 4.2 %shard_map.87 = bf16[320,256]{1,0:T(8,128)(2,1)S(1)} custom-call(bf16[384,256]{1,0:T(8,128)(2,1)S(1)} %project_other.1.q_ref, bf16[32,12,2,8,128]{4,3,2,1,0:T(8,128)(2,1)S(1)} %bitcast.46), custom_call_target="tpu_custom_call" | custom-call | tf_op jit(solution)/shard_map/pallas_call | solution.py:117
  170.9 1.7 collective-permute-done.11
  172.7 0.7 pad_maximum_fusion.1
  173.4 0.0 all-gather.7.cloned.1.call-update
  173.4 3.9 %collective-permute-start.12 = (bf16[4,128,256]{2,1,0:T(8,128)(2,1)}, bf16[4,128,256]{2,1,0:T(8,128)(2,1)S(1)}, u32[]{:S(2)}, u32[]{:S(2)}) collective-permute-start(bf16[4,128,256]{2,1,0:T(8,128)(2,1)} %all_gather.18), channel_id=1, source_target_pairs={{0,64},{64,128},{128,192},{192,256},{256,320},{320,384},{384,448},... | collective-permute-start | bytes 786440 | tf_op jit(solution)/shard_map/ppermute | solution.py:141
  177.4 4.8 %collective-permute-done.12 = bf16[4,128,256]{2,1,0:T(8,128)(2,1)S(1)} collective-permute-done((bf16[4,128,256]{2,1,0:T(8,128)(2,1)}, bf16[4,128,256]{2,1,0:T(8,128)(2,1)S(1)}, u32[]{:S(2)}, u32[]{:S(2)}) %collective-permute-start.12) | collective-permute-done | bytes 262176 | tf_op jit(solution)/shard_map/ppermute | solution.py:141
  182.1 4.9 %collective-permute-start.13 = (bf16[4,128,256]{2,1,0:T(8,128)(2,1)S(1)}, bf16[4,128,256]{2,1,0:T(8,128)(2,1)S(1)}, u32[]{:S(2)}, u32[]{:S(2)}) collective-permute-start(bf16[4,128,256]{2,1,0:T(8,128)(2,1)S(1)} %collective-permute-done.12), channel_id=1, source_target_pairs={{0,64},{64,128},{128,192},{192,256},{256,320},{320,384},{384,448},... | collective-permute-start | bytes 786440 | tf_op jit(solution)/shard_map/ppermute | solution.py:141
  187.1 1.9 collective-permute-start.16
  189.0 2.7 %collective-permute-done.13 = bf16[4,128,256]{2,1,0:T(8,128)(2,1)S(1)} collective-permute-done((bf16[4,128,256]{2,1,0:T(8,128)(2,1)S(1)}, bf16[4,128,256]{2,1,0:T(8,128)(2,1)S(1)}, u32[]{:S(2)}, u32[]{:S(2)}) %collective-permute-start.13) | collective-permute-done | bytes 262176 | tf_op jit(solution)/shard_map/ppermute | solution.py:141
  191.6 5.6 %collective-permute-start.14 = (bf16[4,128,256]{2,1,0:T(8,128)(2,1)S(1)}, bf16[4,128,256]{2,1,0:T(8,128)(2,1)S(1)}, u32[]{:S(2)}, u32[]{:S(2)}) collective-permute-start(bf16[4,128,256]{2,1,0:T(8,128)(2,1)S(1)} %collective-permute-done.13), channel_id=1, source_target_pairs={{0,64},{64,128},{128,192},{192,256},{256,320},{320,384},{384,448},... | collective-permute-start | bytes 786440 | tf_op jit(solution)/shard_map/ppermute | solution.py:141
  197.2 0.1 collective-permute-done.16
  197.3 1.9 collective-permute-start.17
  199.3 3.3 %collective-permute-done.14 = bf16[4,128,256]{2,1,0:T(8,128)(2,1)S(1)} collective-permute-done((bf16[4,128,256]{2,1,0:T(8,128)(2,1)S(1)}, bf16[4,128,256]{2,1,0:T(8,128)(2,1)S(1)}, u32[]{:S(2)}, u32[]{:S(2)}) %collective-permute-start.14) | collective-permute-done | bytes 262176 | tf_op jit(solution)/shard_map/ppermute | solution.py:141
  202.6 5.6 %collective-permute-start.15 = (bf16[4,128,256]{2,1,0:T(8,128)(2,1)S(1)}, bf16[4,128,256]{2,1,0:T(8,128)(2,1)S(1)}, u32[]{:S(2)}, u32[]{:S(2)}) collective-permute-start(bf16[4,128,256]{2,1,0:T(8,128)(2,1)S(1)} %collective-permute-done.14), channel_id=1, source_target_pairs={{0,64},{64,128},{128,192},{192,256},{256,320},{320,384},{384,448},... | collective-permute-start | bytes 786440 | tf_op jit(solution)/shard_map/ppermute | solution.py:141
  208.2 0.4 multiply_reduce_fusion.past
  208.6 1.9 collective-permute-start.18
  210.5 1.5 collective-permute-done.15
  212.2 5.8 %collective-permute-done.18 = bf16[4,128,256]{2,1,0:T(8,128)(2,1)S(1)} collective-permute-done((bf16[4,128,256]{2,1,0:T(8,128)(2,1)S(1)}, bf16[4,128,256]{2,1,0:T(8,128)(2,1)S(1)}, u32[]{:S(2)}, u32[]{:S(2)}) %collective-permute-start.18) | collective-permute-done | bytes 262176 | tf_op jit(solution)/shard_map/ppermute | solution.py:144
  218.1 0.0 all-gather.7.cloned.1.call-done
  218.1 4.5 %finish.1 = (bf16[384,256]{1,0:T(8,128)(2,1)}, bf16[384,256]{1,0:T(8,128)(2,1)}) custom-call(s32[1]{0:T(128)} %bitcast.y, f32[9]{0:T(128)S(1)} %copy-done.3, bf16[16,384,256]{2,1,0:T(8,128)(2,1)} %bitcast.52, bf16[8,4,128,256]{3,2,1,0:T(8,128)(2,1)S(1)} %bitcast_dynamic-update-slice_fusion.weights, bf16[384,256]{1,0:T(8,128)(2,1)S(1)} %copy-done.2, ...), custom_call_target="tpu_custom_call" | custom-call | tf_op jit(solution)/shard_map/finish/pallas_call | solution.py:221
  (44 shorter events, 0.4 us)
Async XLA Ops:
  10.2 10.7 %copy-start.2 = (bf16[384,256]{1,0:T(8,128)(2,1)S(1)}, bf16[384,256]{1,0:T(8,128)(2,1)}, u32[]{:S(2)}) copy-start(bf16[384,256]{1,0:T(8,128)(2,1)} %stream.1) | copy-start | bytes 589828
  10.2 64.3 %copy-start.12 = (bf16[256,128]{1,0:T(8,128)(2,1)S(1)}, bf16[256,128]{1,0:T(8,128)(2,1)}, u32[]{:S(2)}) copy-start(bf16[256,128]{1,0:T(8,128)(2,1)} %param.11) | copy-start | bytes 196612
  10.2 106.8 %all-to-all-start = ((bf16[16,384,128]{2,1,0:T(8,128)(2,1)}), bf16[16,384,128]{2,1,0:T(8,128)(2,1)S(1)}, u32[]{:S(2)}, u32[]{:S(2)}) async-start(bf16[16,384,128]{2,1,0:T(8,128)(2,1)} %bitcast.51), calls=%async_computation | async-start | bytes 3145728 | tf_op jit(solution)/shard_map/all_to_all | solution.py:266
  20.8 96.3 %copy-start.4 = (s32[384]{0:T(512)S(1)}, s32[384]{0:T(512)}, u32[]{:S(2)}) copy-start(s32[384]{0:T(512)} %ids.1) | copy-start | bytes 4612
  20.8 112.1 %all-gather.5.cloned.1.call-start = ((), (), s32[]{:S(2)}) async-start(), calls=%async_computation.2 | async-start | bytes 2162688 | tf_op jit(solution)/shard_map/all_gather | solution.py:264
  20.9 6.1 %collective-permute-start = (bf16[64,256]{1,0:T(8,128)(2,1)S(1)}, bf16[64,256]{1,0:T(8,128)(2,1)S(1)}, u32[]{:S(2)}, u32[]{:S(2)}) collective-permute-start(bf16[64,256]{1,0:T(8,128)(2,1)S(1)} %slice.19), channel_id=1, source_target_pairs={{16,0},{32,16},{48,32},{64,48},{80,64},{96,80},{112,96},{128,112},... | collective-permute-start | bytes 98312 | tf_op jit(solution)/shard_map/ppermute | solution.py:129
  27.0 36.1 %collective-permute-start.1 = (bf16[384,256]{1,0:T(8,128)(2,1)S(1)}, bf16[384,256]{1,0:T(8,128)(2,1)S(1)}, u32[]{:S(2)}, u32[]{:S(2)}) collective-permute-start(bf16[384,256]{1,0:T(8,128)(2,1)S(1)} %pad_maximum_fusion), channel_id=1, source_target_pairs={{0,2},{2,4},{4,6},{6,8},{8,10},{10,12},{12,14},{14,0},{1,3},{3,5},... | collective-permute-start | bytes 589832 | tf_op jit(solution)/shard_map/ppermute | solution.py:141
  63.1 34.2 %copy-start.7 = (bf16[384,256]{1,0:T(8,128)(2,1)}, bf16[384,256]{1,0:T(8,128)(2,1)S(1)}, u32[]{:S(2)}) copy-start(bf16[384,256]{1,0:T(8,128)(2,1)S(1)} %collective-permute-done.1) | copy-start | bytes 589828
  63.1 9.5 %collective-permute-start.2 = (bf16[384,256]{1,0:T(8,128)(2,1)S(1)}, bf16[384,256]{1,0:T(8,128)(2,1)S(1)}, u32[]{:S(2)}, u32[]{:S(2)}) collective-permute-start(bf16[384,256]{1,0:T(8,128)(2,1)S(1)} %collective-permute-done.1), channel_id=1, source_target_pairs={{0,2},{2,4},{4,6},{6,8},{8,10},{10,12},{12,14},{14,0},{1,3},{3,5},... | collective-permute-start | bytes 589832 | tf_op jit(solution)/shard_map/ppermute | solution.py:141
  65.0 20.9 %collective-permute-start.5 = (bf16[384,256]{1,0:T(8,128)(2,1)S(1)}, bf16[384,256]{1,0:T(8,128)(2,1)S(1)}, u32[]{:S(2)}, u32[]{:S(2)}) collective-permute-start(bf16[384,256]{1,0:T(8,128)(2,1)S(1)} %pad_maximum_fusion), channel_id=1, source_target_pairs={{0,14},{2,0},{4,2},{6,4},{8,6},{10,8},{12,10},{14,12},{1,15},{3,1}... | collective-permute-start | bytes 589832 | tf_op jit(solution)/shard_map/ppermute | solution.py:144
  72.6 44.4 %copy-start.10 = (bf16[384,256]{1,0:T(8,128)(2,1)}, bf16[384,256]{1,0:T(8,128)(2,1)S(1)}, u32[]{:S(2)}) copy-start(bf16[384,256]{1,0:T(8,128)(2,1)S(1)} %collective-permute-done.2) | copy-start | bytes 589828
  72.6 22.7 %collective-permute-start.3 = (bf16[384,256]{1,0:T(8,128)(2,1)S(1)}, bf16[384,256]{1,0:T(8,128)(2,1)S(1)}, u32[]{:S(2)}, u32[]{:S(2)}) collective-permute-start(bf16[384,256]{1,0:T(8,128)(2,1)S(1)} %collective-permute-done.2), channel_id=1, source_target_pairs={{0,2},{2,4},{4,6},{6,8},{8,10},{10,12},{12,14},{14,0},{1,3},{3,5},... | collective-permute-start | bytes 589832 | tf_op jit(solution)/shard_map/ppermute | solution.py:141
  74.5 22.7 %collective-permute-start.10 = (bf16[128,128]{1,0:T(8,128)(2,1)S(1)}, bf16[128,128]{1,0:T(8,128)(2,1)S(1)}, u32[]{:S(2)}, u32[]{:S(2)}) collective-permute-start(bf16[128,128]{1,0:T(8,128)(2,1)S(1)} %get-tuple-element.7), channel_id=1, source_target_pairs={{0,16},{1,48},{2,80},{3,112},{4,144},{5,176},{6,208},{7,240},{8,27... | collective-permute-start | bytes 98312 | tf_op jit(solution)/shard_map/ppermute | solution.py:248
  81.3 16.0 %collective-permute-start.9 = (bf16[128,128]{1,0:T(8,128)(2,1)S(1)}, bf16[128,128]{1,0:T(8,128)(2,1)S(1)}, u32[]{:S(2)}, u32[]{:S(2)}) collective-permute-start(bf16[128,128]{1,0:T(8,128)(2,1)S(1)} %get-tuple-element.6), channel_id=1, source_target_pairs={{0,0},{1,32},{2,64},{3,96},{4,128},{5,160},{6,192},{7,224},{8,256}... | collective-permute-start | bytes 98312 | tf_op jit(solution)/shard_map/ppermute | solution.py:248
  85.9 31.0 %copy-start.8 = (bf16[384,256]{1,0:T(8,128)(2,1)}, bf16[384,256]{1,0:T(8,128)(2,1)S(1)}, u32[]{:S(2)}) copy-start(bf16[384,256]{1,0:T(8,128)(2,1)S(1)} %collective-permute-done.5) | copy-start | bytes 589828
  85.9 25.9 %collective-permute-start.6 = (bf16[384,256]{1,0:T(8,128)(2,1)S(1)}, bf16[384,256]{1,0:T(8,128)(2,1)}, u32[]{:S(2)}, u32[]{:S(2)}) collective-permute-start(bf16[384,256]{1,0:T(8,128)(2,1)S(1)} %collective-permute-done.5), channel_id=1, source_target_pairs={{0,14},{2,0},{4,2},{6,4},{8,6},{10,8},{12,10},{14,12},{1,15},{3,1}... | collective-permute-start | bytes 589832 | tf_op jit(solution)/shard_map/ppermute | solution.py:144
  95.3 21.7 %copy-start.11 = (bf16[384,256]{1,0:T(8,128)(2,1)}, bf16[384,256]{1,0:T(8,128)(2,1)S(1)}, u32[]{:S(2)}) copy-start(bf16[384,256]{1,0:T(8,128)(2,1)S(1)} %collective-permute-done.3) | copy-start | bytes 589828
  95.3 21.7 %collective-permute-start.4 = (bf16[384,256]{1,0:T(8,128)(2,1)S(1)}, bf16[384,256]{1,0:T(8,128)(2,1)S(1)}, u32[]{:S(2)}, u32[]{:S(2)}) collective-permute-start(bf16[384,256]{1,0:T(8,128)(2,1)S(1)} %collective-permute-done.3), channel_id=1, source_target_pairs={{0,2},{2,4},{4,6},{6,8},{8,10},{10,12},{12,14},{14,0},{1,3},{3,5},... | collective-permute-start | bytes 589832 | tf_op jit(solution)/shard_map/ppermute | solution.py:141
  111.8 18.1 %collective-permute-start.7 = (bf16[384,256]{1,0:T(8,128)(2,1)}, bf16[384,256]{1,0:T(8,128)(2,1)}, u32[]{:S(2)}, u32[]{:S(2)}) collective-permute-start(bf16[384,256]{1,0:T(8,128)(2,1)} %collective-permute-done.6), channel_id=1, source_target_pairs={{0,14},{2,0},{4,2},{6,4},{8,6},{10,8},{12,10},{14,12},{1,15},{3,1}... | collective-permute-start | bytes 589832 | tf_op jit(solution)/shard_map/ppermute | solution.py:144
  118.9 44.7 %all-to-all-start.1 = ((bf16[32,192,128]{2,1,0:T(8,128)(2,1)}), bf16[32,192,128]{2,1,0:T(8,128)(2,1)S(1)}, u32[]{:S(2)}, u32[]{:S(2)}) async-start(bf16[32,192,128]{2,1,0:T(8,128)(2,1)} %bitcast.16), calls=%async_computation.1 | async-start | bytes 3145728 | tf_op jit(solution)/shard_map/all_to_all | solution.py:276
  126.0 92.1 %all-gather.7.cloned.1.call-start = ((), (), s32[]{:S(2)}) async-start(), calls=%async_computation.3 | async-start | bytes 3342336 | tf_op jit(solution)/shard_map/all_gather | solution.py:289
  126.0 2.9 %copy-start.9 = (bf16[384,256]{1,0:T(8,128)(2,1)S(1)}, bf16[384,256]{1,0:T(8,128)(2,1)}, u32[]{:S(2)}) copy-start(bf16[384,256]{1,0:T(8,128)(2,1)} %copy-done.8) | copy-start | bytes 589828
  130.9 5.4 %collective-permute-start.8 = (bf16[8,384,256]{2,1,0:T(8,128)(2,1)S(1)}, bf16[8,384,256]{2,1,0:T(8,128)(2,1)}, u32[]{:S(2)}, u32[]{:S(2)}) collective-permute-start(bf16[8,384,256]{2,1,0:T(8,128)(2,1)S(1)} %bitcast_dynamic-update-slice_fusion.8.blocks), channel_id=1, source_target_pairs={{0,1},{1,0},{2,3},{3,2},{4,5},{5,4},{6,7},{7,6},{8,9},{9,8},{10,11... | collective-permute-start | bytes 4718600 | tf_op jit(solution)/shard_map/ppermute | solution.py:150
  132.9 1.6 copy-start
  134.5 1.8 copy-start.1
  164.6 43.6 %copy-start.3 = (f32[9]{0:T(128)S(1)}, f32[9]{0:T(128)}, u32[]{:S(2)}) copy-start(f32[9]{0:T(128)} %dwa.1) | copy-start | bytes 112
  164.6 43.6 %copy-start.5 = (bf16[8,384,256]{2,1,0:T(8,128)(2,1)S(1)}, bf16[8,384,256]{2,1,0:T(8,128)(2,1)}, u32[]{:S(2)}) copy-start(bf16[8,384,256]{2,1,0:T(8,128)(2,1)} %param.8) | copy-start | bytes 4718596
  164.6 8.0 %collective-permute-start.11 = (bf16[64,256]{1,0:T(8,128)(2,1)S(1)}, bf16[64,256]{1,0:T(8,128)(2,1)S(1)}, u32[]{:S(2)}, u32[]{:S(2)}) collective-permute-start(bf16[64,256]{1,0:T(8,128)(2,1)S(1)} %shard_map.86), channel_id=1, source_target_pairs={{0,16},{16,32},{32,48},{48,64},{64,80},{80,96},{96,112},{112,128},... | collective-permute-start | bytes 98312 | tf_op jit(solution)/shard_map/ppermute | solution.py:129
  173.4 8.7 %collective-permute-start.12 = (bf16[4,128,256]{2,1,0:T(8,128)(2,1)}, bf16[4,128,256]{2,1,0:T(8,128)(2,1)S(1)}, u32[]{:S(2)}, u32[]{:S(2)}) collective-permute-start(bf16[4,128,256]{2,1,0:T(8,128)(2,1)} %all_gather.18), channel_id=1, source_target_pairs={{0,64},{64,128},{128,192},{192,256},{256,320},{320,384},{384,448},... | collective-permute-start | bytes 786440 | tf_op jit(solution)/shard_map/ppermute | solution.py:141
  182.1 9.5 %collective-permute-start.13 = (bf16[4,128,256]{2,1,0:T(8,128)(2,1)S(1)}, bf16[4,128,256]{2,1,0:T(8,128)(2,1)S(1)}, u32[]{:S(2)}, u32[]{:S(2)}) collective-permute-start(bf16[4,128,256]{2,1,0:T(8,128)(2,1)S(1)} %collective-permute-done.12), channel_id=1, source_target_pairs={{0,64},{64,128},{128,192},{192,256},{256,320},{320,384},{384,448},... | collective-permute-start | bytes 786440 | tf_op jit(solution)/shard_map/ppermute | solution.py:141
  187.1 10.3 %collective-permute-start.16 = (bf16[4,128,256]{2,1,0:T(8,128)(2,1)}, bf16[4,128,256]{2,1,0:T(8,128)(2,1)S(1)}, u32[]{:S(2)}, u32[]{:S(2)}) collective-permute-start(bf16[4,128,256]{2,1,0:T(8,128)(2,1)} %all_gather.18), channel_id=1, source_target_pairs={{0,448},{64,0},{128,64},{192,128},{256,192},{320,256},{384,320},{4... | collective-permute-start | bytes 786440 | tf_op jit(solution)/shard_map/ppermute | solution.py:144
  191.6 10.9 %collective-permute-start.14 = (bf16[4,128,256]{2,1,0:T(8,128)(2,1)S(1)}, bf16[4,128,256]{2,1,0:T(8,128)(2,1)S(1)}, u32[]{:S(2)}, u32[]{:S(2)}) collective-permute-start(bf16[4,128,256]{2,1,0:T(8,128)(2,1)S(1)} %collective-permute-done.13), channel_id=1, source_target_pairs={{0,64},{64,128},{128,192},{192,256},{256,320},{320,384},{384,448},... | collective-permute-start | bytes 786440 | tf_op jit(solution)/shard_map/ppermute | solution.py:141
  197.3 11.2 %collective-permute-start.17 = (bf16[4,128,256]{2,1,0:T(8,128)(2,1)S(1)}, bf16[4,128,256]{2,1,0:T(8,128)(2,1)S(1)}, u32[]{:S(2)}, u32[]{:S(2)}) collective-permute-start(bf16[4,128,256]{2,1,0:T(8,128)(2,1)S(1)} %collective-permute-done.16), channel_id=1, source_target_pairs={{0,448},{64,0},{128,64},{192,128},{256,192},{320,256},{384,320},{4... | collective-permute-start | bytes 786440 | tf_op jit(solution)/shard_map/ppermute | solution.py:144
  202.6 9.5 %collective-permute-start.15 = (bf16[4,128,256]{2,1,0:T(8,128)(2,1)S(1)}, bf16[4,128,256]{2,1,0:T(8,128)(2,1)S(1)}, u32[]{:S(2)}, u32[]{:S(2)}) collective-permute-start(bf16[4,128,256]{2,1,0:T(8,128)(2,1)S(1)} %collective-permute-done.14), channel_id=1, source_target_pairs={{0,64},{64,128},{128,192},{192,256},{256,320},{320,384},{384,448},... | collective-permute-start | bytes 786440 | tf_op jit(solution)/shard_map/ppermute | solution.py:141
  208.2 4.0 %copy-start.6 = (bf16[4,128,256]{2,1,0:T(8,128)(2,1)S(1)}, bf16[4,128,256]{2,1,0:T(8,128)(2,1)}, u32[]{:S(2)}) copy-start(bf16[4,128,256]{2,1,0:T(8,128)(2,1)} %all_gather.18) | copy-start | bytes 786436
  208.6 9.5 %collective-permute-start.18 = (bf16[4,128,256]{2,1,0:T(8,128)(2,1)S(1)}, bf16[4,128,256]{2,1,0:T(8,128)(2,1)S(1)}, u32[]{:S(2)}, u32[]{:S(2)}) collective-permute-start(bf16[4,128,256]{2,1,0:T(8,128)(2,1)S(1)} %collective-permute-done.17), channel_id=1, source_target_pairs={{0,448},{64,0},{128,64},{192,128},{256,192},{320,256},{384,320},{4... | collective-permute-start | bytes 786440 | tf_op jit(solution)/shard_map/ppermute | solution.py:144
Sparse Core Ops, SparseCore 0:
  31.0 83.2 all-gather.4
  173.6 38.0 all-gather.6
